TPU v7x, 256 devices: a whole 4x4x8 slice. The times are simulated.
256 devices in a mesh: group: 4 (over y), dev: 64 (over z, x, core).
Axes of the slice: x: 4, y: 4, z: 8, core: 2. Of those that a mesh axis runs over, the one named last changes fastest.
Arguments:
- q_compressed: bfloat16 [256, 1536], P('group'), may hold values from -6 to 6
- w_q_nope: bfloat16 [1536, 16384], P(None, 'dev'), may hold values from -0.15625 to 0.15625
- w_q_rope: bfloat16 [1536, 8192], P(None, 'dev'), may hold values from -0.15625 to 0.15625
- w_uk: bfloat16 [128, 128, 512], P('dev'), may hold values from -0.5 to 0.5
- w_uv: bfloat16 [128, 512, 128], P('dev'), may hold values from -0.25 to 0.25
- w_o: bfloat16 [16384, 7168], P('dev'), may hold values from -0.046875 to 0.046875
- kv_cache: bfloat16 [4, 64, 2, 2048, 576], P('group', 'dev'), may hold values from -320 to 320
- draft_kv: bfloat16 [256, 576], P('group'), may hold values from -18 to 18
- context_length: int32 [64], replicated, may hold values from 6145 to 24576
- slot_sequence: int32 [4, 64, 2], replicated, may hold values from -1 to 63, as said below
- slot_slab: int32 [4, 64, 2], replicated, may hold values from -1 to 11
Outputs:
- attn_output: float32 [256, 7168], P(('group', 'dev'))
Inputs may be any that keep to these rules, and one draw needn't show every extreme that they name: For each sequence s, slabs 0 to ceil(context_length[s] / 2048) - 1 each stand in exactly one slot of the pool, slot_sequence naming s and slot_slab the slab's number; all other slots hold -1 in both tables. The sequences' slab counts are, in some order, 4 + floor(i * 8 / 63) for i from 0 to 63. A group's slots take the slabs of its own sequences first; slabs beyond a group's 64 * 2 slots stand in free slots of other groups.
All inputs are finite; a program needn't handle non-finite values.
Results may differ from a plain program's by a relative error of at most 0.02.
The roundings to bfloat16 on the way count: a program that leaves them out, or rounds other values in their place, can miss the bound.
Values may be sent and summed in bfloat16 or wider, within the bound.
No kernel may reach another device: no remote copies, remote signals or barrier semaphores. Data moves between devices by JAX's collectives and lax.ppermute only.
A program may use at most 64 MiB of HBM per device.

v0:
```python
import jax
import jax.numpy as jnp
from jax import lax
from jax.sharding import PartitionSpec as P

NOPE = 128
ROPE = 64
LATENT = 512
VDIM = 128
DRAFT = 4


EMPTY = -1e30


def side_by_side(arrays, axis, split_dim, concat_dim, along):
    columns = [a.reshape(*a.shape[:along], -1) for a in arrays]
    both = jnp.concatenate(columns, axis=along)
    whole, at, outs = (
        lax.all_to_all(both, axis, split_axis=split_dim, concat_axis=concat_dim, tiled=True),
        0,
        [],
    )
    for a, column in zip(arrays, columns):
        slab = whole[..., at : at + column.shape[along]]
        outs.append(slab.reshape(*slab.shape[:along], *a.shape[along:]))
        at += column.shape[along]
    return tuple(outs)


def in_blocks(array, dim, peers):
    before, after = (array.shape[:dim], array.shape[dim + 1 :])
    return jnp.moveaxis(array.reshape(*before, peers, -1, *after), dim, 0)


def summed_on_arrival(array, axis, dim):
    peers = lax.axis_size(axis)
    tiles = lax.all_to_all(in_blocks(array, dim, peers), axis, 0, 0, tiled=True)
    return jnp.sum(tiles, axis=0)


def slot_partial(row_block, slab_keys, valid_count):
    scores = lax.dot_general(
        row_block, slab_keys, (((1,), (1,)), ((), ())), preferred_element_type=jnp.float32
    )
    is_valid = jnp.arange(slab_keys.shape[0], dtype=jnp.int32) < valid_count
    masked = jnp.where(is_valid[None, :], scores, EMPTY)
    row_peak = jnp.max(masked, axis=1)
    weights = jnp.where(is_valid[None, :], jnp.exp(masked - row_peak[:, None]), 0.0)
    row_total = jnp.maximum(jnp.sum(weights, axis=1), 1.0)
    mixture = jnp.dot(
        weights.astype(jnp.bfloat16), slab_keys[:, :LATENT], preferred_element_type=jnp.float32
    )
    return (row_peak + jnp.log(row_total), mixture / row_total[:, None])


def merge_blocks(block_log, block_out, block_owner, own_log, own_out):
    owners_count = own_log.shape[0]
    matches = block_owner[None, :] == jnp.arange(owners_count, dtype=jnp.int32)[:, None]
    picked = jnp.where(matches[:, :, None, None], block_log[None], EMPTY)
    top_log = jnp.maximum(jnp.max(picked, axis=1), own_log)
    weights = jnp.where(matches[:, :, None, None], jnp.exp(picked - top_log[:, None]), 0.0)
    own_weight = jnp.exp(own_log - top_log)
    weight_sum = jnp.sum(weights, axis=1) + own_weight
    summed = jnp.einsum("sbtx,btxl->stxl", weights, block_out, precision=lax.Precision.HIGHEST)
    summed = summed + own_weight[..., None] * own_out
    return (top_log + jnp.log(weight_sum), summed / weight_sum[..., None])


def draft_partials(queries_seq, draft_rows):
    scores = jnp.einsum(
        "sthk,suk->sthu", queries_seq, draft_rows, preferred_element_type=jnp.float32
    )
    causal = jnp.arange(DRAFT)[None, :] <= jnp.arange(DRAFT)[:, None]
    masked = jnp.where(causal[None, :, None, :], scores, EMPTY)
    draft_peak = jnp.max(masked, axis=3)
    weights = jnp.where(causal[None, :, None, :], jnp.exp(masked - draft_peak[..., None]), 0.0)
    draft_total = jnp.sum(weights, axis=3)
    mixture = jnp.einsum(
        "sthu,sul->sthl",
        weights.astype(jnp.bfloat16),
        draft_rows[..., :LATENT],
        preferred_element_type=jnp.float32,
    )
    return (draft_peak + jnp.log(draft_total), mixture / draft_total[..., None])


def holder_partials(arrived, cache_slots, valid_counts):
    holder_count, slot_count, draft_count, heads_here, key_width = arrived.shape
    log_list = []
    mix_list = []
    for slot_id in range(slot_count):
        row_block = arrived[:, slot_id].reshape(holder_count * draft_count * heads_here, key_width)
        slot_log, slot_mix = slot_partial(row_block, cache_slots[slot_id], valid_counts[slot_id])
        log_list.append(slot_log.reshape(holder_count, draft_count, heads_here))
        mix_list.append(slot_mix.reshape(holder_count, draft_count, heads_here, LATENT))
    return (jnp.stack(log_list, axis=1), jnp.stack(mix_list, axis=1))


def shards(
    q_compressed,
    w_q_nope,
    w_q_rope,
    w_uk,
    w_uv,
    w_o,
    kv_cache,
    draft_kv,
    context_length,
    slot_sequence,
    slot_slab,
):
    group_count = lax.axis_size("group")
    holder_count = lax.axis_size("dev")
    group_index = lax.axis_index("group")
    holder_index = lax.axis_index("dev")
    token_count = q_compressed.shape[0]
    seq_group = token_count // DRAFT
    heads_here = w_uk.shape[0]
    key_width = LATENT + ROPE
    slab_length = kv_cache.shape[3]
    q_nope = jnp.dot(q_compressed, w_q_nope, preferred_element_type=jnp.float32).astype(
        jnp.bfloat16
    )
    q_nope = q_nope.reshape(token_count, heads_here, NOPE)
    q_rope = jnp.dot(q_compressed, w_q_rope, preferred_element_type=jnp.float32).reshape(
        token_count, heads_here, ROPE
    )
    absorbed = jnp.einsum("thn,hnl->thl", q_nope, w_uk, preferred_element_type=jnp.float32)
    queries = (jnp.concatenate([absorbed, q_rope], axis=2) * (NOPE + ROPE) ** (-0.5)).astype(
        jnp.bfloat16
    )
    queries_seq = queries.reshape(seq_group, DRAFT, heads_here, key_width)
    draft_log, draft_mix = draft_partials(
        queries_seq, draft_kv.reshape(seq_group, DRAFT, key_width)
    )
    group_table = lax.dynamic_index_in_dim(slot_sequence, group_index, 0, keepdims=False)
    own_table = lax.dynamic_index_in_dim(group_table, holder_index, 0, keepdims=False)
    own_slabs = lax.dynamic_index_in_dim(
        lax.dynamic_index_in_dim(slot_slab, group_index, 0, keepdims=False),
        holder_index,
        0,
        keepdims=False,
    )
    chosen = jnp.maximum(own_table, 0)
    valid_counts = jnp.where(own_table >= 0, context_length[chosen] - own_slabs * slab_length, 0)
    cache_slots = kv_cache[0, 0]
    pool_table = slot_sequence.reshape(group_count, -1)
    mine = group_index * seq_group + jnp.arange(seq_group, dtype=jnp.int32)
    present = jnp.any(pool_table[:, :, None] == mine[None, None, :], axis=1)
    outgoing = jnp.where(
        present[:, :, None, None, None], queries_seq[None], jnp.zeros((), jnp.bfloat16)
    )
    gathered = lax.all_to_all(outgoing, "group", split_axis=0, concat_axis=0, tiled=True)
    every_seq = gathered.reshape(group_count * seq_group, DRAFT, heads_here, key_width)
    picked = jnp.take(every_seq, jnp.maximum(group_table, 0).reshape(-1), axis=0)
    picked = picked.reshape(holder_count, -1, DRAFT, heads_here, key_width)
    arrived = lax.all_to_all(picked, "dev", split_axis=0, concat_axis=0, tiled=True)
    slot_log, slot_mix = holder_partials(arrived, cache_slots, valid_counts)
    back_log, back_mix = side_by_side((slot_log, slot_mix), "dev", 0, 0, 4)
    seq_total = group_count * seq_group
    group_log, group_mix = merge_blocks(
        back_log.reshape(-1, DRAFT, heads_here),
        back_mix.reshape(-1, DRAFT, heads_here, LATENT),
        group_table.reshape(-1),
        jnp.full((seq_total, DRAFT, heads_here), EMPTY, jnp.float32),
        jnp.zeros((seq_total, DRAFT, heads_here, LATENT), jnp.float32),
    )
    home_log, home_mix = (
        lax.all_to_all(
            group_log.reshape(group_count, seq_group, DRAFT, heads_here),
            "group",
            split_axis=0,
            concat_axis=0,
            tiled=True,
        ),
        lax.all_to_all(
            group_mix.reshape(group_count, seq_group, DRAFT, heads_here, LATENT),
            "group",
            split_axis=0,
            concat_axis=0,
            tiled=True,
        ),
    )
    home_owner = jnp.tile(jnp.arange(seq_group, dtype=jnp.int32), group_count)
    final_log, final_mix = merge_blocks(
        home_log.reshape(-1, DRAFT, heads_here),
        home_mix.reshape(-1, DRAFT, heads_here, LATENT),
        home_owner,
        draft_log,
        draft_mix,
    )
    attended = final_mix.astype(jnp.bfloat16).reshape(token_count, heads_here, LATENT)
    head_values = jnp.einsum("thl,hlv->thv", attended, w_uv, preferred_element_type=jnp.float32)
    head_values = head_values.astype(jnp.bfloat16).reshape(token_count, heads_here * VDIM)
    return summed_on_arrival(
        jnp.dot(head_values, w_o, preferred_element_type=jnp.float32), "dev", 0
    )


def solution(mesh):
    placed = (
        P("group", None),
        P(None, "dev"),
        P(None, "dev"),
        P("dev", None, None),
        P("dev", None, None),
        P("dev", None),
        P("group", "dev", None, None, None),
        P("group", None),
        P(),
        P(),
        P(),
    )
    return jax.shard_map(
        shards, mesh=mesh, in_specs=placed, out_specs=P(("group", "dev"), None), check_vma=False
    )
```

profile of v0, /device:TPU:32, one launch (start us, length us, event | category | flops | bytes accessed | tf_op | source)
XLA Modules:
  0.0 257.8 jit_solution(4369279342628065032)
XLA Ops:
  7.4 4.5 %all-to-all-start = ((bf16[4,16,4,2,576]{4,3,2,1,0:T(2,128)(2,1)}), bf16[4,16,4,2,576]{4,3,2,1,0:T(2,128)(2,1)S(1)}, u32[]{:S(2)}, u32[]{:S(2)}) async-start(bf16[4,16,4,2,576]{4,3,2,1,0:T(2,128)(2,1)} %broadcast_select_fusion.1), calls=%async_computation | async-start | bytes 1310720 | tf_op jit(solution)/shard_map/all_to_all | solution.py:154
  12.2 10.5 %all-to-all-done = bf16[4,16,4,2,576]{4,3,2,1,0:T(2,128)(2,1)S(1)} async-done(((bf16[4,16,4,2,576]{4,3,2,1,0:T(2,128)(2,1)}), bf16[4,16,4,2,576]{4,3,2,1,0:T(2,128)(2,1)S(1)}, u32[]{:S(2)}, u32[]{:S(2)}) %all-to-all-start) | async-done | bytes 589856 | tf_op jit(solution)/shard_map/all_to_all | solution.py:154
  22.7 3.4 %gather_fusion.1 = bf16[128,4,2,576]{3,2,1,0:T(2,128)(2,1)S(1)} fusion(bf16[64,4,2,576]{3,2,1,0:T(2,128)(2,1)S(1)} %bitcast.96, s32[1024]{0:T(1024)S(1)} %pad_clamp_fusion), kind=kCustom, calls=%fused_computation.1 | custom fusion | bytes 2359808 | tf_op jit(solution)/shard_map/jit(_take)/gather | solution.py:156
  26.2 2.5 broadcast_select_fusion
  28.6 11.8 %all-to-all-start.1 = ((bf16[64,2,4,2,576]{4,3,2,1,0:T(2,128)(2,1)}), bf16[64,2,4,2,576]{4,3,2,1,0:T(2,128)(2,1)S(1)}, u32[]{:S(2)}, u32[]{:S(2)}) async-start(bf16[64,2,4,2,576]{4,3,2,1,0:T(2,128)(2,1)} %broadcast_select_fusion), calls=%async_computation.1 | async-start | bytes 2621440 | tf_op jit(solution)/shard_map/all_to_all | solution.py:158
  44.2 5.2 %slice_bitcast_fusion.1 = (bf16[2048,576]{0,1:T(8,128)(2,1)}, bf16[2048,576]{0,1:T(8,128)(2,1)}) fusion(bf16[1,1,2,2048,576]{3,4,2,1,0:T(8,128)(2,1)} %param.17), kind=kLoop, calls=%fused_computation.14 | loop fusion | bytes 9437184 | tf_op jit(solution)/shard_map/squeeze | solution.py:94
  49.4 24.3 %all-to-all-done.1 = bf16[64,2,4,2,576]{4,3,2,1,0:T(2,128)(2,1)S(1)} async-done(((bf16[64,2,4,2,576]{4,3,2,1,0:T(2,128)(2,1)}), bf16[64,2,4,2,576]{4,3,2,1,0:T(2,128)(2,1)S(1)}, u32[]{:S(2)}, u32[]{:S(2)}) %all-to-all-start.1) | async-done | bytes 1179680 | tf_op jit(solution)/shard_map/all_to_all | solution.py:158
  75.2 3.6 %select_reduce_fusion = (f32[512]{0:T(512)S(1)}, f32[512,2048]{1,0:T(8,128)S(1)}) fusion(pred[2048]{0:T(1024)(128)(4,1)S(1)} %iota_compare_fusion.2, bf16[512,576]{1,0:T(8,128)(2,1)S(1)} %reshape_squeeze.7, bf16[1,1,2,2048,576]{3,4,2,1,0:T(8,128)(2,1)} %param.17), kind=kOutput, calls=%fused_computation.5 | convolution fusion | flops 1210056192 | bytes 7147520 | tf_op jit(solution)/shard_map/dot_general | solution.py:43
  83.2 3.6 %select_reduce_fusion.1 = (f32[512]{0:T(512)S(1)}, f32[512,2048]{1,0:T(8,128)S(1)}) fusion(pred[2048]{0:T(1024)(128)(4,1)S(1)} %iota_compare_fusion.3, bf16[512,576]{1,0:T(8,128)(2,1)S(1)} %reshape_squeeze.6, bf16[1,1,2,2048,576]{3,4,2,1,0:T(8,128)(2,1)} %param.17), kind=kOutput, calls=%fused_computation.6 | convolution fusion | flops 1210056192 | bytes 7147520 | tf_op jit(solution)/shard_map/dot_general | solution.py:43
  89.7 1.6 stack_reshape.8
  91.4 1.5 copy.231
  93.9 3.1 %maximum_maximum_fusion = f32[64,2,4,2,513]{4,2,3,1,0:T(4,128)} fusion(f32[64,1,4,2,512]{4,2,3,1,0:T(4,128)S(1)} %copy.232, f32[64,1,4,2,512]{4,2,3,1,0:T(4,128)S(1)} %copy.231, f32[64,2,4,2,1]{4,2,3,1,0:T(4,128)S(1)} %copy.233), kind=kLoop, calls=%fused_computation.11 | loop fusion | flops 1050624 | bytes 4202496 | tf_op jit(solution)/shard_map/concatenate | solution.py:18
  97.0 6.5 %all-to-all-start.2 = ((f32[64,2,4,2,513]{4,2,3,1,0:T(4,128)}), f32[64,2,4,2,513]{4,2,3,1,0:T(4,128)S(1)}, u32[]{:S(2)}, u32[]{:S(2)}) async-start(f32[64,2,4,2,513]{4,2,3,1,0:T(4,128)} %maximum_maximum_fusion), calls=%async_computation.2 | async-start | bytes 5242880 | tf_op jit(solution)/shard_map/all_to_all | solution.py:20
  105.1 1.9 fusion.56
  108.2 1.7 fusion.62
  109.9 55.3 %all-to-all-done.2 = f32[64,2,4,2,513]{4,2,3,1,0:T(4,128)S(1)} async-done(((f32[64,2,4,2,513]{4,2,3,1,0:T(4,128)}), f32[64,2,4,2,513]{4,2,3,1,0:T(4,128)S(1)}, u32[]{:S(2)}, u32[]{:S(2)}) %all-to-all-start.2) | async-done | bytes 2101280 | tf_op jit(solution)/shard_map/all_to_all | solution.py:20
  166.1 2.7 %copy.236 = f32[64,2,4,2,1]{2,1,0,3,4:T(2,128)S(1)} copy(f32[64,2,4,2,1]{4,2,3,1,0:T(4,128)} %slice.55) | data formatting | bytes 8192 | tf_op jit(solution)/shard_map/slice | solution.py:25
  172.2 3.2 %all-to-all-start.4 = ((f32[4,1,128]{2,1,0:T(1,128)}), f32[4,1,128]{2,1,0:T(1,128)S(1)}, u32[]{:S(2)}, u32[]{:S(2)}) async-start(f32[4,1,128]{2,1,0:T(1,128)} %reshape.321), calls=%async_computation.4 | async-start | bytes 4096 | tf_op jit(solution)/shard_map/all_to_all | solution.py:170
  176.6 2.6 %fusion.26 = f32[64,4,2,512]{3,0,2,1:T(8,128)S(1)} fusion(f32[128,4,2,512]{3,1,2,0:T(4,128)S(1)} %bitcast.98, f32[64,4,2]{0,2,1:T(2,128)S(1)} %get-tuple-element.16, f32[64,4,2]{0,2,1:T(2,128)S(1)} %get-tuple-element.15, f32[64,4,2]{0,2,1:T(2,128)S(1)} %broadcast_maximum_fusion, f32[128,4,2]{0,2,1:T(2,128)S(1)} %copy-done.9, ...), kind=kOutput, calls=%fused_computation.31 | convolution fusion | flops 403374080 | bytes 3164160 | tf_op jit(solution)/shard_map/sbtx,btxl->stxl/dot_general | solution.py:65
  180.5 4.7 %all-to-all-start.3 = ((f32[4,16,4,2,512]{4,1,3,2,0:T(8,128)}), f32[4,16,4,2,512]{4,1,3,2,0:T(8,128)S(1)}, u32[]{:S(2)}, u32[]{:S(2)}) async-start(f32[4,16,4,2,512]{4,1,3,2,0:T(8,128)} %copy.238), calls=%async_computation.3 | async-start | bytes 2097152 | tf_op jit(solution)/shard_map/all_to_all | solution.py:177
  186.9 13.1 %all-to-all-done.3 = f32[4,16,4,2,512]{4,1,3,2,0:T(8,128)S(1)} async-done(((f32[4,16,4,2,512]{4,1,3,2,0:T(8,128)}), f32[4,16,4,2,512]{4,1,3,2,0:T(8,128)S(1)}, u32[]{:S(2)}, u32[]{:S(2)}) %all-to-all-start.3) | async-done | bytes 1048608 | tf_op jit(solution)/shard_map/all_to_all | solution.py:177
  202.8 1.9 copy.254
  204.7 51.0 %all_to_all.30 = f32[64,1,7168]{2,1,0:T(1,128)S(1)} all-to-all(f32[64,1,7168]{2,1,0:T(1,128)S(1)} %copy.254), channel_id=1, replica_groups=mesh['group'=4,'dev'=64] {'dev'}, dimensions={0} | all-to-all | bytes 3670016 | tf_op jit(solution)/shard_map/all_to_all | solution.py:38
  255.7 2.2 reduce_sum.64
  (109 shorter events, 35.1 us)
Async XLA Ops:
  0.0 2.4 copy-start
  0.0 11.8 %copy-start.10 = (s32[4,64,2]{1,2,0:T(2,128)S(1)}, s32[4,64,2]{1,2,0:T(2,128)}, u32[]{:S(2)}) copy-start(s32[4,64,2]{1,2,0:T(2,128)} %param.20) | copy-start | bytes 6148
  4.9 0.7 copy-start.5
  7.4 15.3 %all-to-all-start = ((bf16[4,16,4,2,576]{4,3,2,1,0:T(2,128)(2,1)}), bf16[4,16,4,2,576]{4,3,2,1,0:T(2,128)(2,1)S(1)}, u32[]{:S(2)}, u32[]{:S(2)}) async-start(bf16[4,16,4,2,576]{4,3,2,1,0:T(2,128)(2,1)} %broadcast_select_fusion.1), calls=%async_computation | async-start | bytes 1310720 | tf_op jit(solution)/shard_map/all_to_all | solution.py:154
  22.7 18.6 %copy-start.1 = (s32[64]{0:T(128)S(1)}, s32[64]{0:T(128)}, u32[]{:S(2)}) copy-start(s32[64]{0:T(128)} %param.19) | copy-start | bytes 772
  28.6 45.2 %all-to-all-start.1 = ((bf16[64,2,4,2,576]{4,3,2,1,0:T(2,128)(2,1)}), bf16[64,2,4,2,576]{4,3,2,1,0:T(2,128)(2,1)S(1)}, u32[]{:S(2)}, u32[]{:S(2)}) async-start(bf16[64,2,4,2,576]{4,3,2,1,0:T(2,128)(2,1)} %broadcast_select_fusion), calls=%async_computation.1 | async-start | bytes 2621440 | tf_op jit(solution)/shard_map/all_to_all | solution.py:158
  78.7 1.7 copy-start.4
  86.7 1.7 copy-start.3
  97.0 6.6 %copy-start.6 = (bf16[64,576]{1,0:T(8,128)(2,1)S(1)}, bf16[64,576]{1,0:T(8,128)(2,1)}, u32[]{:S(2)}) copy-start(bf16[64,576]{1,0:T(8,128)(2,1)} %param.18) | copy-start | bytes 221188
  97.0 68.2 %all-to-all-start.2 = ((f32[64,2,4,2,513]{4,2,3,1,0:T(4,128)}), f32[64,2,4,2,513]{4,2,3,1,0:T(4,128)S(1)}, u32[]{:S(2)}, u32[]{:S(2)}) async-start(f32[64,2,4,2,513]{4,2,3,1,0:T(4,128)} %maximum_maximum_fusion), calls=%async_computation.2 | async-start | bytes 5242880 | tf_op jit(solution)/shard_map/all_to_all | solution.py:20
  169.4 7.2 %copy-start.9 = (f32[128,4,2]{0,2,1:T(2,128)S(1)}, f32[128,4,2]{0,2,1:T(2,128)}, u32[]{:S(2)}) copy-start(f32[128,4,2]{0,2,1:T(2,128)} %copy.237) | copy-start | bytes 12292
  172.2 8.3 %all-to-all-start.4 = ((f32[4,1,128]{2,1,0:T(1,128)}), f32[4,1,128]{2,1,0:T(1,128)S(1)}, u32[]{:S(2)}, u32[]{:S(2)}) async-start(f32[4,1,128]{2,1,0:T(1,128)} %reshape.321), calls=%async_computation.4 | async-start | bytes 4096 | tf_op jit(solution)/shard_map/all_to_all | solution.py:170
  176.6 8.6 %copy-start.11 = (s32[64]{0:T(128)S(1)}, s32[64]{0:T(128)}, u32[]{:S(2)}) copy-start(s32[64]{0:T(128)} %eq.69) | copy-start | bytes 772
  179.2 20.9 %copy-start.7 = (f32[16,4,2,512]{3,1,2,0:T(4,128)S(1)}, f32[16,4,2,512]{3,1,2,0:T(4,128)}, u32[]{:S(2)}) copy-start(f32[16,4,2,512]{3,1,2,0:T(4,128)} %fusion.62) | copy-start | bytes 786436
  180.3 20.7 %copy-start.8 = (bf16[2,512,128]{2,1,0:T(8,128)(2,1)S(1)}, bf16[2,512,128]{2,1,0:T(8,128)(2,1)}, u32[]{:S(2)}) copy-start(bf16[2,512,128]{2,1,0:T(8,128)(2,1)} %param.15) | copy-start | bytes 786436
  180.5 19.5 %all-to-all-start.3 = ((f32[4,16,4,2,512]{4,1,3,2,0:T(8,128)}), f32[4,16,4,2,512]{4,1,3,2,0:T(8,128)S(1)}, u32[]{:S(2)}, u32[]{:S(2)}) async-start(f32[4,16,4,2,512]{4,1,3,2,0:T(8,128)} %copy.238), calls=%async_computation.3 | async-start | bytes 2097152 | tf_op jit(solution)/shard_map/all_to_all | solution.py:177
  200.0 2.0 copy-start.2
where the time goes:
time: 260 us; the launch traced here: 258 us
  waiting for transfers between devices  103 us (40%)
  blocking collectives  51 us (20%)
  local copies, waits for them, and re-layouts  34 us (13%)
  starting transfers between devices  30.6 us (12%)
  matrix products  21.3 us (8%)
  other arithmetic  17 us (7%)
    all_to_all x1, waiting for transfers between devices, side_by_side(): lax.all_to_all(both, axis, split_axis=split_dim, concat_axis=concat_dim,...  55.3 us
    all_to_all x1, blocking collectives, summed_on_arrival(): tiles = lax.all_to_all(in_blocks(array, dim, peers), axis, 0, 0, tiled=True)  51 us
    all_to_all x1, waiting for transfers between devices, shards(): lax.all_to_all(picked, 'dev', split_axis=0, concat_axis=0, tiled=True)  24.3 us
    all_to_all x1, waiting for transfers between devices, shards(): lax.all_to_all(group_mix.reshape(group_count, seq_group, DRAFT, heads_her...  13.1 us
    all_to_all x1, starting transfers between devices, shards(): lax.all_to_all(picked, 'dev', split_axis=0, concat_axis=0, tiled=True)  11.8 us
    all_to_all x1, waiting for transfers between devices, shards(): lax.all_to_all(outgoing, 'group', split_axis=0, concat_axis=0, tiled=True)  10.5 us
    dot_general x2, matrix products, slot_partial(): lax.dot_general(row_block, slab_keys, (((1,), (1,)), ((), ())), preferred...  7.14 us
    all_to_all x1, starting transfers between devices, side_by_side(): lax.all_to_all(both, axis, split_axis=split_dim, concat_axis=concat_dim,...  6.51 us
  transfers between devices with their start and end apart: 5, of which 5 were waited for; matrix products, arithmetic and copies ran while one was open for 9% of the time, Pallas kernels for 0%

commit v1 on v0

v1 whole, which is shorter than its diff:
```python
import jax
import jax.numpy as jnp
from jax import lax
from jax.experimental import pallas as pl
from jax.experimental.pallas import tpu as pltpu
from jax.sharding import Mesh
from jax.sharding import PartitionSpec as P

NOPE = 128
ROPE = 64
LATENT = 512
VDIM = 128
DRAFT = 4
SEQ_GRP = 16
TOK_GRP = SEQ_GRP * DRAFT
SLOTS = 2
KEY = LATENT + ROPE
WIDE = 2 * LATENT + 2 * ROPE
PART = SLOTS * 2 * LATENT + 128
NARROW = 2 * NOPE + 2 * ROPE
EMPTY = -1e30
SCALE = (NOPE + ROPE) ** -0.5
F32 = jnp.float32
BF16 = jnp.bfloat16
CONTRACT_LAST = (((1,), (1,)), ((), ()))

VMEM = pl.BlockSpec(memory_space=pltpu.VMEM)
SMEM = pl.BlockSpec(memory_space=pltpu.SMEM)


def dot(a, b):
    return jnp.dot(a, b, preferred_element_type=F32)


def dot_t(a, b):
    return lax.dot_general(a, b, CONTRACT_LAST, preferred_element_type=F32)


def call(kernel, outs, args, specs, scratch=(), vmem=32):
    return pl.pallas_call(
        kernel,
        out_shape=outs,
        in_specs=specs,
        out_specs=jax.tree.map(lambda _: VMEM, outs),
        scratch_shapes=list(scratch),
        compiler_params=pltpu.CompilerParams(vmem_limit_bytes=vmem << 20),
    )(*args)


def three_terms(value):
    high = value.astype(BF16).astype(F32)
    middle = (value - high).astype(BF16).astype(F32)
    return high, middle, (value - high - middle).astype(BF16).astype(F32)


def put_terms(tile, value, first):
    lane = lax.broadcasted_iota(jnp.int32, tile.shape, 1)
    for i, term in enumerate(three_terms(value)):
        tile = jnp.where(lane == first + i, term, tile)
    return tile


def project_kernel(q_ref, wn_ref, wr_ref, out_ref):
    out_ref[:, : 2 * NOPE] = dot(q_ref[...], wn_ref[...]).astype(BF16)
    out_ref[:, 2 * NOPE :] = (dot(q_ref[...], wr_ref[...]) * SCALE).astype(BF16)


def spread_kernel(core_ref, q_ref, code_ref, own_ref, mate_ref, out_ref, rows):
    core = core_ref[0]
    rows[...] = jnp.zeros_like(rows)
    for block in range(q_ref.shape[0] // TOK_GRP):
        at = pl.ds(block * TOK_GRP, TOK_GRP)
        side = pl.multiple_of(jnp.where(core == block % 2, 0, NOPE), NOPE)
        for par in range(2):
            rows[at, pl.ds(par * 2 * NOPE + side, NOPE)] = q_ref[at, par * NOPE : (par + 1) * NOPE]
        rows[at, 4 * NOPE :] = q_ref[at, 2 * NOPE :]
    count = code_ref.shape[0] // SLOTS
    for slot in range(SLOTS):
        code = code_ref[slot * count : (slot + 1) * count, :]
        column = lax.broadcasted_iota(jnp.int32, (count, rows.shape[0]), 1)
        picked = dot(jnp.where(column == code, 1.0, 0.0).astype(BF16), rows[...]).astype(BF16)
        for par in range(2):
            weight = jnp.concatenate([own_ref[par], mate_ref[par]], axis=0)
            absorbed = dot(picked[:, par * 2 * NOPE : (par + 1) * 2 * NOPE], weight) * SCALE
            first = slot * WIDE + par * LATENT
            out_ref[:, first : first + LATENT] = absorbed.astype(BF16)
        out_ref[:, slot * WIDE + 2 * LATENT : (slot + 1) * WIDE] = picked[:, 4 * NOPE :]


def draft_kernel(q_ref, uk_ref, uv_ref, kv_ref, hv_ref, log_ref):
    row = lax.broadcasted_iota(jnp.int32, (TOK_GRP, TOK_GRP), 0)
    col = lax.broadcasted_iota(jnp.int32, (TOK_GRP, TOK_GRP), 1)
    seen = (row // DRAFT == col // DRAFT) & (col <= row)
    lane = lax.broadcasted_iota(jnp.int32, log_ref.shape, 1)
    logs = jnp.zeros(log_ref.shape, F32)
    for par in range(2):
        absorbed = (dot(q_ref[:, par * NOPE : (par + 1) * NOPE], uk_ref[par]) * SCALE).astype(BF16)
        first = 2 * NOPE + par * ROPE
        scores = dot_t(absorbed, kv_ref[:, :LATENT])
        scores += dot_t(q_ref[:, first : first + ROPE], kv_ref[:, LATENT:])
        scores = jnp.where(seen, scores, EMPTY)
        peak = jnp.max(scores, axis=1, keepdims=True)
        weights = jnp.where(seen, jnp.exp(scores - peak), 0.0)
        total = jnp.sum(weights, axis=1, keepdims=True)
        mixture = dot(weights.astype(BF16), kv_ref[:, :LATENT]) / total
        hv_ref[:, par * VDIM : (par + 1) * VDIM] = dot(mixture.astype(BF16), uv_ref[par])
        logs = jnp.where(lane == par, peak + jnp.log(total), logs)
    log_ref[...] = logs


def attend_kernel(count_ref, x_ref, kv_ref, out_ref, queries, scores):
    slot = pl.program_id(0)
    count = count_ref[slot]
    half = x_ref.shape[0]
    for par in range(2):
        at = slice(par * half, (par + 1) * half)
        queries[at, :LATENT] = x_ref[:, par * LATENT : (par + 1) * LATENT]
        first = 2 * LATENT + par * ROPE
        queries[at, LATENT:] = x_ref[:, first : first + ROPE]
    slab = kv_ref.shape[0]
    chunk = 512
    peak = jnp.full((2 * half, 1), EMPTY, F32)
    for first in range(0, slab, chunk):
        score = dot_t(queries[...], kv_ref[first : first + chunk, :])
        position = lax.broadcasted_iota(jnp.int32, score.shape, 1) + first
        score = jnp.where(position < count, score, EMPTY)
        scores[:, first : first + chunk] = score
        peak = jnp.maximum(peak, jnp.max(score, axis=1, keepdims=True))
    reference = jnp.maximum(peak, EMPTY / 10)
    total = jnp.zeros((2 * half, 1), F32)
    mixture = jnp.zeros((2 * half, LATENT), F32)
    for first in range(0, slab, chunk):
        weights = jnp.exp(scores[:, first : first + chunk] - reference)
        total += jnp.sum(weights, axis=1, keepdims=True)
        mixture += dot(weights.astype(BF16), kv_ref[first : first + chunk, :LATENT])
    total = jnp.maximum(total, 1.0)
    mixture = (mixture / total).astype(BF16)
    log = peak + jnp.log(total)
    start = slot * 2 * LATENT
    lane = lax.broadcasted_iota(jnp.int32, (half, 128), 1)
    tile = jnp.where(slot == 0, jnp.zeros((half, 128), F32), out_ref[:, SLOTS * 2 * LATENT :].astype(F32))
    for par in range(2):
        at = slice(par * half, (par + 1) * half)
        out_ref[:, pl.ds(pl.multiple_of(start + par * LATENT, LATENT), LATENT)] = mixture[at]
        for i, term in enumerate(three_terms(log[at])):
            tile = jnp.where(lane == slot * 6 + par * 3 + i, term, tile)
    out_ref[:, SLOTS * 2 * LATENT :] = tile.astype(BF16)


def attend(count, x, kv):
    rows = x.shape[0]
    slab = kv.shape[1]
    return pl.pallas_call(
        attend_kernel,
        out_shape=jax.ShapeDtypeStruct((rows, PART), BF16),
        grid_spec=pltpu.PrefetchScalarGridSpec(
            num_scalar_prefetch=1,
            grid=(SLOTS,),
            in_specs=[
                pl.BlockSpec((rows, WIDE), lambda k, _: (0, k)),
                pl.BlockSpec((None, slab, KEY), lambda k, _: (k, 0, 0)),
            ],
            out_specs=pl.BlockSpec((rows, PART), lambda k, _: (0, 0)),
            scratch_shapes=[
                pltpu.VMEM((2 * rows, KEY), BF16),
                pltpu.VMEM((2 * rows, slab), F32),
            ],
        ),
        compiler_params=pltpu.CompilerParams(
            dimension_semantics=("arbitrary",), vmem_limit_bytes=48 << 20
        ),
    )(count, x, kv)


def merge_kernel(core_ref, y_ref, code_ref, own_ref, mate_ref, out_ref):
    core = core_ref[0]
    rows, cols = out_ref.shape[0], y_ref.shape[0]
    base = SLOTS * 2 * LATENT
    logs = jnp.transpose(y_ref[:, base:].astype(F32))
    row = lax.broadcasted_iota(jnp.int32, (rows, cols), 0)
    match = [row == code_ref[slot : slot + 1, :] for slot in range(SLOTS)]
    is_own = (lax.broadcasted_iota(jnp.int32, (rows, VDIM), 0) // TOK_GRP) % 2 == core
    tile = jnp.zeros((rows, 128), F32)
    for par in range(2):
        held = []
        for slot in range(SLOTS):
            at = slot * 6 + par * 3
            log = logs[at : at + 1, :] + logs[at + 1 : at + 2, :] + logs[at + 2 : at + 3, :]
            held.append(jnp.where(match[slot], log, EMPTY))
        peak = jnp.max(jnp.maximum(held[0], held[1]), axis=1, keepdims=True)
        total = jnp.zeros((rows, 1), F32)
        mixture = jnp.zeros((rows, LATENT), F32)
        for slot in range(SLOTS):
            weights = jnp.where(match[slot], jnp.exp(held[slot] - peak), 0.0)
            total += jnp.sum(weights, axis=1, keepdims=True)
            first = slot * 2 * LATENT + par * LATENT
            mixture += dot(weights.astype(BF16), y_ref[:, first : first + LATENT])
        total = jnp.maximum(total, 1.0)
        mixture = (mixture / total).astype(BF16)
        values = jnp.where(is_own, dot(mixture, own_ref[par]), dot(mixture, mate_ref[par]))
        out_ref[:, par * VDIM : (par + 1) * VDIM] = values.astype(BF16)
        tile = put_terms(tile, peak + jnp.log(total), par * 3)
    out_ref[:, 2 * VDIM :] = tile.astype(BF16)


def finish_kernel(z_ref, hv_ref, log_ref, order_ref, out_ref):
    blocks = z_ref.shape[0] // TOK_GRP
    values = []
    for par in range(2):
        logs = [log_ref[:, par : par + 1]]
        parts = [hv_ref[:, par * VDIM : (par + 1) * VDIM]]
        for block in range(blocks):
            at = slice(block * TOK_GRP, (block + 1) * TOK_GRP)
            terms = z_ref[at, 2 * VDIM :].astype(F32)
            first = par * 3
            logs.append(
                terms[:, first : first + 1]
                + terms[:, first + 1 : first + 2]
                + terms[:, first + 2 : first + 3]
            )
            parts.append(z_ref[at, par * VDIM : (par + 1) * VDIM].astype(F32))
        peak = logs[0]
        for log in logs[1:]:
            peak = jnp.maximum(peak, log)
        total = jnp.zeros_like(peak)
        summed = jnp.zeros_like(parts[0])
        for log, part in zip(logs, parts):
            weight = jnp.exp(log - peak)
            total += weight
            summed += weight * part
        values.append((summed / total).astype(BF16))
    out_ref[...] = dot(order_ref[...], jnp.concatenate(values, axis=1)).astype(BF16)


def exchange(array, axes, peers):
    blocks = array.reshape(peers, array.shape[0] // peers, *array.shape[1:])
    return lax.all_to_all(blocks, axes, 0, 0, tiled=True).reshape(array.shape)


def shards(
    q_compressed,
    w_q_nope,
    w_q_rope,
    w_uk,
    w_uv,
    w_o,
    kv_cache,
    draft_kv,
    context_length,
    slot_sequence,
    slot_slab,
):
    groups, zs, xs, cores = (lax.axis_size(a) for a in ("group", "z", "x", "core"))
    group, z, x, core = (lax.axis_index(a) for a in ("group", "z", "x", "core"))
    chips = zs * xs
    core_id = core.astype(jnp.int32).reshape(1)
    swap = [(i, 1 - i) for i in range(cores)]
    mate_uk = lax.ppermute(w_uk, "core", swap)
    mate_uv = lax.ppermute(w_uv, "core", swap)

    table = lax.dynamic_index_in_dim(slot_sequence, group, 0, keepdims=False)
    table = table.reshape(chips, cores, SLOTS)
    held = lax.dynamic_index_in_dim(table, core, 1, keepdims=False)
    code = (held >> 4) * (2 * TOK_GRP) + (held & 15) * DRAFT
    inner = jnp.arange(2, dtype=jnp.int32)[:, None] * TOK_GRP + jnp.arange(DRAFT, dtype=jnp.int32)
    code = code.T[:, :, None] + inner.reshape(-1)
    code = jnp.where((held >= 0).T[:, :, None], code, -1)
    code_row = code.reshape(SLOTS, -1)
    code_col = code.reshape(-1, 1)

    chip = z * xs + x
    mine = lax.dynamic_index_in_dim(held, chip, 0, keepdims=False)
    slabs = lax.dynamic_index_in_dim(slot_slab, group, 0, keepdims=False).reshape(chips, cores, SLOTS)
    slabs = lax.dynamic_index_in_dim(slabs, chip, 0, keepdims=False)
    slabs = lax.dynamic_index_in_dim(slabs, core, 0, keepdims=False)
    is_mine = mine[:, None] == jnp.arange(context_length.shape[0], dtype=jnp.int32)
    length = jnp.sum(jnp.where(is_mine, context_length, 0), axis=1)
    count = jnp.where(mine >= 0, length - slabs * kv_cache.shape[3], 0).astype(jnp.int32)

    narrow = call(
        project_kernel,
        jax.ShapeDtypeStruct((TOK_GRP, NARROW), BF16),
        (q_compressed, w_q_nope, w_q_rope),
        [VMEM] * 3,
    )
    copies = groups * cores
    spread = jnp.broadcast_to(narrow, (copies, *narrow.shape))
    every = lax.all_to_all(spread, ("group", "core"), 0, 0, tiled=True).reshape(-1, NARROW)
    draft_hv, draft_log = call(
        draft_kernel,
        (
            jax.ShapeDtypeStruct((TOK_GRP, 2 * VDIM), F32),
            jax.ShapeDtypeStruct((TOK_GRP, 128), F32),
        ),
        (narrow, w_uk, w_uv, draft_kv),
        [VMEM] * 4,
    )
    rows = chips * cores * DRAFT
    wide = call(
        spread_kernel,
        jax.ShapeDtypeStruct((rows, SLOTS * WIDE), BF16),
        (core_id, every, code_col, w_uk, mate_uk),
        [SMEM] + [VMEM] * 4,
        [pltpu.VMEM((copies * TOK_GRP, 5 * NOPE), BF16)],
    )
    arrived = exchange(wide, ("z", "x"), chips)
    partials = attend(count, arrived, kv_cache.reshape(kv_cache.shape[2:]))
    back = exchange(partials, ("z", "x"), chips)
    merged = call(
        merge_kernel,
        jax.ShapeDtypeStruct((copies * TOK_GRP, NARROW), BF16),
        (core_id, back, code_row, w_uv, mate_uv),
        [SMEM] + [VMEM] * 4,
    )
    home = exchange(merged, ("group", "core"), copies)
    token = jnp.arange(TOK_GRP, dtype=jnp.int32).reshape(zs, xs, cores)
    token = token.transpose(2, 1, 0).reshape(-1, 1)
    order = (token == jnp.arange(TOK_GRP, dtype=jnp.int32)).astype(BF16)
    head_values = call(
        finish_kernel,
        jax.ShapeDtypeStruct((TOK_GRP, 2 * VDIM), BF16),
        (home, draft_hv, draft_log, order),
        [VMEM] * 4,
    )
    sums = jnp.dot(head_values, w_o, preferred_element_type=F32)
    for axis, peers in (("core", cores), ("x", xs), ("z", zs)):
        sums = sums.astype(BF16).reshape(peers, -1, w_o.shape[1])
        tiles = lax.all_to_all(sums, axis, 0, 0, tiled=True)
        sums = jnp.sum(tiles.astype(F32), axis=0)
    return sums


def solution(mesh):
    fine = Mesh(mesh.devices.reshape(4, 8, 4, 2), ("group", "z", "x", "core"))
    dev = ("z", "x", "core")
    placed = (
        P("group", None),
        P(None, dev),
        P(None, dev),
        P(dev, None, None),
        P(dev, None, None),
        P(dev, None),
        P("group", dev, None, None, None),
        P("group", None),
        P(),
        P(),
        P(),
    )
    return jax.shard_map(
        shards, mesh=fine, in_specs=placed, out_specs=P(("group", *dev), None), check_vma=False
    )
```

time: 260 us -> 157 us (0.60)
  waiting for transfers between devices: 103 us -> 63.3 us
  blocking collectives: 51 us -> 28.6 us
  local copies, waits for them, and re-layouts: 34 us -> 14.9 us
  matrix products: 21.3 us -> 2.81 us
  Pallas kernels: 0 us -> 17.3 us
  other arithmetic: 17 us -> 2.67 us
  starting transfers between devices: 30.6 us -> 26.3 us
    all_to_all x5 -> x4, waiting for transfers between devices: 103 us -> 61.5 us  [the longest x3 54.5 us: exchange(): return lax.all_to_all(blocks, axes, 0, 0, tiled=True).reshape(array.shape)]
    all_to_all x1 -> x3, blocking collectives: 51 us -> 28.6 us  [shards(): tiles = lax.all_to_all(sums, axis, 0, 0, tiled=True)]
    dot_general x13 -> x1, matrix products: 21.3 us -> 2.81 us  [shards(): sums = jnp.dot(head_values, w_o, preferred_element_type=F32)]
    pallas_call x0 -> x6, Pallas kernels: none -> 17.3 us  [the longest x1 10.4 us: attend(): pl.pallas_call(attend_kernel, out_shape=jax.ShapeDtypeStruct((rows, PART)...]
    unnamed x27 -> x22, local copies, waits for them, and re-layouts: 4.57 us -> 12 us
    slice x5 -> x0, local copies, waits for them, and re-layouts: 6.29 us -> none  [the longest x3 4.72 us: side_by_side(): slab = whole[..., at:at + column.shape[along]]]
    squeeze x1 -> x0, local copies, waits for them, and re-layouts: 5.22 us -> none  [holder_partials(): cache_slots[slot_id]]
    another operation x7 -> x0, local copies, waits for them, and re-layouts: 5.03 us -> none  [the longest x4 3.99 us: holder_partials(): return (jnp.stack(log_list, axis=1), jnp.stack(mix_list, axis=1))]
  transfers between devices with their start and end apart: 5 -> 6, of which waited for: 5 -> 6; matrix products, arithmetic and copies ran while one was open for 9% -> 7% of each run, Pallas kernels for 0% -> 1%
where the time goes in v1:
time: 157 us; the launch traced here: 156 us
  waiting for transfers between devices  63.3 us (40%)
  blocking collectives  28.6 us (18%)
  starting transfers between devices  26.3 us (17%)
  Pallas kernels  17.3 us (11%)
  local copies, waits for them, and re-layouts  14.9 us (9%)
  matrix products  2.81 us (2%)
  other arithmetic  2.67 us (2%)
    all_to_all x3, waiting for transfers between devices, exchange(): return lax.all_to_all(blocks, axes, 0, 0, tiled=True).reshape(array.shape)  54.5 us
    all_to_all x3, blocking collectives, shards(): tiles = lax.all_to_all(sums, axis, 0, 0, tiled=True)  28.6 us
    all_to_all x3, starting transfers between devices, exchange(): return lax.all_to_all(blocks, axes, 0, 0, tiled=True).reshape(array.shape)  21.2 us
    unnamed x22, local copies, waits for them, and re-layouts  12 us
    pallas_call x1, Pallas kernels, attend(): pl.pallas_call(attend_kernel, out_shape=jax.ShapeDtypeStruct((rows, PART)...  10.4 us
    all_to_all x1, waiting for transfers between devices, shards(): lax.all_to_all(spread, ('group', 'core'), 0, 0, tiled=True)  7.07 us
    pallas_call x5, Pallas kernels, call(): pl.pallas_call(kernel, out_shape=outs, in_specs=specs, out_specs=jax.tree...  6.96 us
    all_to_all x1, starting transfers between devices, shards(): lax.all_to_all(spread, ('group', 'core'), 0, 0, tiled=True)  4.47 us
  transfers between devices with their start and end apart: 6, of which 6 were waited for; matrix products, arithmetic and copies ran while one was open for 7% of the time, Pallas kernels for 1%

profile of v1, /device:TPU:32, one launch (start us, length us, event | category | flops | bytes accessed | tf_op | source)
XLA Modules:
  0.0 156.1 jit_solution(15465267412782068627)
XLA Ops:
  0.0 1.1 copy-done.4
  1.2 1.0 copy-done.5
  2.1 0.9 copy-done.6
  4.2 4.5 %all-to-all-start = ((bf16[8,64,384]{2,1,0:T(8,128)(2,1)}), bf16[8,64,384]{2,1,0:T(8,128)(2,1)S(1)}, u32[]{:S(2)}, u32[]{:S(2)}) async-start(bf16[8,64,384]{2,1,0:T(8,128)(2,1)} %broadcast_in_dim.38), calls=%async_computation | async-start | bytes 786432 | tf_op jit(solution)/shard_map/all_to_all | solution.py:288
  10.5 7.1 %all-to-all-done = bf16[8,64,384]{2,1,0:T(8,128)(2,1)S(1)} async-done(((bf16[8,64,384]{2,1,0:T(8,128)(2,1)}), bf16[8,64,384]{2,1,0:T(8,128)(2,1)S(1)}, u32[]{:S(2)}, u32[]{:S(2)}) %all-to-all-start) | async-done | bytes 393248 | tf_op jit(solution)/shard_map/all_to_all | solution.py:288
  17.6 0.9 copy-done.1
  18.5 2.0 %shard_map.110 = bf16[256,2304]{1,0:T(8,128)(2,1)} custom-call(s32[1]{0:T(128)} %bitcast.core_ref, bf16[512,384]{1,0:T(8,128)(2,1)S(1)} %bitcast.29, s32[512,1]{1,0:T(8,128)S(1)} %select_n.56.code_ref, bf16[2,128,512]{2,1,0:T(8,128)(2,1)S(1)} %copy-done.1, bf16[2,128,512]{2,1,0:T(8,128)(2,1)S(1)} %collective-permute-done.mate_ref), custom_call_target="tpu_custom_call" | custom-call | tf_op jit(solution)/shard_map/pallas_call | solution.py:40
  20.6 11.2 %all-to-all-start.1 = ((bf16[32,8,2304]{2,1,0:T(8,128)(2,1)}), bf16[32,8,2304]{2,1,0:T(8,128)(2,1)S(1)}, u32[]{:S(2)}, u32[]{:S(2)}) async-start(bf16[32,8,2304]{2,1,0:T(8,128)(2,1)} %bitcast.6), calls=%async_computation.1 | async-start | bytes 2359296 | tf_op jit(solution)/shard_map/all_to_all | solution.py:237
  32.6 7.7 %copy.25 = bf16[1,1,2,2048,576]{4,3,2,1,0:T(8,128)(2,1)} copy(bf16[1,1,2,2048,576]{3,4,2,1,0:T(8,128)(2,1)} %param.17) | data formatting | bytes 9437184 | tf_op args[6]
  40.7 20.8 %all-to-all-done.1 = bf16[32,8,2304]{2,1,0:T(8,128)(2,1)S(1)} async-done(((bf16[32,8,2304]{2,1,0:T(8,128)(2,1)}), bf16[32,8,2304]{2,1,0:T(8,128)(2,1)S(1)}, u32[]{:S(2)}, u32[]{:S(2)}) %all-to-all-start.1) | async-done | bytes 1179680 | tf_op jit(solution)/shard_map/all_to_all | solution.py:237
  61.6 10.4 %shard_map.111 = bf16[256,2176]{1,0:T(8,128)(2,1)} custom-call(s32[2]{0:T(128)S(1)} %compare_select_fusion.1.count_ref, bf16[256,2304]{1,0:T(8,128)(2,1)S(1)} %bitcast.27, bf16[2,2048,576]{2,1,0:T(8,128)(2,1)} %bitcast.31), custom_call_target="tpu_custom_call" | custom-call | tf_op jit(solution)/shard_map/pallas_call | solution.py:153
  71.9 6.6 %all-to-all-start.2 = ((bf16[32,8,2176]{2,1,0:T(8,128)(2,1)}), bf16[32,8,2176]{2,1,0:T(8,128)(2,1)S(1)}, u32[]{:S(2)}, u32[]{:S(2)}) async-start(bf16[32,8,2176]{2,1,0:T(8,128)(2,1)} %bitcast.9), calls=%async_computation.2 | async-start | bytes 2228224 | tf_op jit(solution)/shard_map/all_to_all | solution.py:237
  79.1 1.1 collective-permute-done.1.mate_ref
  80.2 26.1 %all-to-all-done.2 = bf16[32,8,2176]{2,1,0:T(8,128)(2,1)S(1)} async-done(((bf16[32,8,2176]{2,1,0:T(8,128)(2,1)}), bf16[32,8,2176]{2,1,0:T(8,128)(2,1)S(1)}, u32[]{:S(2)}, u32[]{:S(2)}) %all-to-all-start.2) | async-done | bytes 1114144 | tf_op jit(solution)/shard_map/all_to_all | solution.py:237
  106.2 2.7 %shard_map.112 = bf16[512,384]{1,0:T(8,128)(2,1)} custom-call(s32[1]{0:T(128)} %bitcast.core_ref, bf16[256,2176]{1,0:T(8,128)(2,1)S(1)} %bitcast.28, s32[2,256]{1,0:T(2,128)S(1)} %add_select_fusion.1.code_ref, bf16[2,512,128]{2,1,0:T(8,128)(2,1)S(1)} %copy-done.3, bf16[2,512,128]{2,1,0:T(8,128)(2,1)S(1)} %collective-permute-done.1.mate_ref), custom_call_target="tpu_custom_call" | custom-call | tf_op jit(solution)/shard_map/pallas_call | solution.py:40
  108.9 3.5 %all-to-all-start.3 = ((bf16[8,64,384]{2,1,0:T(8,128)(2,1)}), bf16[8,64,384]{2,1,0:T(8,128)(2,1)S(1)}, u32[]{:S(2)}, u32[]{:S(2)}) async-start(bf16[8,64,384]{2,1,0:T(8,128)(2,1)} %bitcast.11), calls=%async_computation.3 | async-start | bytes 786432 | tf_op jit(solution)/shard_map/all_to_all | solution.py:237
  112.4 1.1 shard_map.113
  113.6 7.6 %all-to-all-done.3 = bf16[8,64,384]{2,1,0:T(8,128)(2,1)S(1)} async-done(((bf16[8,64,384]{2,1,0:T(8,128)(2,1)}), bf16[8,64,384]{2,1,0:T(8,128)(2,1)S(1)}, u32[]{:S(2)}, u32[]{:S(2)}) %all-to-all-start.3) | async-done | bytes 393248 | tf_op jit(solution)/shard_map/all_to_all | solution.py:237
  121.2 0.8 shard_map.114
  122.0 2.8 %convolution_convert_fusion = bf16[64,7168]{1,0:T(8,128)(2,1)S(1)} fusion(bf16[64,256]{1,0:T(8,128)(2,1)S(1)} %shard_map.114, bf16[256,7168]{1,0:T(8,128)(2,1)} %param.16), kind=kOutput, calls=%fused_computation | convolution fusion | flops 235339776 | bytes 4620288 | tf_op jit(solution)/shard_map/dot_general | solution.py:325
  124.9 4.5 %all_to_all.35 = bf16[2,32,7168]{2,1,0:T(8,128)(2,1)S(1)} all-to-all(bf16[2,32,7168]{2,1,0:T(8,128)(2,1)S(1)} %bitcast.32), channel_id=1, replica_groups=mesh['group'=4,'z'=8,'x'=4,'core'=2] {'core'}, dimensions={0} | all-to-all | bytes 1835008 | tf_op jit(solution)/shard_map/all_to_all | solution.py:328
  129.7 12.9 %all_to_all.36 = bf16[4,8,7168]{2,1,0:T(8,128)(2,1)S(1)} all-to-all(bf16[4,8,7168]{2,1,0:T(8,128)(2,1)S(1)} %bitcast.33), channel_id=1, replica_groups=mesh['group'=4,'z'=8,'x'=4,'core'=2] {'x'}, dimensions={0} | all-to-all | bytes 917504 | tf_op jit(solution)/shard_map/all_to_all | solution.py:328
  143.9 11.3 %all_to_all.37 = bf16[8,2,3584]{2,1,0:T(2,128)(2,1)S(1)} all-to-all(bf16[8,2,3584]{2,1,0:T(2,128)(2,1)S(1)} %reshape.199), channel_id=1, replica_groups=mesh['group'=4,'z'=8,'x'=4,'core'=2] {'z'}, dimensions={0} | all-to-all | bytes 229376 | tf_op jit(solution)/shard_map/all_to_all | solution.py:328
  155.3 0.8 convert_reduce_fusion
  (51 shorter events, 6.7 us)
Async XLA Ops:
  0.0 9.2 %copy-start = (s32[4,64,2]{1,2,0:T(2,128)S(1)}, s32[4,64,2]{1,2,0:T(2,128)}, u32[]{:S(2)}) copy-start(s32[4,64,2]{1,2,0:T(2,128)} %param.20) | copy-start | bytes 6148
  0.0 1.1 copy-start.4
  1.2 1.0 copy-start.5
  2.1 0.9 copy-start.6
  4.2 13.4 %all-to-all-start = ((bf16[8,64,384]{2,1,0:T(8,128)(2,1)}), bf16[8,64,384]{2,1,0:T(8,128)(2,1)S(1)}, u32[]{:S(2)}, u32[]{:S(2)}) async-start(bf16[8,64,384]{2,1,0:T(8,128)(2,1)} %broadcast_in_dim.38), calls=%async_computation | async-start | bytes 786432 | tf_op jit(solution)/shard_map/all_to_all | solution.py:288
  8.6 1.9 %collective-permute-start = (bf16[2,128,512]{2,1,0:T(8,128)(2,1)}, bf16[2,128,512]{2,1,0:T(8,128)(2,1)S(1)}, u32[]{:S(2)}, u32[]{:S(2)}) collective-permute-start(bf16[2,128,512]{2,1,0:T(8,128)(2,1)} %uk_ref.1), channel_id=1, source_target_pairs={{0,1},{1,0},{2,3},{3,2},{4,5},{5,4},{6,7},{7,6},{8,9},{9,8},{10,11... | collective-permute-start | bytes 786440 | tf_op jit(solution)/shard_map/ppermute | solution.py:258
  17.6 1.0 copy-start.1
  20.6 41.0 %all-to-all-start.1 = ((bf16[32,8,2304]{2,1,0:T(8,128)(2,1)}), bf16[32,8,2304]{2,1,0:T(8,128)(2,1)S(1)}, u32[]{:S(2)}, u32[]{:S(2)}) async-start(bf16[32,8,2304]{2,1,0:T(8,128)(2,1)} %bitcast.6), calls=%async_computation.1 | async-start | bytes 2359296 | tf_op jit(solution)/shard_map/all_to_all | solution.py:237
  32.6 7.9 %copy-start.8 = (s32[64]{0:T(128)S(1)}, s32[64]{0:T(128)}, u32[]{:S(2)}) copy-start(s32[64]{0:T(128)} %param.19) | copy-start | bytes 772
  61.6 17.0 %copy-start.3 = (bf16[2,512,128]{2,1,0:T(8,128)(2,1)S(1)}, bf16[2,512,128]{2,1,0:T(8,128)(2,1)}, u32[]{:S(2)}) copy-start(bf16[2,512,128]{2,1,0:T(8,128)(2,1)} %uv_ref.1) | copy-start | bytes 786436
  71.9 40.4 %copy-start.2 = (bf16[2,128,512]{2,1,0:T(8,128)(2,1)S(1)}, bf16[2,128,512]{2,1,0:T(8,128)(2,1)}, u32[]{:S(2)}) copy-start(bf16[2,128,512]{2,1,0:T(8,128)(2,1)} %uk_ref.1) | copy-start | bytes 786436
  71.9 40.4 %copy-start.7 = (bf16[64,576]{1,0:T(8,128)(2,1)S(1)}, bf16[64,576]{1,0:T(8,128)(2,1)}, u32[]{:S(2)}) copy-start(bf16[64,576]{1,0:T(8,128)(2,1)} %kv_ref.1) | copy-start | bytes 221188
  71.9 34.3 %all-to-all-start.2 = ((bf16[32,8,2176]{2,1,0:T(8,128)(2,1)}), bf16[32,8,2176]{2,1,0:T(8,128)(2,1)S(1)}, u32[]{:S(2)}, u32[]{:S(2)}) async-start(bf16[32,8,2176]{2,1,0:T(8,128)(2,1)} %bitcast.9), calls=%async_computation.2 | async-start | bytes 2228224 | tf_op jit(solution)/shard_map/all_to_all | solution.py:237
  78.5 1.6 %collective-permute-start.1 = (bf16[2,512,128]{2,1,0:T(8,128)(2,1)S(1)}, bf16[2,512,128]{2,1,0:T(8,128)(2,1)S(1)}, u32[]{:S(2)}, u32[]{:S(2)}) collective-permute-start(bf16[2,512,128]{2,1,0:T(8,128)(2,1)S(1)} %copy-done.3), channel_id=1, source_target_pairs={{0,1},{1,0},{2,3},{3,2},{4,5},{5,4},{6,7},{7,6},{8,9},{9,8},{10,11... | collective-permute-start | bytes 786440 | tf_op jit(solution)/shard_map/ppermute | solution.py:259
  108.9 12.3 %all-to-all-start.3 = ((bf16[8,64,384]{2,1,0:T(8,128)(2,1)}), bf16[8,64,384]{2,1,0:T(8,128)(2,1)S(1)}, u32[]{:S(2)}, u32[]{:S(2)}) async-start(bf16[8,64,384]{2,1,0:T(8,128)(2,1)} %bitcast.11), calls=%async_computation.3 | async-start | bytes 786432 | tf_op jit(solution)/shard_map/all_to_all | solution.py:237

commit v2 on v1

v2 whole, which is shorter than its diff:
```python
import jax
import jax.numpy as jnp
from jax import lax
from jax.experimental import pallas as pl
from jax.experimental.pallas import tpu as pltpu
from jax.sharding import Mesh
from jax.sharding import PartitionSpec as P

NOPE = 128
ROPE = 64
LATENT = 512
VDIM = 128
DRAFT = 4
SEQ_GRP = 16
TOK_GRP = SEQ_GRP * DRAFT
SLOTS = 2
KEY = LATENT + ROPE
WIDE = 2 * LATENT + 2 * ROPE
PART = SLOTS * 2 * LATENT + 128
NARROW = 2 * NOPE + 2 * ROPE
EMPTY = -1e30
SCALE = (NOPE + ROPE) ** -0.5
F32 = jnp.float32
BF16 = jnp.bfloat16
CONTRACT_LAST = (((1,), (1,)), ((), ()))

VMEM = pl.BlockSpec(memory_space=pltpu.VMEM)
SMEM = pl.BlockSpec(memory_space=pltpu.SMEM)


def dot(a, b):
    return jnp.dot(a, b, preferred_element_type=F32)


def dot_t(a, b):
    return lax.dot_general(a, b, CONTRACT_LAST, preferred_element_type=F32)


def call(kernel, outs, args, specs, scratch=(), vmem=32):
    return pl.pallas_call(
        kernel,
        out_shape=outs,
        in_specs=specs,
        out_specs=jax.tree.map(lambda _: VMEM, outs),
        scratch_shapes=list(scratch),
        compiler_params=pltpu.CompilerParams(vmem_limit_bytes=vmem << 20),
    )(*args)


def three_terms(value):
    high = value.astype(BF16).astype(F32)
    middle = (value - high).astype(BF16).astype(F32)
    return high, middle, (value - high - middle).astype(BF16).astype(F32)


def put_terms(tile, value, first):
    lane = lax.broadcasted_iota(jnp.int32, tile.shape, 1)
    for i, term in enumerate(three_terms(value)):
        tile = jnp.where(lane == first + i, term, tile)
    return tile


def project_kernel(q_ref, wn_ref, wr_ref, out_ref):
    narrow = dot(q_ref[...], wn_ref[...]).astype(BF16)
    ropes = (dot(q_ref[...], wr_ref[...]) * SCALE).astype(BF16)
    for copy in range(out_ref.shape[0]):
        out_ref[copy, :, : 2 * NOPE] = narrow
        out_ref[copy, :, 2 * NOPE :] = ropes


def spread_kernel(core_ref, q_ref, code_ref, own_ref, mate_ref, out_ref, rows):
    core = core_ref[0]
    rows[...] = jnp.zeros_like(rows)
    for block in range(q_ref.shape[0] // TOK_GRP):
        at = pl.ds(block * TOK_GRP, TOK_GRP)
        side = pl.multiple_of(jnp.where(core == block % 2, 0, NOPE), NOPE)
        for par in range(2):
            rows[at, pl.ds(par * 2 * NOPE + side, NOPE)] = q_ref[at, par * NOPE : (par + 1) * NOPE]
        rows[at, 4 * NOPE :] = q_ref[at, 2 * NOPE :]
    count = code_ref.shape[0] // SLOTS
    for slot in range(SLOTS):
        code = code_ref[slot * count : (slot + 1) * count, :]
        column = lax.broadcasted_iota(jnp.int32, (count, rows.shape[0]), 1)
        picked = dot(jnp.where(column == code, 1.0, 0.0).astype(BF16), rows[...]).astype(BF16)
        for par in range(2):
            weight = jnp.concatenate([own_ref[par], mate_ref[par]], axis=0)
            absorbed = dot(picked[:, par * 2 * NOPE : (par + 1) * 2 * NOPE], weight) * SCALE
            first = slot * WIDE + par * LATENT
            out_ref[:, first : first + LATENT] = absorbed.astype(BF16)
        out_ref[:, slot * WIDE + 2 * LATENT : (slot + 1) * WIDE] = picked[:, 4 * NOPE :]


def draft_kernel(place_ref, q_ref, own_uk, mate_uk, own_uv, mate_uv, kv_ref, hv_ref, log_ref):
    group, core = place_ref[0], place_ref[1]
    half = hv_ref.shape[0]
    row = 2 * lax.broadcasted_iota(jnp.int32, (half, TOK_GRP), 0) + core
    col = lax.broadcasted_iota(jnp.int32, (half, TOK_GRP), 1)
    seen = (row // DRAFT == col // DRAFT) & (col <= row)
    pick = jnp.where(row == col, 1.0, 0.0).astype(BF16)
    lane = lax.broadcasted_iota(jnp.int32, log_ref.shape, 1)
    logs = jnp.zeros(log_ref.shape, F32)
    for hp in range(2):
        at = pl.multiple_of((group * 2 + hp) * TOK_GRP, TOK_GRP)
        rows = dot(pick, q_ref[pl.ds(at, TOK_GRP), :]).astype(BF16)
        for par in range(2):
            uk = jnp.where(core == hp, own_uk[par], mate_uk[par])
            uv = jnp.where(core == hp, own_uv[par], mate_uv[par])
            absorbed = (dot(rows[:, par * NOPE : (par + 1) * NOPE], uk) * SCALE).astype(BF16)
            first = 2 * NOPE + par * ROPE
            scores = dot_t(absorbed, kv_ref[:, :LATENT])
            scores += dot_t(rows[:, first : first + ROPE], kv_ref[:, LATENT:])
            scores = jnp.where(seen, scores, EMPTY)
            peak = jnp.max(scores, axis=1, keepdims=True)
            weights = jnp.where(seen, jnp.exp(scores - peak), 0.0)
            total = jnp.sum(weights, axis=1, keepdims=True)
            mixture = dot(weights.astype(BF16), kv_ref[:, :LATENT]) / total
            head = hp * 2 + par
            hv_ref[:, head * VDIM : (head + 1) * VDIM] = dot(mixture.astype(BF16), uv)
            logs = jnp.where(lane == head, peak + jnp.log(total), logs)
    log_ref[...] = logs


def attend_kernel(count_ref, x_ref, kv_ref, out_ref, queries, scores):
    slot = pl.program_id(0)
    count = count_ref[slot]
    half = x_ref.shape[0]
    for par in range(2):
        at = slice(par * half, (par + 1) * half)
        queries[at, :LATENT] = x_ref[:, par * LATENT : (par + 1) * LATENT]
        first = 2 * LATENT + par * ROPE
        queries[at, LATENT:] = x_ref[:, first : first + ROPE]
    slab = kv_ref.shape[1]
    chunk = 512
    peak = jnp.full((2 * half, 1), EMPTY, F32)
    for first in range(0, slab, chunk):
        score = dot(queries[...], kv_ref[:, first : first + chunk])
        position = lax.broadcasted_iota(jnp.int32, score.shape, 1) + first
        score = jnp.where(position < count, score, EMPTY)
        scores[:, first : first + chunk] = score
        peak = jnp.maximum(peak, jnp.max(score, axis=1, keepdims=True))
    reference = jnp.maximum(peak, EMPTY / 10)
    total = jnp.zeros((2 * half, 1), F32)
    mixture = jnp.zeros((2 * half, LATENT), F32)
    for first in range(0, slab, chunk):
        weights = jnp.exp(scores[:, first : first + chunk] - reference)
        total += jnp.sum(weights, axis=1, keepdims=True)
        mixture += dot_t(weights.astype(BF16), kv_ref[:LATENT, first : first + chunk])
    total = jnp.maximum(total, 1.0)
    mixture = (mixture / total).astype(BF16)
    log = peak + jnp.log(total)
    start = slot * 2 * LATENT
    lane = lax.broadcasted_iota(jnp.int32, (half, 128), 1)
    tile = jnp.where(slot == 0, jnp.zeros((half, 128), F32), out_ref[:, SLOTS * 2 * LATENT :].astype(F32))
    for par in range(2):
        at = slice(par * half, (par + 1) * half)
        out_ref[:, pl.ds(pl.multiple_of(start + par * LATENT, LATENT), LATENT)] = mixture[at]
        for i, term in enumerate(three_terms(log[at])):
            tile = jnp.where(lane == slot * 6 + par * 3 + i, term, tile)
    out_ref[:, SLOTS * 2 * LATENT :] = tile.astype(BF16)


def attend(count, x, kv):
    rows = x.shape[0]
    slab = kv.shape[2]
    return pl.pallas_call(
        attend_kernel,
        out_shape=jax.ShapeDtypeStruct((rows, PART), BF16),
        grid_spec=pltpu.PrefetchScalarGridSpec(
            num_scalar_prefetch=1,
            grid=(SLOTS,),
            in_specs=[
                pl.BlockSpec((rows, WIDE), lambda k, _: (0, k)),
                pl.BlockSpec((None, KEY, slab), lambda k, _: (k, 0, 0)),
            ],
            out_specs=pl.BlockSpec((rows, PART), lambda k, _: (0, 0)),
            scratch_shapes=[
                pltpu.VMEM((2 * rows, KEY), BF16),
                pltpu.VMEM((2 * rows, slab), F32),
            ],
        ),
        compiler_params=pltpu.CompilerParams(
            dimension_semantics=("arbitrary",), vmem_limit_bytes=48 << 20
        ),
    )(count, x, kv)


def merge_kernel(core_ref, y_ref, code_ref, own_ref, mate_ref, out_ref):
    core = core_ref[0]
    rows, cols = out_ref.shape[0], y_ref.shape[0]
    base = SLOTS * 2 * LATENT
    logs = jnp.transpose(y_ref[:, base:].astype(F32))
    row = lax.broadcasted_iota(jnp.int32, (rows, cols), 0)
    tile = jnp.zeros((rows, 128), F32)
    for hp in range(2):
        match = [row == code_ref[hp * 2 + slot : hp * 2 + slot + 1, :] for slot in range(SLOTS)]
        for par in range(2):
            held = []
            for slot in range(SLOTS):
                at = slot * 6 + par * 3
                log = logs[at : at + 1, :] + logs[at + 1 : at + 2, :] + logs[at + 2 : at + 3, :]
                held.append(jnp.where(match[slot], log, EMPTY))
            peak = jnp.max(jnp.maximum(held[0], held[1]), axis=1, keepdims=True)
            total = jnp.zeros((rows, 1), F32)
            mixture = jnp.zeros((rows, LATENT), F32)
            for slot in range(SLOTS):
                weights = jnp.where(match[slot], jnp.exp(held[slot] - peak), 0.0)
                total += jnp.sum(weights, axis=1, keepdims=True)
                first = slot * 2 * LATENT + par * LATENT
                mixture += dot(weights.astype(BF16), y_ref[:, first : first + LATENT])
            total = jnp.maximum(total, 1.0)
            mixture = (mixture / total).astype(BF16)
            head = hp * 2 + par
            values = dot(mixture, jnp.where(core == hp, own_ref[par], mate_ref[par]))
            out_ref[:, head * VDIM : (head + 1) * VDIM] = values.astype(BF16)
            tile = put_terms(tile, peak + jnp.log(total), head * 3)
    out_ref[:, 4 * VDIM :] = tile.astype(BF16)


def finish_kernel(core_ref, z_ref, hv_ref, log_ref, own_ref, mate_ref, out_ref):
    half = hv_ref.shape[0]
    values = []
    for head in range(4):
        logs = [log_ref[:, head : head + 1]]
        parts = [hv_ref[:, head * VDIM : (head + 1) * VDIM]]
        for block in range(z_ref.shape[0] // half):
            at = slice(block * half, (block + 1) * half)
            terms = z_ref[at, 4 * VDIM :].astype(F32)
            first = head * 3
            logs.append(
                terms[:, first : first + 1]
                + terms[:, first + 1 : first + 2]
                + terms[:, first + 2 : first + 3]
            )
            parts.append(z_ref[at, head * VDIM : (head + 1) * VDIM].astype(F32))
        peak = logs[0]
        for log in logs[1:]:
            peak = jnp.maximum(peak, log)
        total = jnp.zeros_like(peak)
        summed = jnp.zeros_like(parts[0])
        for log, part in zip(logs, parts):
            weight = jnp.exp(log - peak)
            total += weight
            summed += weight * part
        values.append(summed / total)
    pairs = [jnp.concatenate(values[hp * 2 : hp * 2 + 2], axis=1) for hp in range(2)]
    own = jnp.where(core_ref[0] == 0, pairs[0], pairs[1]).astype(BF16)
    mate = jnp.where(core_ref[0] == 0, pairs[1], pairs[0]).astype(BF16)
    out_ref[...] = (dot(own, own_ref[...]) + dot(mate, mate_ref[...])).astype(BF16)


def exchange(array, axes, peers):
    blocks = array.reshape(peers, array.shape[0] // peers, *array.shape[1:])
    return lax.all_to_all(blocks, axes, 0, 0, tiled=True).reshape(array.shape)


def shards(
    q_compressed,
    w_q_nope,
    w_q_rope,
    w_uk,
    w_uv,
    w_o,
    kv_cache,
    draft_kv,
    context_length,
    slot_sequence,
    slot_slab,
):
    groups, zs, xs, cores = (lax.axis_size(a) for a in ("group", "z", "x", "core"))
    group, z, x, core = (lax.axis_index(a) for a in ("group", "z", "x", "core"))
    chips = zs * xs
    core_id = core.astype(jnp.int32).reshape(1)
    swap = [(i, 1 - i) for i in range(cores)]
    mate_uk = lax.ppermute(w_uk, "core", swap)

    table = lax.dynamic_index_in_dim(slot_sequence, group, 0, keepdims=False)
    table = table.reshape(chips, cores, SLOTS)
    held = lax.dynamic_index_in_dim(table, core, 1, keepdims=False)
    hp = jnp.arange(2, dtype=jnp.int32)[:, None]
    draft = jnp.arange(DRAFT, dtype=jnp.int32)
    filled = (held >= 0).T[:, :, None]
    code = ((held >> 4) * (2 * TOK_GRP) + (held & 15) * DRAFT).T[:, :, None]
    code = jnp.where(filled, code + (hp * TOK_GRP + draft).reshape(-1), -1).reshape(-1, 1)
    row = ((held >> 4) * TOK_GRP + (held & 15) * 2).T[:, :, None, None]
    row = row + (draft & 1) * (TOK_GRP // 2) + (draft >> 1)
    row = jnp.where(filled[..., None], row, -1)
    row = jnp.where(hp == hp.reshape(2, 1, 1, 1, 1), row, -1).reshape(2 * SLOTS, -1)

    chip = z * xs + x
    mine = lax.dynamic_index_in_dim(held, chip, 0, keepdims=False)
    slabs = lax.dynamic_index_in_dim(slot_slab, group, 0, keepdims=False).reshape(chips, cores, SLOTS)
    slabs = lax.dynamic_index_in_dim(slabs, chip, 0, keepdims=False)
    slabs = lax.dynamic_index_in_dim(slabs, core, 0, keepdims=False)
    is_mine = mine[:, None] == jnp.arange(context_length.shape[0], dtype=jnp.int32)
    length = jnp.sum(jnp.where(is_mine, context_length, 0), axis=1)
    count = jnp.where(mine >= 0, length - slabs * kv_cache.shape[3], 0).astype(jnp.int32)

    copies = groups * cores
    narrow = pl.pallas_call(
        project_kernel,
        out_shape=jax.ShapeDtypeStruct((copies, TOK_GRP, NARROW), BF16),
        compiler_params=pltpu.CompilerParams(vmem_limit_bytes=32 << 20),
    )(q_compressed, w_q_nope, w_q_rope)
    every = lax.all_to_all(narrow, ("group", "core"), 0, 0, tiled=True).reshape(-1, NARROW)
    rows = chips * cores * DRAFT
    wide = call(
        spread_kernel,
        jax.ShapeDtypeStruct((rows, SLOTS * WIDE), BF16),
        (core_id, every, code, w_uk, mate_uk),
        [SMEM] + [VMEM] * 4,
        [pltpu.VMEM((copies * TOK_GRP, 5 * NOPE), BF16)],
    )
    late_o, late_uv, wide = lax.optimization_barrier((w_o, w_uv, wide))
    mate_uv = lax.ppermute(late_uv, "core", swap)
    mate_o = lax.ppermute(late_o, "core", swap)
    arrived = exchange(wide, ("z", "x"), chips)
    place = jnp.stack([group, core]).astype(jnp.int32)
    draft_hv, draft_log = call(
        draft_kernel,
        (
            jax.ShapeDtypeStruct((TOK_GRP // 2, 4 * VDIM), F32),
            jax.ShapeDtypeStruct((TOK_GRP // 2, 128), F32),
        ),
        (place, every, w_uk, mate_uk, w_uv, mate_uv, draft_kv),
        [SMEM] + [VMEM] * 6,
    )
    partials = attend(count, arrived, jnp.swapaxes(kv_cache.reshape(kv_cache.shape[2:]), 1, 2))
    back = exchange(partials, ("z", "x"), chips)
    merged = call(
        merge_kernel,
        jax.ShapeDtypeStruct((groups * TOK_GRP, 4 * VDIM + 128), BF16),
        (core_id, back, row, w_uv, mate_uv),
        [SMEM] + [VMEM] * 4,
    )
    home = exchange(merged, ("group", "core"), copies)
    sums = call(
        finish_kernel,
        jax.ShapeDtypeStruct((chips, w_o.shape[1]), BF16),
        (core_id, home, draft_hv, draft_log, w_o, mate_o),
        [SMEM] + [VMEM] * 5,
    )
    tiles = lax.all_to_all(sums.reshape(chips, 8, -1), ("z", "x"), 0, 0, tiled=True)
    return jnp.sum(tiles.astype(F32), axis=0).reshape(1, -1)


def solution(mesh):
    fine = Mesh(mesh.devices.reshape(4, 8, 4, 2), ("group", "z", "x", "core"))
    dev = ("z", "x", "core")
    placed = (
        P("group", None),
        P(None, dev),
        P(None, dev),
        P(dev, None, None),
        P(dev, None, None),
        P(dev, None),
        P("group", dev, None, None, None),
        P("group", None),
        P(),
        P(),
        P(),
    )
    return jax.shard_map(
        shards, mesh=fine, in_specs=placed, out_specs=P(("group", *dev), None), check_vma=False
    )
```

time: 157 us -> 149 us (0.949)
  local copies, waits for them, and re-layouts: 14.9 us -> 7.31 us
  blocking collectives: 28.6 us -> 21.5 us
  waiting for transfers between devices: 63.3 us -> 69.2 us
  Pallas kernels: 17.3 us -> 22.8 us
  matrix products: 2.81 us -> 0 us
  other arithmetic: 2.67 us -> 0.96 us
    all_to_all x3 -> x1, blocking collectives: 28.6 us -> 21.5 us  [shards(): lax.all_to_all(sums.reshape(chips, 8, -1), ('z', 'x'), 0, 0, tiled=True)]
    unnamed x22 -> x21, local copies, waits for them, and re-layouts: 12 us -> 5.94 us
    all_to_all x3, waiting for transfers between devices: 54.5 us -> 59.7 us  [exchange(): return lax.all_to_all(blocks, axes, 0, 0, tiled=True).reshape(array.shape)]
    pallas_call x5 -> x4, Pallas kernels: 6.96 us -> 11.5 us  [call(): pl.pallas_call(kernel, out_shape=outs, in_specs=specs, out_specs=jax.tree...]
    dot_general x1 -> x0, matrix products: 2.81 us -> none  [shards(): sums = jnp.dot(head_values, w_o, preferred_element_type=F32)]
  transfers between devices with their start and end apart: 6 -> 7, of which waited for: 6 -> 5; matrix products, arithmetic and copies ran while one was open for 7% -> 2% of each run, Pallas kernels for 1% -> 11%
where the time goes in v2:
time: 149 us; the launch traced here: 148 us
  waiting for transfers between devices  69.2 us (46%)
  starting transfers between devices  26.1 us (18%)
  Pallas kernels  22.8 us (15%)
  blocking collectives  21.5 us (14%)
  local copies, waits for them, and re-layouts  7.31 us (5%)
    all_to_all x3, waiting for transfers between devices, exchange(): return lax.all_to_all(blocks, axes, 0, 0, tiled=True).reshape(array.shape)  59.7 us
    all_to_all x1, blocking collectives, shards(): lax.all_to_all(sums.reshape(chips, 8, -1), ('z', 'x'), 0, 0, tiled=True)  21.5 us
    all_to_all x3, starting transfers between devices, exchange(): return lax.all_to_all(blocks, axes, 0, 0, tiled=True).reshape(array.shape)  21.3 us
    pallas_call x4, Pallas kernels, call(): pl.pallas_call(kernel, out_shape=outs, in_specs=specs, out_specs=jax.tree...  11.5 us
    pallas_call x1, Pallas kernels, attend(): pl.pallas_call(attend_kernel, out_shape=jax.ShapeDtypeStruct((rows, PART)...  10.2 us
    all_to_all x1, waiting for transfers between devices, shards(): lax.all_to_all(narrow, ('group', 'core'), 0, 0, tiled=True)  8.22 us
    unnamed x21, local copies, waits for them, and re-layouts  5.94 us
    all_to_all x1, starting transfers between devices, shards(): lax.all_to_all(narrow, ('group', 'core'), 0, 0, tiled=True)  4.53 us
  transfers between devices with their start and end apart: 7, of which 5 were waited for; matrix products, arithmetic and copies ran while one was open for 2% of the time, Pallas kernels for 11%

profile of v2, /device:TPU:32, one launch (start us, length us, event | category | flops | bytes accessed | tf_op | source)
XLA Modules:
  0.0 148.0 jit_solution(18187047070659434909)
XLA Ops:
  0.0 1.2 copy-done.4
  1.2 1.0 copy-done.5
  2.2 0.9 copy-done.6
  3.1 1.1 shard_map.109
  4.2 4.5 %all-to-all-start = ((bf16[8,64,384]{2,1,0:T(8,128)(2,1)}), bf16[8,64,384]{2,1,0:T(8,128)(2,1)S(1)}, u32[]{:S(2)}, u32[]{:S(2)}) async-start(bf16[8,64,384]{2,1,0:T(8,128)(2,1)} %shard_map.109), calls=%async_computation | async-start | bytes 786432 | tf_op jit(solution)/shard_map/all_to_all | solution.py:304
  9.4 8.2 %all-to-all-done = bf16[8,64,384]{2,1,0:T(8,128)(2,1)S(1)} async-done(((bf16[8,64,384]{2,1,0:T(8,128)(2,1)}), bf16[8,64,384]{2,1,0:T(8,128)(2,1)S(1)}, u32[]{:S(2)}, u32[]{:S(2)}) %all-to-all-start) | async-done | bytes 393248 | tf_op jit(solution)/shard_map/all_to_all | solution.py:304
  17.7 2.0 %shard_map.110 = bf16[256,2304]{1,0:T(8,128)(2,1)} custom-call(s32[1]{0:T(128)} %bitcast.core_ref, bf16[512,384]{1,0:T(8,128)(2,1)S(1)} %bitcast.35, s32[512,1]{1,0:T(8,128)S(1)} %select_n.70.code_ref, bf16[2,128,512]{2,1,0:T(8,128)(2,1)S(1)} %copy-done.2, bf16[2,128,512]{2,1,0:T(8,128)(2,1)S(1)} %collective-permute-done.mate_ref.mate_uk), custom_call_target="tpu_custom_call" | custom-call | tf_op jit(solution)/shard_map/pallas_call | solution.py:40
  19.7 11.3 %all-to-all-start.1 = ((bf16[32,8,2304]{2,1,0:T(8,128)(2,1)}), bf16[32,8,2304]{2,1,0:T(8,128)(2,1)S(1)}, u32[]{:S(2)}, u32[]{:S(2)}) async-start(bf16[32,8,2304]{2,1,0:T(8,128)(2,1)} %bitcast.6), calls=%async_computation.1 | async-start | bytes 2359296 | tf_op jit(solution)/shard_map/all_to_all | solution.py:253
  31.1 0.7 constant_dynamic-slice_fusion.2
  31.9 0.2 fusion
  32.3 28.4 %all-to-all-done.1 = bf16[32,8,2304]{2,1,0:T(8,128)(2,1)S(1)} async-done(((bf16[32,8,2304]{2,1,0:T(8,128)(2,1)}), bf16[32,8,2304]{2,1,0:T(8,128)(2,1)S(1)}, u32[]{:S(2)}, u32[]{:S(2)}) %all-to-all-start.1) | async-done | bytes 1179680 | tf_op jit(solution)/shard_map/all_to_all | solution.py:253
  60.8 10.2 %shard_map.111 = bf16[256,2176]{1,0:T(8,128)(2,1)} custom-call(s32[2]{0:T(128)S(1)} %compare_select_fusion.1.count_ref, bf16[256,2304]{1,0:T(8,128)(2,1)S(1)} %bitcast.33, bf16[2,576,2048]{2,1,0:T(8,128)(2,1)} %bitcast.39), custom_call_target="tpu_custom_call" | custom-call | tf_op jit(solution)/shard_map/pallas_call | solution.py:165
  71.0 6.6 %all-to-all-start.2 = ((bf16[32,8,2176]{2,1,0:T(8,128)(2,1)}), bf16[32,8,2176]{2,1,0:T(8,128)(2,1)S(1)}, u32[]{:S(2)}, u32[]{:S(2)}) async-start(bf16[32,8,2176]{2,1,0:T(8,128)(2,1)} %bitcast.10), calls=%async_computation.2 | async-start | bytes 2228224 | tf_op jit(solution)/shard_map/all_to_all | solution.py:253
  77.9 0.2 select_n.69.code_ref
  78.1 1.2 collective-permute-done.1.mate_ref.mate_uv
  79.3 26.0 %all-to-all-done.2 = bf16[32,8,2176]{2,1,0:T(8,128)(2,1)S(1)} async-done(((bf16[32,8,2176]{2,1,0:T(8,128)(2,1)}), bf16[32,8,2176]{2,1,0:T(8,128)(2,1)S(1)}, u32[]{:S(2)}, u32[]{:S(2)}) %all-to-all-start.2) | async-done | bytes 1114144 | tf_op jit(solution)/shard_map/all_to_all | solution.py:253
  105.3 2.7 %shard_map.112 = bf16[256,640]{1,0:T(8,128)(2,1)} custom-call(s32[1]{0:T(128)} %bitcast.core_ref, bf16[256,2176]{1,0:T(8,128)(2,1)S(1)} %bitcast.34, s32[4,256]{1,0:T(4,128)S(1)} %select_n.69.code_ref, bf16[2,512,128]{2,1,0:T(8,128)(2,1)S(1)} %copy-done.3, bf16[2,512,128]{2,1,0:T(8,128)(2,1)S(1)} %collective-permute-done.1.mate_ref.mate_uv), custom_call_target="tpu_custom_call" | custom-call | tf_op jit(solution)/shard_map/pallas_call | solution.py:40
  108.0 3.4 %all-to-all-start.3 = ((bf16[8,32,640]{2,1,0:T(8,128)(2,1)}), bf16[8,32,640]{2,1,0:T(8,128)(2,1)S(1)}, u32[]{:S(2)}, u32[]{:S(2)}) async-start(bf16[8,32,640]{2,1,0:T(8,128)(2,1)} %bitcast.15), calls=%async_computation.3 | async-start | bytes 655360 | tf_op jit(solution)/shard_map/all_to_all | solution.py:253
  111.5 2.7 %shard_map.113 = (f32[32,512]{1,0:T(8,128)S(1)}, f32[32,128]{1,0:T(8,128)S(1)}) custom-call(s32[2]{0:T(128)S(1)} %pad_add_fusion.place_ref, bf16[512,384]{1,0:T(8,128)(2,1)S(1)} %bitcast.36, bf16[2,128,512]{2,1,0:T(8,128)(2,1)S(1)} %copy-done.2, bf16[2,128,512]{2,1,0:T(8,128)(2,1)S(1)} %collective-permute-done.mate_ref.mate_uk, ...), custom_call_target="tpu_custom_call" | custom-call | tf_op jit(solution)/shard_map/pallas_call | solution.py:40
  114.3 5.3 %all-to-all-done.3 = bf16[8,32,640]{2,1,0:T(8,128)(2,1)S(1)} async-done(((bf16[8,32,640]{2,1,0:T(8,128)(2,1)}), bf16[8,32,640]{2,1,0:T(8,128)(2,1)S(1)}, u32[]{:S(2)}, u32[]{:S(2)}) %all-to-all-start.3) | async-done | bytes 327712 | tf_op jit(solution)/shard_map/all_to_all | solution.py:253
  119.6 2.0 %copy-done.1 = bf16[256,7168]{1,0:T(8,128)(2,1)S(1)} copy-done((bf16[256,7168]{1,0:T(8,128)(2,1)S(1)}, bf16[256,7168]{1,0:T(8,128)(2,1)}, u32[]{:S(2)}) %copy-start.1) | copy-done | bytes 3670040
  121.6 4.0 %shard_map.114 = bf16[32,7168]{1,0:T(8,128)(2,1)S(1)} custom-call(s32[1]{0:T(128)} %bitcast.core_ref, bf16[256,640]{1,0:T(8,128)(2,1)S(1)} %bitcast.38, f32[32,512]{1,0:T(8,128)S(1)} %get-tuple-element.12.hv_ref, f32[32,128]{1,0:T(8,128)S(1)} %get-tuple-element.13.log_ref, bf16[256,7168]{1,0:T(8,128)(2,1)S(1)} %copy-done.1, ...), custom_call_target="tpu_custom_call" | custom-call | tf_op jit(solution)/shard_map/pallas_call | solution.py:40
  125.7 21.5 %all_to_all.25 = bf16[32,8,896]{2,1,0:T(8,128)(2,1)S(1)} all-to-all(bf16[32,8,896]{2,1,0:T(8,128)(2,1)S(1)} %bitcast.40), channel_id=1, replica_groups=mesh['group'=4,'z'=8,'x'=4,'core'=2] {'z','x'}, dimensions={0} | all-to-all | bytes 917504 | tf_op jit(solution)/shard_map/all_to_all | solution.py:342
  147.3 0.6 copy.18
  (40 shorter events, 1.6 us)
Async XLA Ops:
  0.0 8.7 %copy-start = (s32[4,64,2]{1,2,0:T(2,128)S(1)}, s32[4,64,2]{1,2,0:T(2,128)}, u32[]{:S(2)}) copy-start(s32[4,64,2]{1,2,0:T(2,128)} %param.20) | copy-start | bytes 6148
  0.0 17.7 %copy-start.2 = (bf16[2,128,512]{2,1,0:T(8,128)(2,1)S(1)}, bf16[2,128,512]{2,1,0:T(8,128)(2,1)}, u32[]{:S(2)}) copy-start(bf16[2,128,512]{2,1,0:T(8,128)(2,1)} %own_uk.1) | copy-start | bytes 786436
  0.0 9.4 %collective-permute-start = (bf16[2,128,512]{2,1,0:T(8,128)(2,1)}, bf16[2,128,512]{2,1,0:T(8,128)(2,1)S(1)}, u32[]{:S(2)}, u32[]{:S(2)}) collective-permute-start(bf16[2,128,512]{2,1,0:T(8,128)(2,1)} %own_uk.1), channel_id=1, source_target_pairs={{0,1},{1,0},{2,3},{3,2},{4,5},{5,4},{6,7},{7,6},{8,9},{9,8},{10,11... | collective-permute-start | bytes 786440 | tf_op jit(solution)/shard_map/ppermute | solution.py:274
  0.0 1.2 copy-start.4
  1.2 1.0 copy-start.5
  2.2 0.9 copy-start.6
  4.2 13.5 %all-to-all-start = ((bf16[8,64,384]{2,1,0:T(8,128)(2,1)}), bf16[8,64,384]{2,1,0:T(8,128)(2,1)S(1)}, u32[]{:S(2)}, u32[]{:S(2)}) async-start(bf16[8,64,384]{2,1,0:T(8,128)(2,1)} %shard_map.109), calls=%async_computation | async-start | bytes 786432 | tf_op jit(solution)/shard_map/all_to_all | solution.py:304
  19.7 12.5 %copy-start.8 = (s32[64]{0:T(128)S(1)}, s32[64]{0:T(128)}, u32[]{:S(2)}) copy-start(s32[64]{0:T(128)} %param.19) | copy-start | bytes 772
  19.7 41.1 %all-to-all-start.1 = ((bf16[32,8,2304]{2,1,0:T(8,128)(2,1)}), bf16[32,8,2304]{2,1,0:T(8,128)(2,1)S(1)}, u32[]{:S(2)}, u32[]{:S(2)}) async-start(bf16[32,8,2304]{2,1,0:T(8,128)(2,1)} %bitcast.6), calls=%async_computation.1 | async-start | bytes 2359296 | tf_op jit(solution)/shard_map/all_to_all | solution.py:253
  31.0 83.3 %collective-permute-start.2 = (bf16[256,7168]{1,0:T(8,128)(2,1)}, bf16[256,7168]{1,0:T(8,128)(2,1)}, u32[]{:S(2)}, u32[]{:S(2)}) collective-permute-start(bf16[256,7168]{1,0:T(8,128)(2,1)} %own_ref.5), channel_id=1, source_target_pairs={{0,1},{1,0},{2,3},{3,2},{4,5},{5,4},{6,7},{7,6},{8,9},{9,8},{10,11... | collective-permute-start | bytes 11010056 | tf_op jit(solution)/shard_map/ppermute | solution.py:315
  71.0 6.7 %copy-start.3 = (bf16[2,512,128]{2,1,0:T(8,128)(2,1)S(1)}, bf16[2,512,128]{2,1,0:T(8,128)(2,1)}, u32[]{:S(2)}) copy-start(bf16[2,512,128]{2,1,0:T(8,128)(2,1)} %own_uv.1) | copy-start | bytes 786436
  71.0 34.3 %all-to-all-start.2 = ((bf16[32,8,2176]{2,1,0:T(8,128)(2,1)}), bf16[32,8,2176]{2,1,0:T(8,128)(2,1)S(1)}, u32[]{:S(2)}, u32[]{:S(2)}) async-start(bf16[32,8,2176]{2,1,0:T(8,128)(2,1)} %bitcast.10), calls=%async_computation.2 | async-start | bytes 2228224 | tf_op jit(solution)/shard_map/all_to_all | solution.py:253
  77.7 1.6 %collective-permute-start.1 = (bf16[2,512,128]{2,1,0:T(8,128)(2,1)S(1)}, bf16[2,512,128]{2,1,0:T(8,128)(2,1)S(1)}, u32[]{:S(2)}, u32[]{:S(2)}) collective-permute-start(bf16[2,512,128]{2,1,0:T(8,128)(2,1)S(1)} %copy-done.3), channel_id=1, source_target_pairs={{0,1},{1,0},{2,3},{3,2},{4,5},{5,4},{6,7},{7,6},{8,9},{9,8},{10,11... | collective-permute-start | bytes 786440 | tf_op jit(solution)/shard_map/ppermute | solution.py:314
  105.3 6.2 %copy-start.7 = (bf16[64,576]{1,0:T(8,128)(2,1)S(1)}, bf16[64,576]{1,0:T(8,128)(2,1)}, u32[]{:S(2)}) copy-start(bf16[64,576]{1,0:T(8,128)(2,1)} %kv_ref.1) | copy-start | bytes 221188
  108.0 11.6 %all-to-all-start.3 = ((bf16[8,32,640]{2,1,0:T(8,128)(2,1)}), bf16[8,32,640]{2,1,0:T(8,128)(2,1)S(1)}, u32[]{:S(2)}, u32[]{:S(2)}) async-start(bf16[8,32,640]{2,1,0:T(8,128)(2,1)} %bitcast.15), calls=%async_computation.3 | async-start | bytes 655360 | tf_op jit(solution)/shard_map/all_to_all | solution.py:253
  119.6 2.0 %copy-start.1 = (bf16[256,7168]{1,0:T(8,128)(2,1)S(1)}, bf16[256,7168]{1,0:T(8,128)(2,1)}, u32[]{:S(2)}) copy-start(bf16[256,7168]{1,0:T(8,128)(2,1)} %own_ref.5) | copy-start | bytes 11010052

commit v3 on v2

--- a/solution.py
+++ b/solution.py
@@ -18,6 +18,7 @@
 WIDE = 2 * LATENT + 2 * ROPE
 PART = SLOTS * 2 * LATENT + 128
 NARROW = 2 * NOPE + 2 * ROPE
+PIECES = 4
 EMPTY = -1e30
 SCALE = (NOPE + ROPE) ** -0.5
 F32 = jnp.float32
@@ -26,6 +27,11 @@
 
 VMEM = pl.BlockSpec(memory_space=pltpu.VMEM)
 SMEM = pl.BlockSpec(memory_space=pltpu.SMEM)
+HBM = pl.BlockSpec(memory_space=pltpu.HBM)
+
+
+def in_hbm(array):
+    return pltpu.with_memory_space_constraint(array, pltpu.HBM)
 
 
 def dot(a, b):
@@ -60,9 +66,22 @@
     return tile
 
 
-def project_kernel(q_ref, wn_ref, wr_ref, out_ref):
+def project_kernel(q_hbm, wn_hbm, wr_hbm, out_ref, q_ref, wn_ref, wr_ref, sems):
+    copies = []
+    depth = wn_ref.shape[0] // 2
+    for i, (source, target) in enumerate(((q_hbm, q_ref), (wr_hbm, wr_ref))):
+        copies.append(pltpu.make_async_copy(source, target, sems.at[i]))
+    for i in range(2):
+        at = pl.ds(i * depth, depth)
+        copies.append(pltpu.make_async_copy(wn_hbm.at[at], wn_ref.at[at], sems.at[2 + i]))
+    for copy in copies:
+        copy.start()
+    copies[0].wait()
+    copies[1].wait()
+    ropes = (dot(q_ref[...], wr_ref[...]) * SCALE).astype(BF16)
+    copies[2].wait()
+    copies[3].wait()
     narrow = dot(q_ref[...], wn_ref[...]).astype(BF16)
-    ropes = (dot(q_ref[...], wr_ref[...]) * SCALE).astype(BF16)
     for copy in range(out_ref.shape[0]):
         out_ref[copy, :, : 2 * NOPE] = narrow
         out_ref[copy, :, 2 * NOPE :] = ropes
@@ -70,24 +89,26 @@
 
 def spread_kernel(core_ref, q_ref, code_ref, own_ref, mate_ref, out_ref, rows):
     core = core_ref[0]
-    rows[...] = jnp.zeros_like(rows)
-    for block in range(q_ref.shape[0] // TOK_GRP):
-        at = pl.ds(block * TOK_GRP, TOK_GRP)
-        side = pl.multiple_of(jnp.where(core == block % 2, 0, NOPE), NOPE)
-        for par in range(2):
-            rows[at, pl.ds(par * 2 * NOPE + side, NOPE)] = q_ref[at, par * NOPE : (par + 1) * NOPE]
-        rows[at, 4 * NOPE :] = q_ref[at, 2 * NOPE :]
-    count = code_ref.shape[0] // SLOTS
-    for slot in range(SLOTS):
-        code = code_ref[slot * count : (slot + 1) * count, :]
-        column = lax.broadcasted_iota(jnp.int32, (count, rows.shape[0]), 1)
-        picked = dot(jnp.where(column == code, 1.0, 0.0).astype(BF16), rows[...]).astype(BF16)
-        for par in range(2):
-            weight = jnp.concatenate([own_ref[par], mate_ref[par]], axis=0)
-            absorbed = dot(picked[:, par * 2 * NOPE : (par + 1) * 2 * NOPE], weight) * SCALE
-            first = slot * WIDE + par * LATENT
-            out_ref[:, first : first + LATENT] = absorbed.astype(BF16)
-        out_ref[:, slot * WIDE + 2 * LATENT : (slot + 1) * WIDE] = picked[:, 4 * NOPE :]
+
+    @pl.when(pl.program_id(0) == 0)
+    def _():
+        rows[...] = jnp.zeros_like(rows)
+        for block in range(q_ref.shape[0] // TOK_GRP):
+            at = pl.ds(block * TOK_GRP, TOK_GRP)
+            side = pl.multiple_of(jnp.where(core == block % 2, 0, NOPE), NOPE)
+            for par in range(2):
+                part = q_ref[at, par * NOPE : (par + 1) * NOPE]
+                rows[at, pl.ds(par * 2 * NOPE + side, NOPE)] = part
+            rows[at, 4 * NOPE :] = q_ref[at, 2 * NOPE :]
+
+    column = lax.broadcasted_iota(jnp.int32, (code_ref.shape[0], rows.shape[0]), 1)
+    pick = jnp.where(column == code_ref[...], 1.0, 0.0).astype(BF16)
+    picked = dot(pick, rows[...]).astype(BF16)
+    for par in range(2):
+        weight = jnp.concatenate([own_ref[par], mate_ref[par]], axis=0)
+        absorbed = dot(picked[:, par * 2 * NOPE : (par + 1) * 2 * NOPE], weight) * SCALE
+        out_ref[:, par * LATENT : (par + 1) * LATENT] = absorbed.astype(BF16)
+    out_ref[:, 2 * LATENT :] = picked[:, 4 * NOPE :]
 
 
 def draft_kernel(place_ref, q_ref, own_uk, mate_uk, own_uv, mate_uv, kv_ref, hv_ref, log_ref):
@@ -120,68 +141,81 @@
     log_ref[...] = logs
 
 
-def attend_kernel(count_ref, x_ref, kv_ref, out_ref, queries, scores):
-    slot = pl.program_id(0)
-    count = count_ref[slot]
+def attend_kernel(count_ref, x_ref, kv_hbm, out_hbm, queries, scores, out_ref, kv_ref, sems, in_sems):
     half = x_ref.shape[0]
-    for par in range(2):
-        at = slice(par * half, (par + 1) * half)
-        queries[at, :LATENT] = x_ref[:, par * LATENT : (par + 1) * LATENT]
-        first = 2 * LATENT + par * ROPE
-        queries[at, LATENT:] = x_ref[:, first : first + ROPE]
-    slab = kv_ref.shape[1]
-    chunk = 512
-    peak = jnp.full((2 * half, 1), EMPTY, F32)
-    for first in range(0, slab, chunk):
-        score = dot(queries[...], kv_ref[:, first : first + chunk])
-        position = lax.broadcasted_iota(jnp.int32, score.shape, 1) + first
-        score = jnp.where(position < count, score, EMPTY)
-        scores[:, first : first + chunk] = score
-        peak = jnp.maximum(peak, jnp.max(score, axis=1, keepdims=True))
-    reference = jnp.maximum(peak, EMPTY / 10)
-    total = jnp.zeros((2 * half, 1), F32)
-    mixture = jnp.zeros((2 * half, LATENT), F32)
-    for first in range(0, slab, chunk):
-        weights = jnp.exp(scores[:, first : first + chunk] - reference)
-        total += jnp.sum(weights, axis=1, keepdims=True)
-        mixture += dot_t(weights.astype(BF16), kv_ref[:LATENT, first : first + chunk])
-    total = jnp.maximum(total, 1.0)
-    mixture = (mixture / total).astype(BF16)
-    log = peak + jnp.log(total)
-    start = slot * 2 * LATENT
+    slab = kv_ref.shape[2]
+    chunk = 256
+    piece = slab // PIECES
+    arriving = []
+    for i in range(SLOTS * PIECES):
+        at = (i // PIECES, slice(None), pl.ds(i % PIECES * piece, piece))
+        arriving.append(pltpu.make_async_copy(kv_hbm.at[at], kv_ref.at[at], in_sems.at[i]))
+        arriving[-1].start()
+    base = SLOTS * 2 * LATENT
     lane = lax.broadcasted_iota(jnp.int32, (half, 128), 1)
-    tile = jnp.where(slot == 0, jnp.zeros((half, 128), F32), out_ref[:, SLOTS * 2 * LATENT :].astype(F32))
-    for par in range(2):
-        at = slice(par * half, (par + 1) * half)
-        out_ref[:, pl.ds(pl.multiple_of(start + par * LATENT, LATENT), LATENT)] = mixture[at]
-        for i, term in enumerate(three_terms(log[at])):
-            tile = jnp.where(lane == slot * 6 + par * 3 + i, term, tile)
-    out_ref[:, SLOTS * 2 * LATENT :] = tile.astype(BF16)
+    tile = jnp.zeros((half, 128), F32)
+    copies = []
+    for slot in range(SLOTS):
+        count = count_ref[slot]
+        for par in range(2):
+            at = slice(par * half, (par + 1) * half)
+            first = slot * WIDE + par * LATENT
+            queries[at, :LATENT] = x_ref[:, first : first + LATENT]
+            first = slot * WIDE + 2 * LATENT + par * ROPE
+            queries[at, LATENT:] = x_ref[:, first : first + ROPE]
+        peak = jnp.full((2 * half, 1), EMPTY, F32)
+        for first in range(0, slab, chunk):
+            if first % piece == 0:
+                arriving[slot * PIECES + first // piece].wait()
+            score = dot(queries[...], kv_ref[slot, :, first : first + chunk])
+            position = lax.broadcasted_iota(jnp.int32, score.shape, 1) + first
+            score = jnp.where(position < count, score, EMPTY)
+            scores[:, first : first + chunk] = score
+            peak = jnp.maximum(peak, jnp.max(score, axis=1, keepdims=True))
+        reference = jnp.maximum(peak, EMPTY / 10)
+        total = jnp.zeros((2 * half, 1), F32)
+        mixture = jnp.zeros((2 * half, LATENT), F32)
+        for first in range(0, slab, chunk):
+            weights = jnp.exp(scores[:, first : first + chunk] - reference)
+            total += jnp.sum(weights, axis=1, keepdims=True)
+            mixture += dot_t(weights.astype(BF16), kv_ref[slot, :LATENT, first : first + chunk])
+        total = jnp.maximum(total, 1.0)
+        mixture = (mixture * (1.0 / total)).astype(BF16)
+        log = peak + jnp.log(total)
+        start = slot * 2 * LATENT
+        for par in range(2):
+            at = slice(par * half, (par + 1) * half)
+            out_ref[:, start + par * LATENT : start + (par + 1) * LATENT] = mixture[at]
+            for i, term in enumerate(three_terms(log[at])):
+                tile = jnp.where(lane == slot * 6 + par * 3 + i, term, tile)
+        end = start + 2 * LATENT
+        if slot == SLOTS - 1:
+            out_ref[:, base:] = tile.astype(BF16)
+            end = PART
+        at = pl.ds(start, end - start)
+        copies.append(pltpu.make_async_copy(out_ref.at[:, at], out_hbm.at[:, at], sems.at[slot]))
+        copies[-1].start()
+    for copy in copies:
+        copy.wait()
 
 
 def attend(count, x, kv):
     rows = x.shape[0]
-    slab = kv.shape[2]
     return pl.pallas_call(
         attend_kernel,
         out_shape=jax.ShapeDtypeStruct((rows, PART), BF16),
-        grid_spec=pltpu.PrefetchScalarGridSpec(
-            num_scalar_prefetch=1,
-            grid=(SLOTS,),
-            in_specs=[
-                pl.BlockSpec((rows, WIDE), lambda k, _: (0, k)),
-                pl.BlockSpec((None, KEY, slab), lambda k, _: (k, 0, 0)),
-            ],
-            out_specs=pl.BlockSpec((rows, PART), lambda k, _: (0, 0)),
-            scratch_shapes=[
-                pltpu.VMEM((2 * rows, KEY), BF16),
-                pltpu.VMEM((2 * rows, slab), F32),
-            ],
-        ),
-        compiler_params=pltpu.CompilerParams(
-            dimension_semantics=("arbitrary",), vmem_limit_bytes=48 << 20
-        ),
-    )(count, x, kv)
+        in_specs=[SMEM, VMEM, HBM],
+        out_specs=HBM,
+        scratch_shapes=[
+            pltpu.VMEM((2 * rows, KEY), BF16),
+            pltpu.VMEM((2 * rows, kv.shape[2]), F32),
+            pltpu.VMEM((rows, PART), BF16),
+            pltpu.VMEM(kv.shape, BF16),
+            pltpu.SemaphoreType.DMA((SLOTS,)),
+            pltpu.SemaphoreType.DMA((SLOTS * PIECES,)),
+        ],
+        compiler_params=pltpu.CompilerParams(vmem_limit_bytes=32 << 20),
+    )(count, x, in_hbm(kv))
 
 
 def merge_kernel(core_ref, y_ref, code_ref, own_ref, mate_ref, out_ref):
@@ -216,8 +250,16 @@
     out_ref[:, 4 * VDIM :] = tile.astype(BF16)
 
 
-def finish_kernel(core_ref, z_ref, hv_ref, log_ref, own_ref, mate_ref, out_ref):
+def finish_kernel(core_ref, z_ref, hv_ref, log_ref, own_hbm, mate_hbm, out_ref, o_ref, sems):
     half = hv_ref.shape[0]
+    piece = out_ref.shape[1] // PIECES
+    arriving = []
+    for i in range(PIECES):
+        at = (slice(None), pl.ds(i * piece, piece))
+        for side, source in enumerate((own_hbm, mate_hbm)):
+            target = o_ref.at[side].at[at]
+            arriving.append(pltpu.make_async_copy(source.at[at], target, sems.at[2 * i + side]))
+            arriving[-1].start()
     values = []
     for head in range(4):
         logs = [log_ref[:, head : head + 1]]
@@ -245,7 +287,18 @@
     pairs = [jnp.concatenate(values[hp * 2 : hp * 2 + 2], axis=1) for hp in range(2)]
     own = jnp.where(core_ref[0] == 0, pairs[0], pairs[1]).astype(BF16)
     mate = jnp.where(core_ref[0] == 0, pairs[1], pairs[0]).astype(BF16)
-    out_ref[...] = (dot(own, own_ref[...]) + dot(mate, mate_ref[...])).astype(BF16)
+    for i in range(PIECES):
+        arriving[2 * i].wait()
+        arriving[2 * i + 1].wait()
+        at = slice(i * piece, (i + 1) * piece)
+        out_ref[:, at] = (dot(own, o_ref[0, :, at]) + dot(mate, o_ref[1, :, at])).astype(BF16)
+
+
+def total_kernel(tiles_ref, out_ref):
+    total = jnp.sum(tiles_ref[...].astype(F32), axis=0)
+    width = total.shape[1]
+    for i in range(total.shape[0]):
+        out_ref[:, i * width : (i + 1) * width] = total[i : i + 1]
 
 
 def exchange(array, axes, peers):
@@ -299,17 +352,28 @@
     narrow = pl.pallas_call(
         project_kernel,
         out_shape=jax.ShapeDtypeStruct((copies, TOK_GRP, NARROW), BF16),
-        compiler_params=pltpu.CompilerParams(vmem_limit_bytes=32 << 20),
-    )(q_compressed, w_q_nope, w_q_rope)
+        in_specs=[HBM] * 3,
+        out_specs=VMEM,
+        scratch_shapes=[
+            *(pltpu.VMEM(a.shape, BF16) for a in (q_compressed, w_q_nope, w_q_rope)),
+            pltpu.SemaphoreType.DMA((4,)),
+        ],
+        compiler_params=pltpu.CompilerParams(vmem_limit_bytes=16 << 20),
+    )(*(in_hbm(a) for a in (q_compressed, w_q_nope, w_q_rope)))
     every = lax.all_to_all(narrow, ("group", "core"), 0, 0, tiled=True).reshape(-1, NARROW)
     rows = chips * cores * DRAFT
-    wide = call(
+    wide = pl.pallas_call(
         spread_kernel,
-        jax.ShapeDtypeStruct((rows, SLOTS * WIDE), BF16),
-        (core_id, every, code, w_uk, mate_uk),
-        [SMEM] + [VMEM] * 4,
-        [pltpu.VMEM((copies * TOK_GRP, 5 * NOPE), BF16)],
-    )
+        out_shape=jax.ShapeDtypeStruct((rows, SLOTS * WIDE), BF16),
+        grid=(SLOTS,),
+        in_specs=[SMEM, VMEM, pl.BlockSpec((rows, 1), lambda k: (k, 0)), VMEM, VMEM],
+        out_specs=pl.BlockSpec((rows, WIDE), lambda k: (0, k)),
+        scratch_shapes=[pltpu.VMEM((copies * TOK_GRP, 5 * NOPE), BF16)],
+        compiler_params=pltpu.CompilerParams(
+            dimension_semantics=("arbitrary",), vmem_limit_bytes=16 << 20
+        ),
+    )(core_id, every, code, w_uk, mate_uk)
+    slabs_kv = jnp.swapaxes(kv_cache.reshape(kv_cache.shape[2:]), 1, 2)
     late_o, late_uv, wide = lax.optimization_barrier((w_o, w_uv, wide))
     mate_uv = lax.ppermute(late_uv, "core", swap)
     mate_o = lax.ppermute(late_o, "core", swap)
@@ -324,7 +388,7 @@
         (place, every, w_uk, mate_uk, w_uv, mate_uv, draft_kv),
         [SMEM] + [VMEM] * 6,
     )
-    partials = attend(count, arrived, jnp.swapaxes(kv_cache.reshape(kv_cache.shape[2:]), 1, 2))
+    partials = attend(count, arrived, slabs_kv)
     back = exchange(partials, ("z", "x"), chips)
     merged = call(
         merge_kernel,
@@ -336,11 +400,14 @@
     sums = call(
         finish_kernel,
         jax.ShapeDtypeStruct((chips, w_o.shape[1]), BF16),
-        (core_id, home, draft_hv, draft_log, w_o, mate_o),
-        [SMEM] + [VMEM] * 5,
+        (core_id, home, draft_hv, draft_log, in_hbm(w_o), in_hbm(mate_o)),
+        [SMEM, VMEM, VMEM, VMEM, HBM, HBM],
+        [pltpu.VMEM((2, *w_o.shape), BF16), pltpu.SemaphoreType.DMA((2 * PIECES,))],
     )
     tiles = lax.all_to_all(sums.reshape(chips, 8, -1), ("z", "x"), 0, 0, tiled=True)
-    return jnp.sum(tiles.astype(F32), axis=0).reshape(1, -1)
+    return call(
+        total_kernel, jax.ShapeDtypeStruct((1, w_o.shape[1]), F32), (tiles,), [VMEM]
+    )
 
 
 def solution(mesh):

time: 149 us -> 145 us (0.973)
  local copies, waits for them, and re-layouts: 7.31 us -> 1.53 us
  Pallas kernels: 22.8 us -> 25.4 us
    unnamed x21 -> x12, local copies, waits for them, and re-layouts: 5.94 us -> 0.16 us
    pallas_call x0 -> x1, Pallas kernels: none -> 2.09 us  [shards(): pl.pallas_call(spread_kernel, out_shape=jax.ShapeDtypeStruct((rows, SLOTS...]
  transfers between devices with their start and end apart: 7 -> 7, of which waited for: 5 -> 5; matrix products, arithmetic and copies ran while one was open for 2% -> 2% of each run, Pallas kernels for 11% -> 13%
where the time goes in v3:
time: 145 us
  waiting for transfers between devices  69 us (48%)
  starting transfers between devices  26.3 us (18%)
  Pallas kernels  25.4 us (18%)
  blocking collectives  21.5 us (15%)
  local copies, waits for them, and re-layouts  1.53 us (1%)
    all_to_all x3, waiting for transfers between devices, exchange(): return lax.all_to_all(blocks, axes, 0, 0, tiled=True).reshape(array.shape)  59.6 us
    all_to_all x3, starting transfers between devices, exchange(): return lax.all_to_all(blocks, axes, 0, 0, tiled=True).reshape(array.shape)  21.5 us
    all_to_all x1, blocking collectives, shards(): lax.all_to_all(sums.reshape(chips, 8, -1), ('z', 'x'), 0, 0, tiled=True)  21.5 us
    pallas_call x1, Pallas kernels, attend(): pl.pallas_call(attend_kernel, out_shape=jax.ShapeDtypeStruct((rows, PART)...  10.5 us
    pallas_call x4, Pallas kernels, call(): pl.pallas_call(kernel, out_shape=outs, in_specs=specs, out_specs=jax.tree...  10.4 us
    all_to_all x1, waiting for transfers between devices, shards(): lax.all_to_all(narrow, ('group', 'core'), 0, 0, tiled=True)  8.22 us
    all_to_all x1, starting transfers between devices, shards(): lax.all_to_all(narrow, ('group', 'core'), 0, 0, tiled=True)  4.55 us
  transfers between devices with their start and end apart: 7, of which 5 were waited for; matrix products, arithmetic and copies ran while one was open for 2% of the time, Pallas kernels for 13%

profile of v3, /device:TPU:32, one launch (start us, length us, event | category | flops | bytes accessed | tf_op | source)
XLA Modules:
  0.0 144.9 jit_solution(15904507111541824100)
XLA Ops:
  0.0 2.4 %shard_map.109 = bf16[8,64,384]{2,1,0:T(8,128)(2,1)} custom-call(bf16[64,1536]{1,0:T(8,128)(2,1)} %q_hbm.1, bf16[1536,256]{1,0:T(8,128)(2,1)} %wn_hbm.1, bf16[1536,128]{1,0:T(8,128)(2,1)} %wr_hbm.1), custom_call_target="tpu_custom_call" | custom-call | tf_op jit(solution)/shard_map/pallas_call | solution.py:352
  2.4 4.6 %all-to-all-start = ((bf16[8,64,384]{2,1,0:T(8,128)(2,1)}), bf16[8,64,384]{2,1,0:T(8,128)(2,1)S(1)}, u32[]{:S(2)}, u32[]{:S(2)}) async-start(bf16[8,64,384]{2,1,0:T(8,128)(2,1)} %shard_map.109), calls=%async_computation | async-start | bytes 786432 | tf_op jit(solution)/shard_map/all_to_all | solution.py:363
  7.6 0.1 select_n.70.code_ref
  7.7 8.2 %all-to-all-done = bf16[8,64,384]{2,1,0:T(8,128)(2,1)S(1)} async-done(((bf16[8,64,384]{2,1,0:T(8,128)(2,1)}), bf16[8,64,384]{2,1,0:T(8,128)(2,1)S(1)}, u32[]{:S(2)}, u32[]{:S(2)}) %all-to-all-start) | async-done | bytes 393248 | tf_op jit(solution)/shard_map/all_to_all | solution.py:363
  15.9 2.1 %shard_map.110 = bf16[256,2304]{1,0:T(8,128)(2,1)} custom-call(s32[1]{0:T(128)} %bitcast.core_ref, bf16[512,384]{1,0:T(8,128)(2,1)S(1)} %bitcast.32, s32[512,1]{1,0:T(8,128)S(1)} %select_n.70.code_ref, bf16[2,128,512]{2,1,0:T(8,128)(2,1)S(1)} %copy-done.1, bf16[2,128,512]{2,1,0:T(8,128)(2,1)S(1)} %collective-permute-done.mate_ref.mate_uk), custom_call_target="tpu_custom_call" | custom-call | tf_op jit(solution)/shard_map/pallas_call | solution.py:365
  18.0 11.3 %all-to-all-start.1 = ((bf16[32,8,2304]{2,1,0:T(8,128)(2,1)}), bf16[32,8,2304]{2,1,0:T(8,128)(2,1)S(1)}, u32[]{:S(2)}, u32[]{:S(2)}) async-start(bf16[32,8,2304]{2,1,0:T(8,128)(2,1)} %bitcast.6), calls=%async_computation.1 | async-start | bytes 2359296 | tf_op jit(solution)/shard_map/all_to_all | solution.py:306
  29.5 0.7 constant_dynamic-slice_fusion.2
  30.2 0.1 reshape.165
  30.3 0.2 fusion
  30.5 0.2 fusion.2
  30.7 28.4 %all-to-all-done.1 = bf16[32,8,2304]{2,1,0:T(8,128)(2,1)S(1)} async-done(((bf16[32,8,2304]{2,1,0:T(8,128)(2,1)}), bf16[32,8,2304]{2,1,0:T(8,128)(2,1)S(1)}, u32[]{:S(2)}, u32[]{:S(2)}) %all-to-all-start.1) | async-done | bytes 1179680 | tf_op jit(solution)/shard_map/all_to_all | solution.py:306
  59.2 10.5 %shard_map.111 = bf16[256,2176]{1,0:T(8,128)(2,1)} custom-call(s32[2]{0:T(128)S(1)} %compare_select_fusion.1.count_ref, bf16[256,2304]{1,0:T(8,128)(2,1)S(1)} %bitcast.30, bf16[2,576,2048]{2,1,0:T(8,128)(2,1)} %bitcast.36), custom_call_target="tpu_custom_call" | custom-call | tf_op jit(solution)/shard_map/pallas_call | solution.py:204
  69.7 6.6 %all-to-all-start.2 = ((bf16[32,8,2176]{2,1,0:T(8,128)(2,1)}), bf16[32,8,2176]{2,1,0:T(8,128)(2,1)S(1)}, u32[]{:S(2)}, u32[]{:S(2)}) async-start(bf16[32,8,2176]{2,1,0:T(8,128)(2,1)} %bitcast.10), calls=%async_computation.2 | async-start | bytes 2228224 | tf_op jit(solution)/shard_map/all_to_all | solution.py:306
  76.5 0.1 broadcast_select_fusion
  76.6 0.2 select_n.69.code_ref
  76.8 1.2 collective-permute-done.1.mate_ref.mate_uv
  78.0 26.0 %all-to-all-done.2 = bf16[32,8,2176]{2,1,0:T(8,128)(2,1)S(1)} async-done(((bf16[32,8,2176]{2,1,0:T(8,128)(2,1)}), bf16[32,8,2176]{2,1,0:T(8,128)(2,1)S(1)}, u32[]{:S(2)}, u32[]{:S(2)}) %all-to-all-start.2) | async-done | bytes 1114144 | tf_op jit(solution)/shard_map/all_to_all | solution.py:306
  104.0 2.7 %shard_map.112 = bf16[256,640]{1,0:T(8,128)(2,1)} custom-call(s32[1]{0:T(128)} %bitcast.core_ref, bf16[256,2176]{1,0:T(8,128)(2,1)S(1)} %bitcast.31, s32[4,256]{1,0:T(4,128)S(1)} %select_n.69.code_ref, bf16[2,512,128]{2,1,0:T(8,128)(2,1)S(1)} %copy-done.2, bf16[2,512,128]{2,1,0:T(8,128)(2,1)S(1)} %collective-permute-done.1.mate_ref.mate_uv), custom_call_target="tpu_custom_call" | custom-call | tf_op jit(solution)/shard_map/pallas_call | solution.py:46
  106.7 3.6 %all-to-all-start.3 = ((bf16[8,32,640]{2,1,0:T(8,128)(2,1)}), bf16[8,32,640]{2,1,0:T(8,128)(2,1)S(1)}, u32[]{:S(2)}, u32[]{:S(2)}) async-start(bf16[8,32,640]{2,1,0:T(8,128)(2,1)} %bitcast.15), calls=%async_computation.3 | async-start | bytes 655360 | tf_op jit(solution)/shard_map/all_to_all | solution.py:306
  110.4 2.7 %shard_map.113 = (f32[32,512]{1,0:T(8,128)S(1)}, f32[32,128]{1,0:T(8,128)S(1)}) custom-call(s32[2]{0:T(128)S(1)} %pad_add_fusion.place_ref, bf16[512,384]{1,0:T(8,128)(2,1)S(1)} %bitcast.33, bf16[2,128,512]{2,1,0:T(8,128)(2,1)S(1)} %copy-done.1, bf16[2,128,512]{2,1,0:T(8,128)(2,1)S(1)} %collective-permute-done.mate_ref.mate_uk, ...), custom_call_target="tpu_custom_call" | custom-call | tf_op jit(solution)/shard_map/pallas_call | solution.py:46
  113.1 5.2 %all-to-all-done.3 = bf16[8,32,640]{2,1,0:T(8,128)(2,1)S(1)} async-done(((bf16[8,32,640]{2,1,0:T(8,128)(2,1)}), bf16[8,32,640]{2,1,0:T(8,128)(2,1)S(1)}, u32[]{:S(2)}, u32[]{:S(2)}) %all-to-all-start.3) | async-done | bytes 327712 | tf_op jit(solution)/shard_map/all_to_all | solution.py:306
  118.3 4.3 %shard_map.114 = bf16[32,7168]{1,0:T(8,128)(2,1)S(1)} custom-call(s32[1]{0:T(128)} %bitcast.core_ref, bf16[256,640]{1,0:T(8,128)(2,1)S(1)} %bitcast.35, f32[32,512]{1,0:T(8,128)S(1)} %get-tuple-element.12.hv_ref, f32[32,128]{1,0:T(8,128)S(1)} %get-tuple-element.13.log_ref, bf16[256,7168]{1,0:T(8,128)(2,1)} %own_hbm.1, ...), custom_call_target="tpu_custom_call" | custom-call | tf_op jit(solution)/shard_map/pallas_call | solution.py:46
  122.7 21.5 %all_to_all.25.tiles_ref = bf16[32,8,896]{2,1,0:T(8,128)(2,1)S(1)} all-to-all(bf16[32,8,896]{2,1,0:T(8,128)(2,1)S(1)} %bitcast.37), channel_id=1, replica_groups=mesh['group'=4,'z'=8,'x'=4,'core'=2] {'z','x'}, dimensions={0} | all-to-all | bytes 917504 | tf_op jit(solution)/shard_map/all_to_all | solution.py:407
  144.2 0.7 shard_map.115
  (31 shorter events, 1.0 us)
Async XLA Ops:
  0.0 7.0 %copy-start = (s32[4,64,2]{1,2,0:T(2,128)S(1)}, s32[4,64,2]{1,2,0:T(2,128)}, u32[]{:S(2)}) copy-start(s32[4,64,2]{1,2,0:T(2,128)} %param.20) | copy-start | bytes 6148
  0.0 15.9 %copy-start.1 = (bf16[2,128,512]{2,1,0:T(8,128)(2,1)S(1)}, bf16[2,128,512]{2,1,0:T(8,128)(2,1)}, u32[]{:S(2)}) copy-start(bf16[2,128,512]{2,1,0:T(8,128)(2,1)} %own_uk.1) | copy-start | bytes 786436
  0.0 7.7 %collective-permute-start = (bf16[2,128,512]{2,1,0:T(8,128)(2,1)}, bf16[2,128,512]{2,1,0:T(8,128)(2,1)S(1)}, u32[]{:S(2)}, u32[]{:S(2)}) collective-permute-start(bf16[2,128,512]{2,1,0:T(8,128)(2,1)} %own_uk.1), channel_id=1, source_target_pairs={{0,1},{1,0},{2,3},{3,2},{4,5},{5,4},{6,7},{7,6},{8,9},{9,8},{10,11... | collective-permute-start | bytes 786440 | tf_op jit(solution)/shard_map/ppermute | solution.py:327
  2.4 13.5 %all-to-all-start = ((bf16[8,64,384]{2,1,0:T(8,128)(2,1)}), bf16[8,64,384]{2,1,0:T(8,128)(2,1)S(1)}, u32[]{:S(2)}, u32[]{:S(2)}) async-start(bf16[8,64,384]{2,1,0:T(8,128)(2,1)} %shard_map.109), calls=%async_computation | async-start | bytes 786432 | tf_op jit(solution)/shard_map/all_to_all | solution.py:363
  18.0 12.5 %copy-start.4 = (s32[64]{0:T(128)S(1)}, s32[64]{0:T(128)}, u32[]{:S(2)}) copy-start(s32[64]{0:T(128)} %param.19) | copy-start | bytes 772
  18.0 41.1 %all-to-all-start.1 = ((bf16[32,8,2304]{2,1,0:T(8,128)(2,1)}), bf16[32,8,2304]{2,1,0:T(8,128)(2,1)S(1)}, u32[]{:S(2)}, u32[]{:S(2)}) async-start(bf16[32,8,2304]{2,1,0:T(8,128)(2,1)} %bitcast.6), calls=%async_computation.1 | async-start | bytes 2359296 | tf_op jit(solution)/shard_map/all_to_all | solution.py:306
  29.4 83.8 %collective-permute-start.2 = (bf16[256,7168]{1,0:T(8,128)(2,1)}, bf16[256,7168]{1,0:T(8,128)(2,1)}, u32[]{:S(2)}, u32[]{:S(2)}) collective-permute-start(bf16[256,7168]{1,0:T(8,128)(2,1)} %own_hbm.1), channel_id=1, source_target_pairs={{0,1},{1,0},{2,3},{3,2},{4,5},{5,4},{6,7},{7,6},{8,9},{9,8},{10,11... | collective-permute-start | bytes 11010056 | tf_op jit(solution)/shard_map/ppermute | solution.py:379
  69.7 6.7 %copy-start.2 = (bf16[2,512,128]{2,1,0:T(8,128)(2,1)S(1)}, bf16[2,512,128]{2,1,0:T(8,128)(2,1)}, u32[]{:S(2)}) copy-start(bf16[2,512,128]{2,1,0:T(8,128)(2,1)} %own_uv.1) | copy-start | bytes 786436
  69.7 34.3 %all-to-all-start.2 = ((bf16[32,8,2176]{2,1,0:T(8,128)(2,1)}), bf16[32,8,2176]{2,1,0:T(8,128)(2,1)S(1)}, u32[]{:S(2)}, u32[]{:S(2)}) async-start(bf16[32,8,2176]{2,1,0:T(8,128)(2,1)} %bitcast.10), calls=%async_computation.2 | async-start | bytes 2228224 | tf_op jit(solution)/shard_map/all_to_all | solution.py:306
  76.4 1.6 %collective-permute-start.1 = (bf16[2,512,128]{2,1,0:T(8,128)(2,1)S(1)}, bf16[2,512,128]{2,1,0:T(8,128)(2,1)S(1)}, u32[]{:S(2)}, u32[]{:S(2)}) collective-permute-start(bf16[2,512,128]{2,1,0:T(8,128)(2,1)S(1)} %copy-done.2), channel_id=1, source_target_pairs={{0,1},{1,0},{2,3},{3,2},{4,5},{5,4},{6,7},{7,6},{8,9},{9,8},{10,11... | collective-permute-start | bytes 786440 | tf_op jit(solution)/shard_map/ppermute | solution.py:378
  104.0 6.4 %copy-start.3 = (bf16[64,576]{1,0:T(8,128)(2,1)S(1)}, bf16[64,576]{1,0:T(8,128)(2,1)}, u32[]{:S(2)}) copy-start(bf16[64,576]{1,0:T(8,128)(2,1)} %kv_ref.1) | copy-start | bytes 221188
  106.7 11.6 %all-to-all-start.3 = ((bf16[8,32,640]{2,1,0:T(8,128)(2,1)}), bf16[8,32,640]{2,1,0:T(8,128)(2,1)S(1)}, u32[]{:S(2)}, u32[]{:S(2)}) async-start(bf16[8,32,640]{2,1,0:T(8,128)(2,1)} %bitcast.15), calls=%async_computation.3 | async-start | bytes 655360 | tf_op jit(solution)/shard_map/all_to_all | solution.py:306

commit v4 on v3

--- a/solution.py
+++ b/solution.py
@@ -78,28 +78,23 @@
         copy.start()
     copies[0].wait()
     copies[1].wait()
-    ropes = (dot(q_ref[...], wr_ref[...]) * SCALE).astype(BF16)
+    out_ref[:, 2 * NOPE :] = (dot(q_ref[...], wr_ref[...]) * SCALE).astype(BF16)
     copies[2].wait()
     copies[3].wait()
-    narrow = dot(q_ref[...], wn_ref[...]).astype(BF16)
-    for copy in range(out_ref.shape[0]):
-        out_ref[copy, :, : 2 * NOPE] = narrow
-        out_ref[copy, :, 2 * NOPE :] = ropes
-
-
-def spread_kernel(core_ref, q_ref, code_ref, own_ref, mate_ref, out_ref, rows):
-    core = core_ref[0]
-
+    out_ref[:, : 2 * NOPE] = dot(q_ref[...], wn_ref[...]).astype(BF16)
+
+
+def spread_kernel(own_q, mate_q, code_ref, own_ref, mate_ref, out_ref, rows):
     @pl.when(pl.program_id(0) == 0)
     def _():
         rows[...] = jnp.zeros_like(rows)
-        for block in range(q_ref.shape[0] // TOK_GRP):
-            at = pl.ds(block * TOK_GRP, TOK_GRP)
-            side = pl.multiple_of(jnp.where(core == block % 2, 0, NOPE), NOPE)
+        count = own_q.shape[0]
+        for rel, q_ref in enumerate((own_q, mate_q)):
+            at = slice(rel * count, (rel + 1) * count)
             for par in range(2):
-                part = q_ref[at, par * NOPE : (par + 1) * NOPE]
-                rows[at, pl.ds(par * 2 * NOPE + side, NOPE)] = part
-            rows[at, 4 * NOPE :] = q_ref[at, 2 * NOPE :]
+                first = par * 2 * NOPE + rel * NOPE
+                rows[at, first : first + NOPE] = q_ref[:, par * NOPE : (par + 1) * NOPE]
+            rows[at, 4 * NOPE :] = q_ref[:, 2 * NOPE :]
 
     column = lax.broadcasted_iota(jnp.int32, (code_ref.shape[0], rows.shape[0]), 1)
     pick = jnp.where(column == code_ref[...], 1.0, 0.0).astype(BF16)
@@ -111,8 +106,10 @@
     out_ref[:, 2 * LATENT :] = picked[:, 4 * NOPE :]
 
 
-def draft_kernel(place_ref, q_ref, own_uk, mate_uk, own_uv, mate_uv, kv_ref, hv_ref, log_ref):
-    group, core = place_ref[0], place_ref[1]
+def draft_kernel(
+    core_ref, own_q, mate_q, own_uk, mate_uk, own_uv, mate_uv, kv_ref, hv_ref, log_ref
+):
+    core = core_ref[0]
     half = hv_ref.shape[0]
     row = 2 * lax.broadcasted_iota(jnp.int32, (half, TOK_GRP), 0) + core
     col = lax.broadcasted_iota(jnp.int32, (half, TOK_GRP), 1)
@@ -120,13 +117,12 @@
     pick = jnp.where(row == col, 1.0, 0.0).astype(BF16)
     lane = lax.broadcasted_iota(jnp.int32, log_ref.shape, 1)
     logs = jnp.zeros(log_ref.shape, F32)
-    for hp in range(2):
-        at = pl.multiple_of((group * 2 + hp) * TOK_GRP, TOK_GRP)
-        rows = dot(pick, q_ref[pl.ds(at, TOK_GRP), :]).astype(BF16)
+    sides = ((core, own_q, own_uk, own_uv), (1 - core, mate_q, mate_uk, mate_uv))
+    for hp, q_ref, uk_ref, uv_ref in sides:
+        rows = dot(pick, q_ref[:TOK_GRP, :]).astype(BF16)
         for par in range(2):
-            uk = jnp.where(core == hp, own_uk[par], mate_uk[par])
-            uv = jnp.where(core == hp, own_uv[par], mate_uv[par])
-            absorbed = (dot(rows[:, par * NOPE : (par + 1) * NOPE], uk) * SCALE).astype(BF16)
+            narrow = rows[:, par * NOPE : (par + 1) * NOPE]
+            absorbed = (dot(narrow, uk_ref[par]) * SCALE).astype(BF16)
             first = 2 * NOPE + par * ROPE
             scores = dot_t(absorbed, kv_ref[:, :LATENT])
             scores += dot_t(rows[:, first : first + ROPE], kv_ref[:, LATENT:])
@@ -136,20 +132,21 @@
             total = jnp.sum(weights, axis=1, keepdims=True)
             mixture = dot(weights.astype(BF16), kv_ref[:, :LATENT]) / total
             head = hp * 2 + par
-            hv_ref[:, head * VDIM : (head + 1) * VDIM] = dot(mixture.astype(BF16), uv)
+            at = pl.ds(pl.multiple_of(head * VDIM, VDIM), VDIM)
+            hv_ref[:, at] = dot(mixture.astype(BF16), uv_ref[par])
             logs = jnp.where(lane == head, peak + jnp.log(total), logs)
     log_ref[...] = logs
 
 
-def attend_kernel(count_ref, x_ref, kv_hbm, out_hbm, queries, scores, out_ref, kv_ref, sems, in_sems):
+def attend_kernel(
+    count_ref, x_ref, kv_hbm, out_hbm, queries, scores, weights, out_ref, kv_ref, sems, in_sems
+):
     half = x_ref.shape[0]
     slab = kv_ref.shape[2]
     chunk = 256
-    piece = slab // PIECES
     arriving = []
-    for i in range(SLOTS * PIECES):
-        at = (i // PIECES, slice(None), pl.ds(i % PIECES * piece, piece))
-        arriving.append(pltpu.make_async_copy(kv_hbm.at[at], kv_ref.at[at], in_sems.at[i]))
+    for slot in range(SLOTS):
+        arriving.append(pltpu.make_async_copy(kv_hbm.at[slot], kv_ref.at[slot], in_sems.at[slot]))
         arriving[-1].start()
     base = SLOTS * 2 * LATENT
     lane = lax.broadcasted_iota(jnp.int32, (half, 128), 1)
@@ -164,9 +161,8 @@
             first = slot * WIDE + 2 * LATENT + par * ROPE
             queries[at, LATENT:] = x_ref[:, first : first + ROPE]
         peak = jnp.full((2 * half, 1), EMPTY, F32)
+        arriving[slot].wait()
         for first in range(0, slab, chunk):
-            if first % piece == 0:
-                arriving[slot * PIECES + first // piece].wait()
             score = dot(queries[...], kv_ref[slot, :, first : first + chunk])
             position = lax.broadcasted_iota(jnp.int32, score.shape, 1) + first
             score = jnp.where(position < count, score, EMPTY)
@@ -174,12 +170,12 @@
             peak = jnp.maximum(peak, jnp.max(score, axis=1, keepdims=True))
         reference = jnp.maximum(peak, EMPTY / 10)
         total = jnp.zeros((2 * half, 1), F32)
-        mixture = jnp.zeros((2 * half, LATENT), F32)
         for first in range(0, slab, chunk):
-            weights = jnp.exp(scores[:, first : first + chunk] - reference)
-            total += jnp.sum(weights, axis=1, keepdims=True)
-            mixture += dot_t(weights.astype(BF16), kv_ref[slot, :LATENT, first : first + chunk])
+            weight = jnp.exp(scores[:, first : first + chunk] - reference)
+            total += jnp.sum(weight, axis=1, keepdims=True)
+            weights[:, first : first + chunk] = weight.astype(BF16)
         total = jnp.maximum(total, 1.0)
+        mixture = dot_t(weights[...], kv_ref[slot, :LATENT, :])
         mixture = (mixture * (1.0 / total)).astype(BF16)
         log = peak + jnp.log(total)
         start = slot * 2 * LATENT
@@ -209,10 +205,11 @@
         scratch_shapes=[
             pltpu.VMEM((2 * rows, KEY), BF16),
             pltpu.VMEM((2 * rows, kv.shape[2]), F32),
+            pltpu.VMEM((2 * rows, kv.shape[2]), BF16),
             pltpu.VMEM((rows, PART), BF16),
             pltpu.VMEM(kv.shape, BF16),
             pltpu.SemaphoreType.DMA((SLOTS,)),
-            pltpu.SemaphoreType.DMA((SLOTS * PIECES,)),
+            pltpu.SemaphoreType.DMA((SLOTS,)),
         ],
         compiler_params=pltpu.CompilerParams(vmem_limit_bytes=32 << 20),
     )(count, x, in_hbm(kv))
@@ -324,7 +321,6 @@
     chips = zs * xs
     core_id = core.astype(jnp.int32).reshape(1)
     swap = [(i, 1 - i) for i in range(cores)]
-    mate_uk = lax.ppermute(w_uk, "core", swap)
 
     table = lax.dynamic_index_in_dim(slot_sequence, group, 0, keepdims=False)
     table = table.reshape(chips, cores, SLOTS)
@@ -332,8 +328,10 @@
     hp = jnp.arange(2, dtype=jnp.int32)[:, None]
     draft = jnp.arange(DRAFT, dtype=jnp.int32)
     filled = (held >= 0).T[:, :, None]
-    code = ((held >> 4) * (2 * TOK_GRP) + (held & 15) * DRAFT).T[:, :, None]
-    code = jnp.where(filled, code + (hp * TOK_GRP + draft).reshape(-1), -1).reshape(-1, 1)
+    shift = (group - (held >> 4)) & (groups - 1)
+    code = (shift * TOK_GRP + (held & 15) * DRAFT).T[:, :, None]
+    code = code + ((hp != core) * (groups * TOK_GRP) + draft).reshape(-1)
+    code = jnp.where(filled, code, -1).reshape(-1, 1)
     row = ((held >> 4) * TOK_GRP + (held & 15) * 2).T[:, :, None, None]
     row = row + (draft & 1) * (TOK_GRP // 2) + (draft >> 1)
     row = jnp.where(filled[..., None], row, -1)
@@ -351,7 +349,7 @@
     copies = groups * cores
     narrow = pl.pallas_call(
         project_kernel,
-        out_shape=jax.ShapeDtypeStruct((copies, TOK_GRP, NARROW), BF16),
+        out_shape=jax.ShapeDtypeStruct((TOK_GRP, NARROW), BF16),
         in_specs=[HBM] * 3,
         out_specs=VMEM,
         scratch_shapes=[
@@ -360,33 +358,38 @@
         ],
         compiler_params=pltpu.CompilerParams(vmem_limit_bytes=16 << 20),
     )(*(in_hbm(a) for a in (q_compressed, w_q_nope, w_q_rope)))
-    every = lax.all_to_all(narrow, ("group", "core"), 0, 0, tiled=True).reshape(-1, NARROW)
+    late_uk, narrow = lax.optimization_barrier((w_uk, narrow))
+    own_q = [narrow]
+    for k in range(1, groups):
+        own_q.append(lax.ppermute(narrow, "group", [(i, (i + k) % groups) for i in range(groups)]))
+    own_q = jnp.concatenate(own_q, axis=0)
+    mate_q = lax.ppermute(own_q, "core", swap)
+    mate_uk = lax.ppermute(late_uk, "core", swap)
     rows = chips * cores * DRAFT
     wide = pl.pallas_call(
         spread_kernel,
         out_shape=jax.ShapeDtypeStruct((rows, SLOTS * WIDE), BF16),
         grid=(SLOTS,),
-        in_specs=[SMEM, VMEM, pl.BlockSpec((rows, 1), lambda k: (k, 0)), VMEM, VMEM],
+        in_specs=[VMEM, VMEM, pl.BlockSpec((rows, 1), lambda k: (k, 0)), VMEM, VMEM],
         out_specs=pl.BlockSpec((rows, WIDE), lambda k: (0, k)),
         scratch_shapes=[pltpu.VMEM((copies * TOK_GRP, 5 * NOPE), BF16)],
         compiler_params=pltpu.CompilerParams(
             dimension_semantics=("arbitrary",), vmem_limit_bytes=16 << 20
         ),
-    )(core_id, every, code, w_uk, mate_uk)
+    )(own_q, mate_q, code, w_uk, mate_uk)
     slabs_kv = jnp.swapaxes(kv_cache.reshape(kv_cache.shape[2:]), 1, 2)
     late_o, late_uv, wide = lax.optimization_barrier((w_o, w_uv, wide))
     mate_uv = lax.ppermute(late_uv, "core", swap)
     mate_o = lax.ppermute(late_o, "core", swap)
     arrived = exchange(wide, ("z", "x"), chips)
-    place = jnp.stack([group, core]).astype(jnp.int32)
     draft_hv, draft_log = call(
         draft_kernel,
         (
             jax.ShapeDtypeStruct((TOK_GRP // 2, 4 * VDIM), F32),
             jax.ShapeDtypeStruct((TOK_GRP // 2, 128), F32),
         ),
-        (place, every, w_uk, mate_uk, w_uv, mate_uv, draft_kv),
-        [SMEM] + [VMEM] * 6,
+        (core_id, own_q, mate_q, w_uk, mate_uk, w_uv, mate_uv, draft_kv),
+        [SMEM] + [VMEM] * 7,
     )
     partials = attend(count, arrived, slabs_kv)
     back = exchange(partials, ("z", "x"), chips)

time: 145 us -> 142 us (0.979)
  Pallas kernels: 25.4 us -> 23.1 us
  waiting for transfers between devices: 69 us -> 67.2 us
    all_to_all x1 -> x0, waiting for transfers between devices: 8.22 us -> none  [shards(): lax.all_to_all(narrow, ('group', 'core'), 0, 0, tiled=True)]
    ppermute x1 -> x5, waiting for transfers between devices: 0.01 us -> 5.24 us  [the longest x3 4.03 us: shards(): lax.ppermute(narrow, 'group', [(i, (i + k) % groups) for i in range(group...]
    ppermute x1 -> x5, starting transfers between devices: 0.01 us -> 4.79 us  [the longest x3 4.69 us: shards(): lax.ppermute(narrow, 'group', [(i, (i + k) % groups) for i in range(group...]
    all_to_all x1 -> x0, starting transfers between devices: 4.55 us -> none  [shards(): lax.all_to_all(narrow, ('group', 'core'), 0, 0, tiled=True)]
  transfers between devices with their start and end apart: 7 -> 10, of which waited for: 5 -> 6; matrix products, arithmetic and copies ran while one was open for 2% -> 2% of each run, Pallas kernels for 13% -> 10%
where the time goes in v4:
time: 142 us; the launch traced here: 141 us
  waiting for transfers between devices  67.2 us (47%)
  starting transfers between devices  26.5 us (19%)
  Pallas kernels  23.1 us (16%)
  blocking collectives  21.6 us (15%)
  local copies, waits for them, and re-layouts  1.57 us (1%)
    all_to_all x3, waiting for transfers between devices, exchange(): return lax.all_to_all(blocks, axes, 0, 0, tiled=True).reshape(array.shape)  60.7 us
    all_to_all x1, blocking collectives, shards(): lax.all_to_all(sums.reshape(chips, 8, -1), ('z', 'x'), 0, 0, tiled=True)  21.6 us
    all_to_all x3, starting transfers between devices, exchange(): return lax.all_to_all(blocks, axes, 0, 0, tiled=True).reshape(array.shape)  21.3 us
    pallas_call x4, Pallas kernels, call(): pl.pallas_call(kernel, out_shape=outs, in_specs=specs, out_specs=jax.tree...  9.88 us
    pallas_call x1, Pallas kernels, attend(): pl.pallas_call(attend_kernel, out_shape=jax.ShapeDtypeStruct((rows, PART)...  9.49 us
    ppermute x3, starting transfers between devices, shards(): lax.ppermute(narrow, 'group', [(i, (i + k) % groups) for i in range(group...  4.69 us
    ppermute x3, waiting for transfers between devices, shards(): lax.ppermute(narrow, 'group', [(i, (i + k) % groups) for i in range(group...  4.03 us
  transfers between devices with their start and end apart: 10, of which 6 were waited for; matrix products, arithmetic and copies ran while one was open for 2% of the time, Pallas kernels for 10%

profile of v4, /device:TPU:32, one launch (start us, length us, event | category | flops | bytes accessed | tf_op | source)
XLA Modules:
  0.0 141.1 jit_solution(14256726048037326648)
XLA Ops:
  0.0 1.7 %shard_map.109 = bf16[64,384]{1,0:T(8,128)(2,1)S(1)} custom-call(bf16[64,1536]{1,0:T(8,128)(2,1)} %q_hbm.1, bf16[1536,256]{1,0:T(8,128)(2,1)} %wn_hbm.1, bf16[1536,128]{1,0:T(8,128)(2,1)} %wr_hbm.1), custom_call_target="tpu_custom_call" | custom-call | tf_op jit(solution)/shard_map/pallas_call | solution.py:350
  1.7 3.1 %collective-permute-start.2 = (bf16[64,384]{1,0:T(8,128)(2,1)S(1)}, bf16[64,384]{1,0:T(8,128)(2,1)S(1)}, u32[]{:S(2)}, u32[]{:S(2)}) collective-permute-start(bf16[64,384]{1,0:T(8,128)(2,1)S(1)} %shard_map.109), channel_id=1, source_target_pairs={{0,192},{64,0},{128,64},{192,128},{1,193},{65,1},{129,65},{193,129... | collective-permute-start | bytes 147464 | tf_op jit(solution)/shard_map/ppermute | solution.py:364
  4.8 0.6 collective-permute-start.1
  5.4 1.0 collective-permute-start
  6.9 4.0 %collective-permute-done = bf16[64,384]{1,0:T(8,128)(2,1)S(1)} collective-permute-done((bf16[64,384]{1,0:T(8,128)(2,1)S(1)}, bf16[64,384]{1,0:T(8,128)(2,1)S(1)}, u32[]{:S(2)}, u32[]{:S(2)}) %collective-permute-start) | collective-permute-done | bytes 49184 | tf_op jit(solution)/shard_map/ppermute | solution.py:364
  11.3 1.2 collective-permute-done.3.mate_q
  12.5 2.1 %shard_map.110 = bf16[256,2304]{1,0:T(8,128)(2,1)} custom-call(bf16[256,384]{1,0:T(8,128)(2,1)S(1)} %constant_dynamic-update-slice_fusion.own_q, bf16[256,384]{1,0:T(8,128)(2,1)S(1)} %collective-permute-done.3.mate_q, s32[512,1]{1,0:T(8,128)S(1)} %select_n.70.code_ref, bf16[2,128,512]{2,1,0:T(8,128)(2,1)S(1)} %copy-done.1, ...), custom_call_target="tpu_custom_call" | custom-call | tf_op jit(solution)/shard_map/pallas_call | solution.py:369
  14.6 11.3 %all-to-all-start = ((bf16[32,8,2304]{2,1,0:T(8,128)(2,1)}), bf16[32,8,2304]{2,1,0:T(8,128)(2,1)S(1)}, u32[]{:S(2)}, u32[]{:S(2)}) async-start(bf16[32,8,2304]{2,1,0:T(8,128)(2,1)} %bitcast.5), calls=%async_computation | async-start | bytes 2359296 | tf_op jit(solution)/shard_map/all_to_all | solution.py:303
  26.0 0.7 constant_dynamic-slice_fusion.2
  26.8 0.2 fusion
  27.3 28.9 %all-to-all-done = bf16[32,8,2304]{2,1,0:T(8,128)(2,1)S(1)} async-done(((bf16[32,8,2304]{2,1,0:T(8,128)(2,1)}), bf16[32,8,2304]{2,1,0:T(8,128)(2,1)S(1)}, u32[]{:S(2)}, u32[]{:S(2)}) %all-to-all-start) | async-done | bytes 1179680 | tf_op jit(solution)/shard_map/all_to_all | solution.py:303
  56.2 9.5 %shard_map.111 = bf16[256,2176]{1,0:T(8,128)(2,1)} custom-call(s32[2]{0:T(128)S(1)} %compare_select_fusion.2.count_ref, bf16[256,2304]{1,0:T(8,128)(2,1)S(1)} %bitcast.28, bf16[2,576,2048]{2,1,0:T(8,128)(2,1)} %bitcast.32), custom_call_target="tpu_custom_call" | custom-call | tf_op jit(solution)/shard_map/pallas_call | solution.py:200
  65.7 6.6 %all-to-all-start.1 = ((bf16[32,8,2176]{2,1,0:T(8,128)(2,1)}), bf16[32,8,2176]{2,1,0:T(8,128)(2,1)S(1)}, u32[]{:S(2)}, u32[]{:S(2)}) async-start(bf16[32,8,2176]{2,1,0:T(8,128)(2,1)} %bitcast.9), calls=%async_computation.1 | async-start | bytes 2228224 | tf_op jit(solution)/shard_map/all_to_all | solution.py:303
  72.5 0.3 collective-permute-start.5
  72.9 0.2 select_n.69.code_ref
  73.1 1.2 collective-permute-done.5.mate_ref.mate_uv
  74.3 25.8 %all-to-all-done.1 = bf16[32,8,2176]{2,1,0:T(8,128)(2,1)S(1)} async-done(((bf16[32,8,2176]{2,1,0:T(8,128)(2,1)}), bf16[32,8,2176]{2,1,0:T(8,128)(2,1)S(1)}, u32[]{:S(2)}, u32[]{:S(2)}) %all-to-all-start.1) | async-done | bytes 1114144 | tf_op jit(solution)/shard_map/all_to_all | solution.py:303
  100.1 2.7 %shard_map.112 = bf16[256,640]{1,0:T(8,128)(2,1)} custom-call(s32[1]{0:T(128)} %bitcast.core_ref, bf16[256,2176]{1,0:T(8,128)(2,1)S(1)} %bitcast.29, s32[4,256]{1,0:T(4,128)S(1)} %select_n.69.code_ref, bf16[2,512,128]{2,1,0:T(8,128)(2,1)S(1)} %copy-done.2, bf16[2,512,128]{2,1,0:T(8,128)(2,1)S(1)} %collective-permute-done.5.mate_ref.mate_uv), custom_call_target="tpu_custom_call" | custom-call | tf_op jit(solution)/shard_map/pallas_call | solution.py:46
  102.8 3.4 %all-to-all-start.2 = ((bf16[8,32,640]{2,1,0:T(8,128)(2,1)}), bf16[8,32,640]{2,1,0:T(8,128)(2,1)S(1)}, u32[]{:S(2)}, u32[]{:S(2)}) async-start(bf16[8,32,640]{2,1,0:T(8,128)(2,1)} %bitcast.14), calls=%async_computation.2 | async-start | bytes 655360 | tf_op jit(solution)/shard_map/all_to_all | solution.py:303
  106.2 2.2 %shard_map.113 = (f32[32,512]{1,0:T(8,128)S(1)}, f32[32,128]{1,0:T(8,128)S(1)}) custom-call(s32[1]{0:T(128)} %bitcast.core_ref, bf16[256,384]{1,0:T(8,128)(2,1)S(1)} %constant_dynamic-update-slice_fusion.own_q, bf16[256,384]{1,0:T(8,128)(2,1)S(1)} %collective-permute-done.3.mate_q, bf16[2,128,512]{2,1,0:T(8,128)(2,1)S(1)} %copy-done.1, ...), custom_call_target="tpu_custom_call" | custom-call | tf_op jit(solution)/shard_map/pallas_call | solution.py:46
  108.4 6.0 %all-to-all-done.2 = bf16[8,32,640]{2,1,0:T(8,128)(2,1)S(1)} async-done(((bf16[8,32,640]{2,1,0:T(8,128)(2,1)}), bf16[8,32,640]{2,1,0:T(8,128)(2,1)S(1)}, u32[]{:S(2)}, u32[]{:S(2)}) %all-to-all-start.2) | async-done | bytes 327712 | tf_op jit(solution)/shard_map/all_to_all | solution.py:303
  114.4 4.3 %shard_map.114 = bf16[32,7168]{1,0:T(8,128)(2,1)S(1)} custom-call(s32[1]{0:T(128)} %bitcast.core_ref, bf16[256,640]{1,0:T(8,128)(2,1)S(1)} %bitcast.31, f32[32,512]{1,0:T(8,128)S(1)} %get-tuple-element.16.hv_ref, f32[32,128]{1,0:T(8,128)S(1)} %get-tuple-element.17.log_ref, bf16[256,7168]{1,0:T(8,128)(2,1)} %own_hbm.1, ...), custom_call_target="tpu_custom_call" | custom-call | tf_op jit(solution)/shard_map/pallas_call | solution.py:46
  118.8 21.6 %all_to_all.20.tiles_ref = bf16[32,8,896]{2,1,0:T(8,128)(2,1)S(1)} all-to-all(bf16[32,8,896]{2,1,0:T(8,128)(2,1)S(1)} %bitcast.33), channel_id=1, replica_groups=mesh['group'=4,'z'=8,'x'=4,'core'=2] {'z','x'}, dimensions={0} | all-to-all | bytes 917504 | tf_op jit(solution)/shard_map/all_to_all | solution.py:410
  140.4 0.7 shard_map.115
  (40 shorter events, 1.5 us)
Async XLA Ops:
  0.0 6.4 %copy-start = (s32[4,64,2]{1,2,0:T(2,128)S(1)}, s32[4,64,2]{1,2,0:T(2,128)}, u32[]{:S(2)}) copy-start(s32[4,64,2]{1,2,0:T(2,128)} %param.20) | copy-start | bytes 6148
  0.0 6.4 %copy-start.1 = (bf16[2,128,512]{2,1,0:T(8,128)(2,1)S(1)}, bf16[2,128,512]{2,1,0:T(8,128)(2,1)}, u32[]{:S(2)}) copy-start(bf16[2,128,512]{2,1,0:T(8,128)(2,1)} %own_uk.1) | copy-start | bytes 786436
  1.7 9.3 %collective-permute-start.2 = (bf16[64,384]{1,0:T(8,128)(2,1)S(1)}, bf16[64,384]{1,0:T(8,128)(2,1)S(1)}, u32[]{:S(2)}, u32[]{:S(2)}) collective-permute-start(bf16[64,384]{1,0:T(8,128)(2,1)S(1)} %shard_map.109), channel_id=1, source_target_pairs={{0,192},{64,0},{128,64},{192,128},{1,193},{65,1},{129,65},{193,129... | collective-permute-start | bytes 147464 | tf_op jit(solution)/shard_map/ppermute | solution.py:364
  4.8 6.1 %collective-permute-start.1 = (bf16[64,384]{1,0:T(8,128)(2,1)S(1)}, bf16[64,384]{1,0:T(8,128)(2,1)S(1)}, u32[]{:S(2)}, u32[]{:S(2)}) collective-permute-start(bf16[64,384]{1,0:T(8,128)(2,1)S(1)} %shard_map.109), channel_id=1, source_target_pairs={{0,128},{64,192},{128,0},{192,64},{1,129},{65,193},{129,1},{193,65... | collective-permute-start | bytes 147464 | tf_op jit(solution)/shard_map/ppermute | solution.py:364
  5.4 5.5 %collective-permute-start = (bf16[64,384]{1,0:T(8,128)(2,1)S(1)}, bf16[64,384]{1,0:T(8,128)(2,1)S(1)}, u32[]{:S(2)}, u32[]{:S(2)}) collective-permute-start(bf16[64,384]{1,0:T(8,128)(2,1)S(1)} %shard_map.109), channel_id=1, source_target_pairs={{0,64},{64,128},{128,192},{192,0},{1,65},{65,129},{129,193},{193,1... | collective-permute-start | bytes 147464 | tf_op jit(solution)/shard_map/ppermute | solution.py:364
  6.4 6.1 %collective-permute-start.4 = (bf16[2,128,512]{2,1,0:T(8,128)(2,1)S(1)}, bf16[2,128,512]{2,1,0:T(8,128)(2,1)S(1)}, u32[]{:S(2)}, u32[]{:S(2)}) collective-permute-start(bf16[2,128,512]{2,1,0:T(8,128)(2,1)S(1)} %copy-done.1), channel_id=1, source_target_pairs={{0,1},{1,0},{2,3},{3,2},{4,5},{5,4},{6,7},{7,6},{8,9},{9,8},{10,11... | collective-permute-start | bytes 786440 | tf_op jit(solution)/shard_map/ppermute | solution.py:367
  11.0 1.5 %collective-permute-start.3 = (bf16[256,384]{1,0:T(8,128)(2,1)S(1)}, bf16[256,384]{1,0:T(8,128)(2,1)S(1)}, u32[]{:S(2)}, u32[]{:S(2)}) collective-permute-start(bf16[256,384]{1,0:T(8,128)(2,1)S(1)} %constant_dynamic-update-slice_fusion.own_q), channel_id=1, source_target_pairs={{0,1},{1,0},{2,3},{3,2},{4,5},{5,4},{6,7},{7,6},{8,9},{9,8},{10,11... | collective-permute-start | bytes 589832 | tf_op jit(solution)/shard_map/ppermute | solution.py:366
  14.6 12.5 %copy-start.4 = (s32[64]{0:T(128)S(1)}, s32[64]{0:T(128)}, u32[]{:S(2)}) copy-start(s32[64]{0:T(128)} %param.19) | copy-start | bytes 772
  14.6 41.6 %all-to-all-start = ((bf16[32,8,2304]{2,1,0:T(8,128)(2,1)}), bf16[32,8,2304]{2,1,0:T(8,128)(2,1)S(1)}, u32[]{:S(2)}, u32[]{:S(2)}) async-start(bf16[32,8,2304]{2,1,0:T(8,128)(2,1)} %bitcast.5), calls=%async_computation | async-start | bytes 2359296 | tf_op jit(solution)/shard_map/all_to_all | solution.py:303
  25.9 82.5 %collective-permute-start.6 = (bf16[256,7168]{1,0:T(8,128)(2,1)}, bf16[256,7168]{1,0:T(8,128)(2,1)}, u32[]{:S(2)}, u32[]{:S(2)}) collective-permute-start(bf16[256,7168]{1,0:T(8,128)(2,1)} %own_hbm.1), channel_id=1, source_target_pairs={{0,1},{1,0},{2,3},{3,2},{4,5},{5,4},{6,7},{7,6},{8,9},{9,8},{10,11... | collective-permute-start | bytes 11010056 | tf_op jit(solution)/shard_map/ppermute | solution.py:383
  65.7 6.7 %copy-start.2 = (bf16[2,512,128]{2,1,0:T(8,128)(2,1)S(1)}, bf16[2,512,128]{2,1,0:T(8,128)(2,1)}, u32[]{:S(2)}) copy-start(bf16[2,512,128]{2,1,0:T(8,128)(2,1)} %own_uv.1) | copy-start | bytes 786436
  65.7 34.4 %all-to-all-start.1 = ((bf16[32,8,2176]{2,1,0:T(8,128)(2,1)}), bf16[32,8,2176]{2,1,0:T(8,128)(2,1)S(1)}, u32[]{:S(2)}, u32[]{:S(2)}) async-start(bf16[32,8,2176]{2,1,0:T(8,128)(2,1)} %bitcast.9), calls=%async_computation.1 | async-start | bytes 2228224 | tf_op jit(solution)/shard_map/all_to_all | solution.py:303
  72.5 1.8 %collective-permute-start.5 = (bf16[2,512,128]{2,1,0:T(8,128)(2,1)S(1)}, bf16[2,512,128]{2,1,0:T(8,128)(2,1)S(1)}, u32[]{:S(2)}, u32[]{:S(2)}) collective-permute-start(bf16[2,512,128]{2,1,0:T(8,128)(2,1)S(1)} %copy-done.2), channel_id=1, source_target_pairs={{0,1},{1,0},{2,3},{3,2},{4,5},{5,4},{6,7},{7,6},{8,9},{9,8},{10,11... | collective-permute-start | bytes 786440 | tf_op jit(solution)/shard_map/ppermute | solution.py:382
  100.1 6.1 %copy-start.3 = (bf16[64,576]{1,0:T(8,128)(2,1)S(1)}, bf16[64,576]{1,0:T(8,128)(2,1)}, u32[]{:S(2)}) copy-start(bf16[64,576]{1,0:T(8,128)(2,1)} %kv_ref.1) | copy-start | bytes 221188
  102.8 11.6 %all-to-all-start.2 = ((bf16[8,32,640]{2,1,0:T(8,128)(2,1)}), bf16[8,32,640]{2,1,0:T(8,128)(2,1)S(1)}, u32[]{:S(2)}, u32[]{:S(2)}) async-start(bf16[8,32,640]{2,1,0:T(8,128)(2,1)} %bitcast.14), calls=%async_computation.2 | async-start | bytes 655360 | tf_op jit(solution)/shard_map/all_to_all | solution.py:303

commit v5 on v4

--- a/solution.py
+++ b/solution.py
@@ -18,7 +18,6 @@
 WIDE = 2 * LATENT + 2 * ROPE
 PART = SLOTS * 2 * LATENT + 128
 NARROW = 2 * NOPE + 2 * ROPE
-PIECES = 4
 EMPTY = -1e30
 SCALE = (NOPE + ROPE) ** -0.5
 F32 = jnp.float32
@@ -42,7 +41,7 @@
     return lax.dot_general(a, b, CONTRACT_LAST, preferred_element_type=F32)
 
 
-def call(kernel, outs, args, specs, scratch=(), vmem=32):
+def call(kernel, outs, args, specs, scratch=(), vmem=32, cost=None):
     return pl.pallas_call(
         kernel,
         out_shape=outs,
@@ -50,6 +49,7 @@
         out_specs=jax.tree.map(lambda _: VMEM, outs),
         scratch_shapes=list(scratch),
         compiler_params=pltpu.CompilerParams(vmem_limit_bytes=vmem << 20),
+        cost_estimate=cost,
     )(*args)
 
 
@@ -139,15 +139,11 @@
 
 
 def attend_kernel(
-    count_ref, x_ref, kv_hbm, out_hbm, queries, scores, weights, out_ref, kv_ref, sems, in_sems
+    count_ref, x_ref, kv_ref, out_hbm, queries, scores, weights, out_ref, sems
 ):
     half = x_ref.shape[0]
     slab = kv_ref.shape[2]
     chunk = 256
-    arriving = []
-    for slot in range(SLOTS):
-        arriving.append(pltpu.make_async_copy(kv_hbm.at[slot], kv_ref.at[slot], in_sems.at[slot]))
-        arriving[-1].start()
     base = SLOTS * 2 * LATENT
     lane = lax.broadcasted_iota(jnp.int32, (half, 128), 1)
     tile = jnp.zeros((half, 128), F32)
@@ -161,7 +157,6 @@
             first = slot * WIDE + 2 * LATENT + par * ROPE
             queries[at, LATENT:] = x_ref[:, first : first + ROPE]
         peak = jnp.full((2 * half, 1), EMPTY, F32)
-        arriving[slot].wait()
         for first in range(0, slab, chunk):
             score = dot(queries[...], kv_ref[slot, :, first : first + chunk])
             position = lax.broadcasted_iota(jnp.int32, score.shape, 1) + first
@@ -200,19 +195,17 @@
     return pl.pallas_call(
         attend_kernel,
         out_shape=jax.ShapeDtypeStruct((rows, PART), BF16),
-        in_specs=[SMEM, VMEM, HBM],
+        in_specs=[SMEM, VMEM, VMEM],
         out_specs=HBM,
         scratch_shapes=[
             pltpu.VMEM((2 * rows, KEY), BF16),
             pltpu.VMEM((2 * rows, kv.shape[2]), F32),
             pltpu.VMEM((2 * rows, kv.shape[2]), BF16),
             pltpu.VMEM((rows, PART), BF16),
-            pltpu.VMEM(kv.shape, BF16),
-            pltpu.SemaphoreType.DMA((SLOTS,)),
             pltpu.SemaphoreType.DMA((SLOTS,)),
         ],
         compiler_params=pltpu.CompilerParams(vmem_limit_bytes=32 << 20),
-    )(count, x, in_hbm(kv))
+    )(count, x, kv)
 
 
 def merge_kernel(core_ref, y_ref, code_ref, own_ref, mate_ref, out_ref):
@@ -247,16 +240,8 @@
     out_ref[:, 4 * VDIM :] = tile.astype(BF16)
 
 
-def finish_kernel(core_ref, z_ref, hv_ref, log_ref, own_hbm, mate_hbm, out_ref, o_ref, sems):
+def finish_kernel(core_ref, z_ref, hv_ref, log_ref, o_ref, out_ref):
     half = hv_ref.shape[0]
-    piece = out_ref.shape[1] // PIECES
-    arriving = []
-    for i in range(PIECES):
-        at = (slice(None), pl.ds(i * piece, piece))
-        for side, source in enumerate((own_hbm, mate_hbm)):
-            target = o_ref.at[side].at[at]
-            arriving.append(pltpu.make_async_copy(source.at[at], target, sems.at[2 * i + side]))
-            arriving[-1].start()
     values = []
     for head in range(4):
         logs = [log_ref[:, head : head + 1]]
@@ -282,13 +267,10 @@
             summed += weight * part
         values.append(summed / total)
     pairs = [jnp.concatenate(values[hp * 2 : hp * 2 + 2], axis=1) for hp in range(2)]
-    own = jnp.where(core_ref[0] == 0, pairs[0], pairs[1]).astype(BF16)
-    mate = jnp.where(core_ref[0] == 0, pairs[1], pairs[0]).astype(BF16)
-    for i in range(PIECES):
-        arriving[2 * i].wait()
-        arriving[2 * i + 1].wait()
-        at = slice(i * piece, (i + 1) * piece)
-        out_ref[:, at] = (dot(own, o_ref[0, :, at]) + dot(mate, o_ref[1, :, at])).astype(BF16)
+    own = jnp.where(core_ref[0] == 0, pairs[0], pairs[1])
+    mate = jnp.where(core_ref[0] == 0, pairs[1], pairs[0])
+    head_values = jnp.concatenate([own, mate], axis=1).astype(BF16)
+    out_ref[...] = dot(head_values, o_ref[...]).astype(BF16)
 
 
 def total_kernel(tiles_ref, out_ref):
@@ -376,9 +358,11 @@
         compiler_params=pltpu.CompilerParams(
             dimension_semantics=("arbitrary",), vmem_limit_bytes=16 << 20
         ),
+        cost_estimate=pl.CostEstimate(flops=30 << 30, transcendentals=0, bytes_accessed=80 << 20),
     )(own_q, mate_q, code, w_uk, mate_uk)
     slabs_kv = jnp.swapaxes(kv_cache.reshape(kv_cache.shape[2:]), 1, 2)
-    late_o, late_uv, wide = lax.optimization_barrier((w_o, w_uv, wide))
+    late_uv, wide = lax.optimization_barrier((w_uv, wide))
+    late_o, count = lax.optimization_barrier((w_o, count))
     mate_uv = lax.ppermute(late_uv, "core", swap)
     mate_o = lax.ppermute(late_o, "core", swap)
     arrived = exchange(wide, ("z", "x"), chips)
@@ -393,19 +377,22 @@
     )
     partials = attend(count, arrived, slabs_kv)
     back = exchange(partials, ("z", "x"), chips)
+    both_o = jnp.concatenate([w_o, mate_o], axis=0)
+    back, draft_hv, draft_log, both_o = lax.optimization_barrier((back, draft_hv, draft_log, both_o))
     merged = call(
         merge_kernel,
         jax.ShapeDtypeStruct((groups * TOK_GRP, 4 * VDIM + 128), BF16),
         (core_id, back, row, w_uv, mate_uv),
         [SMEM] + [VMEM] * 4,
+        vmem=16,
+        cost=pl.CostEstimate(flops=3 << 30, transcendentals=1 << 19, bytes_accessed=8 << 20),
     )
     home = exchange(merged, ("group", "core"), copies)
     sums = call(
         finish_kernel,
         jax.ShapeDtypeStruct((chips, w_o.shape[1]), BF16),
-        (core_id, home, draft_hv, draft_log, in_hbm(w_o), in_hbm(mate_o)),
-        [SMEM, VMEM, VMEM, VMEM, HBM, HBM],
-        [pltpu.VMEM((2, *w_o.shape), BF16), pltpu.SemaphoreType.DMA((2 * PIECES,))],
+        (core_id, home, draft_hv, draft_log, both_o),
+        [SMEM] + [VMEM] * 4,
     )
     tiles = lax.all_to_all(sums.reshape(chips, 8, -1), ("z", "x"), 0, 0, tiled=True)
     return call(

time: 142 us -> 141 us (level)
  blocking collectives: 21.6 us -> 76.5 us
  waiting for transfers between devices: 67.2 us -> 24.1 us
  starting transfers between devices: 26.5 us -> 11.7 us
  other arithmetic: 0.8 us -> 8.01 us
  Pallas kernels: 23.1 us -> 17.7 us
    all_to_all x0 -> x2, blocking collectives: none -> 54.4 us  [exchange(): return lax.all_to_all(blocks, axes, 0, 0, tiled=True).reshape(array.shape)]
    all_to_all x3 -> x1, waiting for transfers between devices: 60.7 us -> 17.5 us  [exchange(): return lax.all_to_all(blocks, axes, 0, 0, tiled=True).reshape(array.shape)]
    all_to_all x3 -> x1, starting transfers between devices: 21.3 us -> 4.78 us  [exchange(): return lax.all_to_all(blocks, axes, 0, 0, tiled=True).reshape(array.shape)]
    concatenate x0 -> x1, other arithmetic: none -> 6.58 us  [shards(): both_o = jnp.concatenate([w_o, mate_o], axis=0)]
    ppermute x1, waiting for transfers between devices: 1.21 us -> 5.36 us  [shards(): mate_q = lax.ppermute(own_q, 'core', swap)]
    ppermute x3, waiting for transfers between devices: 4.03 us -> 0.01 us  [shards(): lax.ppermute(narrow, 'group', [(i, (i + k) % groups) for i in range(group...]
    pallas_call x4, Pallas kernels: 9.88 us -> 6.89 us  [call(): pl.pallas_call(kernel, out_shape=outs, in_specs=specs, out_specs=jax.tree...]
    pallas_call x1, Pallas kernels: 9.49 us -> 7.89 us  [attend(): pl.pallas_call(attend_kernel, out_shape=jax.ShapeDtypeStruct((rows, PART)...]
  transfers between devices with their start and end apart: 10 -> 8, of which waited for: 6 -> 4; matrix products, arithmetic and copies ran while one was open for 2% -> 7% of each run, Pallas kernels for 10% -> 8%
where the time goes in v5:
time: 141 us
  blocking collectives  76.5 us (54%)
  waiting for transfers between devices  24.1 us (17%)
  Pallas kernels  17.7 us (13%)
  starting transfers between devices  11.7 us (8%)
  other arithmetic  8.01 us (6%)
  local copies, waits for them, and re-layouts  2.72 us (2%)
    all_to_all x2, blocking collectives, exchange(): return lax.all_to_all(blocks, axes, 0, 0, tiled=True).reshape(array.shape)  54.4 us
    all_to_all x1, blocking collectives, shards(): lax.all_to_all(sums.reshape(chips, 8, -1), ('z', 'x'), 0, 0, tiled=True)  22.1 us
    all_to_all x1, waiting for transfers between devices, exchange(): return lax.all_to_all(blocks, axes, 0, 0, tiled=True).reshape(array.shape)  17.5 us
    pallas_call x1, Pallas kernels, attend(): pl.pallas_call(attend_kernel, out_shape=jax.ShapeDtypeStruct((rows, PART)...  7.89 us
    pallas_call x4, Pallas kernels, call(): pl.pallas_call(kernel, out_shape=outs, in_specs=specs, out_specs=jax.tree...  6.89 us
    concatenate x1, other arithmetic, shards(): both_o = jnp.concatenate([w_o, mate_o], axis=0)  6.58 us
    ppermute x3, starting transfers between devices, shards(): lax.ppermute(narrow, 'group', [(i, (i + k) % groups) for i in range(group...  5.9 us
    ppermute x1, waiting for transfers between devices, shards(): mate_q = lax.ppermute(own_q, 'core', swap)  5.36 us
  transfers between devices with their start and end apart: 8, of which 4 were waited for; matrix products, arithmetic and copies ran while one was open for 7% of the time, Pallas kernels for 8%

profile of v5, /device:TPU:32, one launch (start us, length us, event | category | flops | bytes accessed | tf_op | source)
XLA Modules:
  0.0 141.0 jit_solution(15573308969301220629)
XLA Ops:
  0.0 1.6 %shard_map.109 = bf16[64,384]{1,0:T(8,128)(2,1)S(1)} custom-call(bf16[64,1536]{1,0:T(8,128)(2,1)} %q_hbm.1, bf16[1536,256]{1,0:T(8,128)(2,1)} %wn_hbm.1, bf16[1536,128]{1,0:T(8,128)(2,1)} %wr_hbm.1), custom_call_target="tpu_custom_call" | custom-call | tf_op jit(solution)/shard_map/pallas_call | solution.py:332
  1.7 1.7 %collective-permute-start = (bf16[64,384]{1,0:T(8,128)(2,1)S(1)}, bf16[64,384]{1,0:T(8,128)(2,1)S(1)}, u32[]{:S(2)}, u32[]{:S(2)}) collective-permute-start(bf16[64,384]{1,0:T(8,128)(2,1)S(1)} %shard_map.109), channel_id=1, source_target_pairs={{0,64},{64,128},{128,192},{192,0},{1,65},{65,129},{129,193},{193,1... | collective-permute-start | bytes 147464 | tf_op jit(solution)/shard_map/ppermute | solution.py:346
  3.3 2.9 %collective-permute-start.1 = (bf16[64,384]{1,0:T(8,128)(2,1)S(1)}, bf16[64,384]{1,0:T(8,128)(2,1)S(1)}, u32[]{:S(2)}, u32[]{:S(2)}) collective-permute-start(bf16[64,384]{1,0:T(8,128)(2,1)S(1)} %shard_map.109), channel_id=1, source_target_pairs={{0,128},{64,192},{128,0},{192,64},{1,129},{65,193},{129,1},{193,65... | collective-permute-start | bytes 147464 | tf_op jit(solution)/shard_map/ppermute | solution.py:346
  6.2 1.3 collective-permute-start.2
  7.7 0.7 constant_dynamic-slice_fusion.2
  8.7 0.2 fusion.3
  8.9 0.8 fusion.2
  9.8 0.5 collective-permute-start.4
  11.2 5.4 %collective-permute-done.3.mate_q = bf16[256,384]{1,0:T(8,128)(2,1)S(1)} collective-permute-done((bf16[256,384]{1,0:T(8,128)(2,1)S(1)}, bf16[256,384]{1,0:T(8,128)(2,1)S(1)}, u32[]{:S(2)}, u32[]{:S(2)}) %collective-permute-start.3) | collective-permute-done | bytes 196640 | tf_op jit(solution)/shard_map/ppermute | solution.py:348
  16.6 0.9 copy-done.3
  17.6 1.3 shard_map.110
  18.9 43.6 %all_to_all.20 = bf16[32,8,2304]{2,1,0:T(8,128)(2,1)S(1)} all-to-all(bf16[32,8,2304]{2,1,0:T(8,128)(2,1)S(1)} %bitcast.32), channel_id=1, replica_groups=mesh['group'=4,'z'=8,'x'=4,'core'=2] {'z','x'}, dimensions={0} | all-to-all | bytes 2359296 | tf_op jit(solution)/shard_map/all_to_all | solution.py:285
  62.5 7.9 %shard_map.111 = bf16[256,2176]{1,0:T(8,128)(2,1)} custom-call(s32[2]{0:T(128)S(1)} %get-tuple-element.17.count_ref, bf16[256,2304]{1,0:T(8,128)(2,1)S(1)} %bitcast.29, bf16[2,576,2048]{2,1,0:T(8,128)(2,1)S(1)} %bitcast.28), custom_call_target="tpu_custom_call" | custom-call | tf_op jit(solution)/shard_map/pallas_call | solution.py:195
  70.4 4.8 %all-to-all-start.1 = ((bf16[32,8,2176]{2,1,0:T(8,128)(2,1)}), bf16[32,8,2176]{2,1,0:T(8,128)(2,1)S(1)}, u32[]{:S(2)}, u32[]{:S(2)}) async-start(bf16[32,8,2176]{2,1,0:T(8,128)(2,1)} %bitcast.9), calls=%async_computation.1 | async-start | bytes 2228224 | tf_op jit(solution)/shard_map/all_to_all | solution.py:285
  75.3 0.3 collective-permute-start.5
  75.9 1.2 collective-permute-done.5.mate_uv.mate_ref
  77.1 2.2 %shard_map.112 = (f32[32,512]{1,0:T(8,128)S(1)}, f32[32,128]{1,0:T(8,128)S(1)}) custom-call(s32[1]{0:T(128)} %bitcast.core_ref, bf16[256,384]{1,0:T(8,128)(2,1)S(1)} %constant_dynamic-update-slice_fusion.own_q, bf16[256,384]{1,0:T(8,128)(2,1)S(1)} %collective-permute-done.3.mate_q, bf16[2,128,512]{2,1,0:T(8,128)(2,1)S(1)} %copy-done.4, ...), custom_call_target="tpu_custom_call" | custom-call | tf_op jit(solution)/shard_map/pallas_call | solution.py:45
  79.3 6.6 %pad_maximum_fusion.o_ref = bf16[512,7168]{1,0:T(8,128)(2,1)} fusion(bf16[256,7168]{1,0:T(8,128)(2,1)} %collective-permute-done.6, bf16[256,7168]{1,0:T(8,128)(2,1)} %param.16), kind=kLoop, calls=%fused_computation | loop fusion | flops 14680064 | bytes 14680064 | tf_op jit(solution)/shard_map/concatenate | solution.py:380
  85.9 17.5 %all-to-all-done.1 = bf16[32,8,2176]{2,1,0:T(8,128)(2,1)S(1)} async-done(((bf16[32,8,2176]{2,1,0:T(8,128)(2,1)}), bf16[32,8,2176]{2,1,0:T(8,128)(2,1)S(1)}, u32[]{:S(2)}, u32[]{:S(2)}) %all-to-all-start.1) | async-done | bytes 1114144 | tf_op jit(solution)/shard_map/all_to_all | solution.py:285
  103.4 2.0 %shard_map.113 = bf16[256,640]{1,0:T(8,128)(2,1)S(1)} custom-call(s32[1]{0:T(128)} %bitcast.core_ref, bf16[256,2176]{1,0:T(8,128)(2,1)S(1)} %bitcast.33, s32[4,256]{1,0:T(4,128)S(1)} %select_n.69.code_ref, bf16[2,512,128]{2,1,0:T(8,128)(2,1)S(1)} %copy-done.5, bf16[2,512,128]{2,1,0:T(8,128)(2,1)S(1)} %collective-permute-done.5.mate_uv.mate_ref), custom_call_target="tpu_custom_call" | custom-call | flops 3221225472 | bytes 8388608 | tf_op jit(solution)/shard_map/pallas_call | solution.py:45
  105.4 10.7 %all_to_all.21 = bf16[8,32,640]{2,1,0:T(8,128)(2,1)S(1)} all-to-all(bf16[8,32,640]{2,1,0:T(8,128)(2,1)S(1)} %bitcast.34), channel_id=1, replica_groups=mesh['group'=4,'z'=8,'x'=4,'core'=2] {'group','core'}, dimensions={0} | all-to-all | bytes 655360 | tf_op jit(solution)/shard_map/all_to_all | solution.py:285
  116.1 2.0 %shard_map.114 = bf16[32,7168]{1,0:T(8,128)(2,1)S(1)} custom-call(s32[1]{0:T(128)} %bitcast.core_ref, bf16[256,640]{1,0:T(8,128)(2,1)S(1)} %bitcast.31, f32[32,512]{1,0:T(8,128)S(1)} %get-tuple-element.26.hv_ref, f32[32,128]{1,0:T(8,128)S(1)} %get-tuple-element.27.log_ref, bf16[512,7168]{1,0:T(8,128)(2,1)S(1)} %copy-done.1), custom_call_target="tpu_custom_call" | custom-call | tf_op jit(solution)/shard_map/pallas_call | solution.py:45
  118.2 22.1 %all_to_all.22.tiles_ref = bf16[32,8,896]{2,1,0:T(8,128)(2,1)S(1)} all-to-all(bf16[32,8,896]{2,1,0:T(8,128)(2,1)S(1)} %bitcast.35), channel_id=1, replica_groups=mesh['group'=4,'z'=8,'x'=4,'core'=2] {'z','x'}, dimensions={0} | all-to-all | bytes 917504 | tf_op jit(solution)/shard_map/all_to_all | solution.py:397
  140.3 0.7 shard_map.115
  (43 shorter events, 1.8 us)
Async XLA Ops:
  0.0 7.6 %copy-start = (s32[4,64,2]{1,2,0:T(2,128)S(1)}, s32[4,64,2]{1,2,0:T(2,128)}, u32[]{:S(2)}) copy-start(s32[4,64,2]{1,2,0:T(2,128)} %param.20) | copy-start | bytes 6148
  1.7 9.0 %collective-permute-start = (bf16[64,384]{1,0:T(8,128)(2,1)S(1)}, bf16[64,384]{1,0:T(8,128)(2,1)S(1)}, u32[]{:S(2)}, u32[]{:S(2)}) collective-permute-start(bf16[64,384]{1,0:T(8,128)(2,1)S(1)} %shard_map.109), channel_id=1, source_target_pairs={{0,64},{64,128},{128,192},{192,0},{1,65},{65,129},{129,193},{193,1... | collective-permute-start | bytes 147464 | tf_op jit(solution)/shard_map/ppermute | solution.py:346
  3.3 7.4 %collective-permute-start.1 = (bf16[64,384]{1,0:T(8,128)(2,1)S(1)}, bf16[64,384]{1,0:T(8,128)(2,1)S(1)}, u32[]{:S(2)}, u32[]{:S(2)}) collective-permute-start(bf16[64,384]{1,0:T(8,128)(2,1)S(1)} %shard_map.109), channel_id=1, source_target_pairs={{0,128},{64,192},{128,0},{192,64},{1,129},{65,193},{129,1},{193,65... | collective-permute-start | bytes 147464 | tf_op jit(solution)/shard_map/ppermute | solution.py:346
  6.2 4.5 %collective-permute-start.2 = (bf16[64,384]{1,0:T(8,128)(2,1)S(1)}, bf16[64,384]{1,0:T(8,128)(2,1)S(1)}, u32[]{:S(2)}, u32[]{:S(2)}) collective-permute-start(bf16[64,384]{1,0:T(8,128)(2,1)S(1)} %shard_map.109), channel_id=1, source_target_pairs={{0,192},{64,0},{128,64},{192,128},{1,193},{65,1},{129,65},{193,129... | collective-permute-start | bytes 147464 | tf_op jit(solution)/shard_map/ppermute | solution.py:346
  9.7 69.6 %collective-permute-start.6 = (bf16[256,7168]{1,0:T(8,128)(2,1)}, bf16[256,7168]{1,0:T(8,128)(2,1)}, u32[]{:S(2)}, u32[]{:S(2)}) collective-permute-start(bf16[256,7168]{1,0:T(8,128)(2,1)} %param.16), channel_id=1, source_target_pairs={{0,1},{1,0},{2,3},{3,2},{4,5},{5,4},{6,7},{7,6},{8,9},{9,8},{10,11... | collective-permute-start | bytes 11010056 | tf_op jit(solution)/shard_map/ppermute | solution.py:367
  9.8 6.8 %collective-permute-start.4 = (bf16[2,128,512]{2,1,0:T(8,128)(2,1)}, bf16[2,128,512]{2,1,0:T(8,128)(2,1)S(1)}, u32[]{:S(2)}, u32[]{:S(2)}) collective-permute-start(bf16[2,128,512]{2,1,0:T(8,128)(2,1)} %own_uk.1), channel_id=1, source_target_pairs={{0,1},{1,0},{2,3},{3,2},{4,5},{5,4},{6,7},{7,6},{8,9},{9,8},{10,11... | collective-permute-start | bytes 786440 | tf_op jit(solution)/shard_map/ppermute | solution.py:349
  10.8 5.8 %collective-permute-start.3 = (bf16[256,384]{1,0:T(8,128)(2,1)S(1)}, bf16[256,384]{1,0:T(8,128)(2,1)S(1)}, u32[]{:S(2)}, u32[]{:S(2)}) collective-permute-start(bf16[256,384]{1,0:T(8,128)(2,1)S(1)} %constant_dynamic-update-slice_fusion.own_q), channel_id=1, source_target_pairs={{0,1},{1,0},{2,3},{3,2},{4,5},{5,4},{6,7},{7,6},{8,9},{9,8},{10,11... | collective-permute-start | bytes 589832 | tf_op jit(solution)/shard_map/ppermute | solution.py:348
  16.6 0.9 copy-start.3
  17.6 45.0 %copy-start.2 = (bf16[1,1,2,2048,576]{3,4,2,1,0:T(8,128)(2,1)S(1)}, bf16[1,1,2,2048,576]{3,4,2,1,0:T(8,128)(2,1)}, u32[]{:S(2)}) copy-start(bf16[1,1,2,2048,576]{3,4,2,1,0:T(8,128)(2,1)} %param.17) | copy-start | bytes 14155780
  62.5 12.8 %copy-start.5 = (bf16[2,512,128]{2,1,0:T(8,128)(2,1)S(1)}, bf16[2,512,128]{2,1,0:T(8,128)(2,1)}, u32[]{:S(2)}) copy-start(bf16[2,512,128]{2,1,0:T(8,128)(2,1)} %own_ref.3) | copy-start | bytes 786436
  62.5 14.6 %copy-start.4 = (bf16[2,128,512]{2,1,0:T(8,128)(2,1)S(1)}, bf16[2,128,512]{2,1,0:T(8,128)(2,1)}, u32[]{:S(2)}) copy-start(bf16[2,128,512]{2,1,0:T(8,128)(2,1)} %own_uk.1) | copy-start | bytes 786436
  62.5 14.6 %copy-start.6 = (bf16[64,576]{1,0:T(8,128)(2,1)S(1)}, bf16[64,576]{1,0:T(8,128)(2,1)}, u32[]{:S(2)}) copy-start(bf16[64,576]{1,0:T(8,128)(2,1)} %kv_ref.1) | copy-start | bytes 221188
  70.4 33.0 %all-to-all-start.1 = ((bf16[32,8,2176]{2,1,0:T(8,128)(2,1)}), bf16[32,8,2176]{2,1,0:T(8,128)(2,1)S(1)}, u32[]{:S(2)}, u32[]{:S(2)}) async-start(bf16[32,8,2176]{2,1,0:T(8,128)(2,1)} %bitcast.9), calls=%async_computation.1 | async-start | bytes 2228224 | tf_op jit(solution)/shard_map/all_to_all | solution.py:285
  75.3 1.8 %collective-permute-start.5 = (bf16[2,512,128]{2,1,0:T(8,128)(2,1)S(1)}, bf16[2,512,128]{2,1,0:T(8,128)(2,1)S(1)}, u32[]{:S(2)}, u32[]{:S(2)}) collective-permute-start(bf16[2,512,128]{2,1,0:T(8,128)(2,1)S(1)} %copy-done.5), channel_id=1, source_target_pairs={{0,1},{1,0},{2,3},{3,2},{4,5},{5,4},{6,7},{7,6},{8,9},{9,8},{10,11... | collective-permute-start | bytes 786440 | tf_op jit(solution)/shard_map/ppermute | solution.py:366
  103.4 12.8 %copy-start.1 = (bf16[512,7168]{1,0:T(8,128)(2,1)S(1)}, bf16[512,7168]{1,0:T(8,128)(2,1)}, u32[]{:S(2)}) copy-start(bf16[512,7168]{1,0:T(8,128)(2,1)} %pad_maximum_fusion.o_ref) | copy-start | bytes 22020100

commit v6 on v5

--- a/solution.py
+++ b/solution.py
@@ -339,6 +339,7 @@
             pltpu.SemaphoreType.DMA((4,)),
         ],
         compiler_params=pltpu.CompilerParams(vmem_limit_bytes=16 << 20),
+        cost_estimate=pl.CostEstimate(flops=2 << 30, transcendentals=0, bytes_accessed=4 << 20),
     )(*(in_hbm(a) for a in (q_compressed, w_q_nope, w_q_rope)))
     late_uk, narrow = lax.optimization_barrier((w_uk, narrow))
     own_q = [narrow]
@@ -361,11 +362,12 @@
         cost_estimate=pl.CostEstimate(flops=30 << 30, transcendentals=0, bytes_accessed=80 << 20),
     )(own_q, mate_q, code, w_uk, mate_uk)
     slabs_kv = jnp.swapaxes(kv_cache.reshape(kv_cache.shape[2:]), 1, 2)
-    late_uv, wide = lax.optimization_barrier((w_uv, wide))
-    late_o, count = lax.optimization_barrier((w_o, count))
+    count, wide = lax.optimization_barrier((count, wide))
+    arrived = exchange(wide, ("z", "x"), chips)
+    partials = attend(count, arrived, slabs_kv)
+    late_o, late_uv, partials = lax.optimization_barrier((w_o, w_uv, partials))
+    mate_o = lax.ppermute(late_o, "core", swap)
     mate_uv = lax.ppermute(late_uv, "core", swap)
-    mate_o = lax.ppermute(late_o, "core", swap)
-    arrived = exchange(wide, ("z", "x"), chips)
     draft_hv, draft_log = call(
         draft_kernel,
         (
@@ -375,7 +377,6 @@
         (core_id, own_q, mate_q, w_uk, mate_uk, w_uv, mate_uv, draft_kv),
         [SMEM] + [VMEM] * 7,
     )
-    partials = attend(count, arrived, slabs_kv)
     back = exchange(partials, ("z", "x"), chips)
     both_o = jnp.concatenate([w_o, mate_o], axis=0)
     back, draft_hv, draft_log, both_o = lax.optimization_barrier((back, draft_hv, draft_log, both_o))

time: 141 us -> 138 us (0.979)
  waiting for transfers between devices: 24.1 us -> 22.1 us
    ppermute x1, waiting for transfers between devices: 5.36 us -> 1.42 us  [shards(): mate_q = lax.ppermute(own_q, 'core', swap)]
    all_to_all x1, waiting for transfers between devices: 17.5 us -> 18.9 us  [exchange(): return lax.all_to_all(blocks, axes, 0, 0, tiled=True).reshape(array.shape)]
  transfers between devices with their start and end apart: 8 -> 8, of which waited for: 4 -> 4; matrix products, arithmetic and copies ran while one was open for 7% -> 6% of each run, Pallas kernels for 8% -> 2%
where the time goes in v6:
time: 138 us
  blocking collectives  77.5 us (56%)
  waiting for transfers between devices  22.1 us (16%)
  Pallas kernels  17.7 us (13%)
  starting transfers between devices  11.4 us (8%)
  other arithmetic  7.38 us (5%)
  local copies, waits for them, and re-layouts  1.59 us (1%)
    all_to_all x2, blocking collectives, exchange(): return lax.all_to_all(blocks, axes, 0, 0, tiled=True).reshape(array.shape)  55.4 us
    all_to_all x1, blocking collectives, shards(): lax.all_to_all(sums.reshape(chips, 8, -1), ('z', 'x'), 0, 0, tiled=True)  22.1 us
    all_to_all x1, waiting for transfers between devices, exchange(): return lax.all_to_all(blocks, axes, 0, 0, tiled=True).reshape(array.shape)  18.9 us
    pallas_call x1, Pallas kernels, attend(): pl.pallas_call(attend_kernel, out_shape=jax.ShapeDtypeStruct((rows, PART)...  7.88 us
    pallas_call x4, Pallas kernels, call(): pl.pallas_call(kernel, out_shape=outs, in_specs=specs, out_specs=jax.tree...  6.86 us
    concatenate x1, other arithmetic, shards(): both_o = jnp.concatenate([w_o, mate_o], axis=0)  6.58 us
    ppermute x3, starting transfers between devices, shards(): lax.ppermute(narrow, 'group', [(i, (i + k) % groups) for i in range(group...  5.9 us
    all_to_all x1, starting transfers between devices, exchange(): return lax.all_to_all(blocks, axes, 0, 0, tiled=True).reshape(array.shape)  4.87 us
  transfers between devices with their start and end apart: 8, of which 4 were waited for; matrix products, arithmetic and copies ran while one was open for 6% of the time, Pallas kernels for 2%

profile of v6, /device:TPU:32, one launch (start us, length us, event | category | flops | bytes accessed | tf_op | source)
XLA Modules:
  0.0 137.9 jit_solution(15591913524784903671)
XLA Ops:
  0.0 1.7 %shard_map.109 = bf16[64,384]{1,0:T(8,128)(2,1)S(1)} custom-call(bf16[64,1536]{1,0:T(8,128)(2,1)} %q_hbm.1, bf16[1536,256]{1,0:T(8,128)(2,1)} %wn_hbm.1, bf16[1536,128]{1,0:T(8,128)(2,1)} %wr_hbm.1), custom_call_target="tpu_custom_call" | custom-call | flops 2147483648 | bytes 4194304 | tf_op jit(solution)/shard_map/pallas_call | solution.py:332
  1.7 1.7 %collective-permute-start = (bf16[64,384]{1,0:T(8,128)(2,1)S(1)}, bf16[64,384]{1,0:T(8,128)(2,1)S(1)}, u32[]{:S(2)}, u32[]{:S(2)}) collective-permute-start(bf16[64,384]{1,0:T(8,128)(2,1)S(1)} %shard_map.109), channel_id=1, source_target_pairs={{0,64},{64,128},{128,192},{192,0},{1,65},{65,129},{129,193},{193,1... | collective-permute-start | bytes 147464 | tf_op jit(solution)/shard_map/ppermute | solution.py:347
  3.3 2.9 %collective-permute-start.1 = (bf16[64,384]{1,0:T(8,128)(2,1)S(1)}, bf16[64,384]{1,0:T(8,128)(2,1)S(1)}, u32[]{:S(2)}, u32[]{:S(2)}) collective-permute-start(bf16[64,384]{1,0:T(8,128)(2,1)S(1)} %shard_map.109), channel_id=1, source_target_pairs={{0,128},{64,192},{128,0},{192,64},{1,129},{65,193},{129,1},{193,65... | collective-permute-start | bytes 147464 | tf_op jit(solution)/shard_map/ppermute | solution.py:347
  6.2 1.3 collective-permute-start.2
  7.9 0.7 constant_dynamic-slice_fusion.2
  8.9 0.2 fusion
  9.1 0.2 fusion.2
  9.6 0.7 collective-permute-done.2
  10.5 1.4 %collective-permute-done.3.mate_q = bf16[256,384]{1,0:T(8,128)(2,1)S(1)} collective-permute-done((bf16[256,384]{1,0:T(8,128)(2,1)S(1)}, bf16[256,384]{1,0:T(8,128)(2,1)S(1)}, u32[]{:S(2)}, u32[]{:S(2)}) %collective-permute-start.3) | collective-permute-done | bytes 196640 | tf_op jit(solution)/shard_map/ppermute | solution.py:349
  11.9 1.3 shard_map.110
  13.2 43.4 %all_to_all.20 = bf16[32,8,2304]{2,1,0:T(8,128)(2,1)S(1)} all-to-all(bf16[32,8,2304]{2,1,0:T(8,128)(2,1)S(1)} %bitcast.32), channel_id=1, replica_groups=mesh['group'=4,'z'=8,'x'=4,'core'=2] {'z','x'}, dimensions={0} | all-to-all | bytes 2359296 | tf_op jit(solution)/shard_map/all_to_all | solution.py:285
  56.6 7.9 %shard_map.111 = bf16[256,2176]{1,0:T(8,128)(2,1)} custom-call(s32[2]{0:T(128)S(1)} %compare_select_fusion.2.count_ref, bf16[256,2304]{1,0:T(8,128)(2,1)S(1)} %bitcast.29, bf16[2,576,2048]{2,1,0:T(8,128)(2,1)S(1)} %bitcast.28), custom_call_target="tpu_custom_call" | custom-call | tf_op jit(solution)/shard_map/pallas_call | solution.py:195
  64.6 4.9 %all-to-all-start.1 = ((bf16[32,8,2176]{2,1,0:T(8,128)(2,1)}), bf16[32,8,2176]{2,1,0:T(8,128)(2,1)S(1)}, u32[]{:S(2)}, u32[]{:S(2)}) async-start(bf16[32,8,2176]{2,1,0:T(8,128)(2,1)} %bitcast.9), calls=%async_computation.1 | async-start | bytes 2228224 | tf_op jit(solution)/shard_map/all_to_all | solution.py:285
  69.6 0.5 collective-permute-start.5
  70.2 0.2 select_n.69.code_ref
  70.4 1.0 collective-permute-done.5.mate_uv.mate_ref
  71.4 2.2 %shard_map.112 = (f32[32,512]{1,0:T(8,128)S(1)}, f32[32,128]{1,0:T(8,128)S(1)}) custom-call(s32[1]{0:T(128)} %bitcast.core_ref, bf16[256,384]{1,0:T(8,128)(2,1)S(1)} %constant_dynamic-update-slice_fusion.own_q, bf16[256,384]{1,0:T(8,128)(2,1)S(1)} %collective-permute-done.3.mate_q, bf16[2,128,512]{2,1,0:T(8,128)(2,1)S(1)} %copy-done.3, ...), custom_call_target="tpu_custom_call" | custom-call | tf_op jit(solution)/shard_map/pallas_call | solution.py:45
  73.6 6.6 %pad_maximum_fusion.o_ref = bf16[512,7168]{1,0:T(8,128)(2,1)} fusion(bf16[256,7168]{1,0:T(8,128)(2,1)} %collective-permute-done.6, bf16[256,7168]{1,0:T(8,128)(2,1)} %param.16), kind=kLoop, calls=%fused_computation | loop fusion | flops 14680064 | bytes 14680064 | tf_op jit(solution)/shard_map/concatenate | solution.py:381
  80.1 18.9 %all-to-all-done.1 = bf16[32,8,2176]{2,1,0:T(8,128)(2,1)S(1)} async-done(((bf16[32,8,2176]{2,1,0:T(8,128)(2,1)}), bf16[32,8,2176]{2,1,0:T(8,128)(2,1)S(1)}, u32[]{:S(2)}, u32[]{:S(2)}) %all-to-all-start.1) | async-done | bytes 1114144 | tf_op jit(solution)/shard_map/all_to_all | solution.py:285
  99.1 2.0 %shard_map.113 = bf16[256,640]{1,0:T(8,128)(2,1)S(1)} custom-call(s32[1]{0:T(128)} %bitcast.core_ref, bf16[256,2176]{1,0:T(8,128)(2,1)S(1)} %bitcast.33, s32[4,256]{1,0:T(4,128)S(1)} %select_n.69.code_ref, bf16[2,512,128]{2,1,0:T(8,128)(2,1)S(1)} %copy-done.4, bf16[2,512,128]{2,1,0:T(8,128)(2,1)S(1)} %collective-permute-done.5.mate_uv.mate_ref), custom_call_target="tpu_custom_call" | custom-call | flops 3221225472 | bytes 8388608 | tf_op jit(solution)/shard_map/pallas_call | solution.py:45
  101.1 12.0 %all_to_all.21 = bf16[8,32,640]{2,1,0:T(8,128)(2,1)S(1)} all-to-all(bf16[8,32,640]{2,1,0:T(8,128)(2,1)S(1)} %bitcast.34), channel_id=1, replica_groups=mesh['group'=4,'z'=8,'x'=4,'core'=2] {'group','core'}, dimensions={0} | all-to-all | bytes 655360 | tf_op jit(solution)/shard_map/all_to_all | solution.py:285
  113.1 2.0 %shard_map.114 = bf16[32,7168]{1,0:T(8,128)(2,1)S(1)} custom-call(s32[1]{0:T(128)} %bitcast.core_ref, bf16[256,640]{1,0:T(8,128)(2,1)S(1)} %bitcast.31, f32[32,512]{1,0:T(8,128)S(1)} %get-tuple-element.28.hv_ref, f32[32,128]{1,0:T(8,128)S(1)} %get-tuple-element.29.log_ref, bf16[512,7168]{1,0:T(8,128)(2,1)S(1)} %copy-done.1), custom_call_target="tpu_custom_call" | custom-call | tf_op jit(solution)/shard_map/pallas_call | solution.py:45
  115.1 22.1 %all_to_all.22.tiles_ref = bf16[32,8,896]{2,1,0:T(8,128)(2,1)S(1)} all-to-all(bf16[32,8,896]{2,1,0:T(8,128)(2,1)S(1)} %bitcast.35), channel_id=1, replica_groups=mesh['group'=4,'z'=8,'x'=4,'core'=2] {'z','x'}, dimensions={0} | all-to-all | bytes 917504 | tf_op jit(solution)/shard_map/all_to_all | solution.py:398
  137.2 0.7 shard_map.115
  (43 shorter events, 1.3 us)
Async XLA Ops:
  0.0 7.6 %copy-start = (s32[4,64,2]{1,2,0:T(2,128)S(1)}, s32[4,64,2]{1,2,0:T(2,128)}, u32[]{:S(2)}) copy-start(s32[4,64,2]{1,2,0:T(2,128)} %param.20) | copy-start | bytes 6148
  0.0 7.6 %copy-start.3 = (bf16[2,128,512]{2,1,0:T(8,128)(2,1)S(1)}, bf16[2,128,512]{2,1,0:T(8,128)(2,1)}, u32[]{:S(2)}) copy-start(bf16[2,128,512]{2,1,0:T(8,128)(2,1)} %own_uk.1) | copy-start | bytes 786436
  0.0 9.1 %copy-start.6 = (s32[64]{0:T(128)S(1)}, s32[64]{0:T(128)}, u32[]{:S(2)}) copy-start(s32[64]{0:T(128)} %param.19) | copy-start | bytes 772
  1.7 7.9 %collective-permute-start = (bf16[64,384]{1,0:T(8,128)(2,1)S(1)}, bf16[64,384]{1,0:T(8,128)(2,1)S(1)}, u32[]{:S(2)}, u32[]{:S(2)}) collective-permute-start(bf16[64,384]{1,0:T(8,128)(2,1)S(1)} %shard_map.109), channel_id=1, source_target_pairs={{0,64},{64,128},{128,192},{192,0},{1,65},{65,129},{129,193},{193,1... | collective-permute-start | bytes 147464 | tf_op jit(solution)/shard_map/ppermute | solution.py:347
  3.3 6.2 %collective-permute-start.1 = (bf16[64,384]{1,0:T(8,128)(2,1)S(1)}, bf16[64,384]{1,0:T(8,128)(2,1)S(1)}, u32[]{:S(2)}, u32[]{:S(2)}) collective-permute-start(bf16[64,384]{1,0:T(8,128)(2,1)S(1)} %shard_map.109), channel_id=1, source_target_pairs={{0,128},{64,192},{128,0},{192,64},{1,129},{65,193},{129,1},{193,65... | collective-permute-start | bytes 147464 | tf_op jit(solution)/shard_map/ppermute | solution.py:347
  6.2 4.1 %collective-permute-start.2 = (bf16[64,384]{1,0:T(8,128)(2,1)S(1)}, bf16[64,384]{1,0:T(8,128)(2,1)S(1)}, u32[]{:S(2)}, u32[]{:S(2)}) collective-permute-start(bf16[64,384]{1,0:T(8,128)(2,1)S(1)} %shard_map.109), channel_id=1, source_target_pairs={{0,192},{64,0},{128,64},{192,128},{1,193},{65,1},{129,65},{193,129... | collective-permute-start | bytes 147464 | tf_op jit(solution)/shard_map/ppermute | solution.py:347
  7.6 4.3 %collective-permute-start.4 = (bf16[2,128,512]{2,1,0:T(8,128)(2,1)S(1)}, bf16[2,128,512]{2,1,0:T(8,128)(2,1)S(1)}, u32[]{:S(2)}, u32[]{:S(2)}) collective-permute-start(bf16[2,128,512]{2,1,0:T(8,128)(2,1)S(1)} %copy-done.3), channel_id=1, source_target_pairs={{0,1},{1,0},{2,3},{3,2},{4,5},{5,4},{6,7},{7,6},{8,9},{9,8},{10,11... | collective-permute-start | bytes 786440 | tf_op jit(solution)/shard_map/ppermute | solution.py:350
  10.3 1.5 %collective-permute-start.3 = (bf16[256,384]{1,0:T(8,128)(2,1)S(1)}, bf16[256,384]{1,0:T(8,128)(2,1)S(1)}, u32[]{:S(2)}, u32[]{:S(2)}) collective-permute-start(bf16[256,384]{1,0:T(8,128)(2,1)S(1)} %constant_dynamic-update-slice_fusion.own_q), channel_id=1, source_target_pairs={{0,1},{1,0},{2,3},{3,2},{4,5},{5,4},{6,7},{7,6},{8,9},{9,8},{10,11... | collective-permute-start | bytes 589832 | tf_op jit(solution)/shard_map/ppermute | solution.py:349
  11.9 44.7 %copy-start.2 = (bf16[1,1,2,2048,576]{3,4,2,1,0:T(8,128)(2,1)S(1)}, bf16[1,1,2,2048,576]{3,4,2,1,0:T(8,128)(2,1)}, u32[]{:S(2)}) copy-start(bf16[1,1,2,2048,576]{3,4,2,1,0:T(8,128)(2,1)} %param.17) | copy-start | bytes 14155780
  56.6 13.0 %copy-start.4 = (bf16[2,512,128]{2,1,0:T(8,128)(2,1)S(1)}, bf16[2,512,128]{2,1,0:T(8,128)(2,1)}, u32[]{:S(2)}) copy-start(bf16[2,512,128]{2,1,0:T(8,128)(2,1)} %own_ref.3) | copy-start | bytes 786436
  56.6 14.8 %copy-start.5 = (bf16[64,576]{1,0:T(8,128)(2,1)S(1)}, bf16[64,576]{1,0:T(8,128)(2,1)}, u32[]{:S(2)}) copy-start(bf16[64,576]{1,0:T(8,128)(2,1)} %kv_ref.1) | copy-start | bytes 221188
  64.5 9.1 %collective-permute-start.6 = (bf16[256,7168]{1,0:T(8,128)(2,1)}, bf16[256,7168]{1,0:T(8,128)(2,1)}, u32[]{:S(2)}, u32[]{:S(2)}) collective-permute-start(bf16[256,7168]{1,0:T(8,128)(2,1)} %param.16), channel_id=1, source_target_pairs={{0,1},{1,0},{2,3},{3,2},{4,5},{5,4},{6,7},{7,6},{8,9},{9,8},{10,11... | collective-permute-start | bytes 11010056 | tf_op jit(solution)/shard_map/ppermute | solution.py:369
  64.6 34.5 %all-to-all-start.1 = ((bf16[32,8,2176]{2,1,0:T(8,128)(2,1)}), bf16[32,8,2176]{2,1,0:T(8,128)(2,1)S(1)}, u32[]{:S(2)}, u32[]{:S(2)}) async-start(bf16[32,8,2176]{2,1,0:T(8,128)(2,1)} %bitcast.9), calls=%async_computation.1 | async-start | bytes 2228224 | tf_op jit(solution)/shard_map/all_to_all | solution.py:285
  69.6 1.8 %collective-permute-start.5 = (bf16[2,512,128]{2,1,0:T(8,128)(2,1)S(1)}, bf16[2,512,128]{2,1,0:T(8,128)(2,1)S(1)}, u32[]{:S(2)}, u32[]{:S(2)}) collective-permute-start(bf16[2,512,128]{2,1,0:T(8,128)(2,1)S(1)} %copy-done.4), channel_id=1, source_target_pairs={{0,1},{1,0},{2,3},{3,2},{4,5},{5,4},{6,7},{7,6},{8,9},{9,8},{10,11... | collective-permute-start | bytes 786440 | tf_op jit(solution)/shard_map/ppermute | solution.py:370
  99.1 14.0 %copy-start.1 = (bf16[512,7168]{1,0:T(8,128)(2,1)S(1)}, bf16[512,7168]{1,0:T(8,128)(2,1)}, u32[]{:S(2)}) copy-start(bf16[512,7168]{1,0:T(8,128)(2,1)} %pad_maximum_fusion.o_ref) | copy-start | bytes 22020100

commit v7 on v6

--- a/solution.py
+++ b/solution.py
@@ -208,9 +208,10 @@
     )(count, x, kv)
 
 
-def merge_kernel(core_ref, y_ref, code_ref, own_ref, mate_ref, out_ref):
+def merge_kernel(core_ref, y_ref, code_ref, own_ref, mate_ref, own_out, mate_out):
     core = core_ref[0]
-    rows, cols = out_ref.shape[0], y_ref.shape[0]
+    half = own_out.shape[0]
+    rows, cols = 2 * half, y_ref.shape[0]
     base = SLOTS * 2 * LATENT
     logs = jnp.transpose(y_ref[:, base:].astype(F32))
     row = lax.broadcasted_iota(jnp.int32, (rows, cols), 0)
@@ -235,19 +236,24 @@
             mixture = (mixture / total).astype(BF16)
             head = hp * 2 + par
             values = dot(mixture, jnp.where(core == hp, own_ref[par], mate_ref[par]))
-            out_ref[:, head * VDIM : (head + 1) * VDIM] = values.astype(BF16)
+            own_out[:, head * VDIM : (head + 1) * VDIM] = values[:half].astype(BF16)
+            mate_out[:, head * VDIM : (head + 1) * VDIM] = values[half:].astype(BF16)
             tile = put_terms(tile, peak + jnp.log(total), head * 3)
-    out_ref[:, 4 * VDIM :] = tile.astype(BF16)
-
-
-def finish_kernel(core_ref, z_ref, hv_ref, log_ref, o_ref, out_ref):
+    own_out[:, 4 * VDIM :] = tile[:half].astype(BF16)
+    mate_out[:, 4 * VDIM :] = tile[half:].astype(BF16)
+
+
+def finish_kernel(core_ref, own_ref, mate_ref, *refs):
+    *others, hv_ref, log_ref, o_ref, out_ref = refs
     half = hv_ref.shape[0]
+    blocks = [(own_ref, slice(0, half)), (mate_ref, slice(0, half))]
+    for other in others:
+        blocks += [(other, slice(0, half)), (other, slice(half, 2 * half))]
     values = []
     for head in range(4):
         logs = [log_ref[:, head : head + 1]]
         parts = [hv_ref[:, head * VDIM : (head + 1) * VDIM]]
-        for block in range(z_ref.shape[0] // half):
-            at = slice(block * half, (block + 1) * half)
+        for z_ref, at in blocks:
             terms = z_ref[at, 4 * VDIM :].astype(F32)
             first = head * 3
             logs.append(
@@ -314,8 +320,10 @@
     code = (shift * TOK_GRP + (held & 15) * DRAFT).T[:, :, None]
     code = code + ((hp != core) * (groups * TOK_GRP) + draft).reshape(-1)
     code = jnp.where(filled, code, -1).reshape(-1, 1)
-    row = ((held >> 4) * TOK_GRP + (held & 15) * 2).T[:, :, None, None]
-    row = row + (draft & 1) * (TOK_GRP // 2) + (draft >> 1)
+    quarter = TOK_GRP // 2
+    ahead = ((held >> 4) - group) & (groups - 1)
+    row = (ahead * quarter + (held & 15) * 2).T[:, :, None, None]
+    row = row + ((draft & 1) != core) * (groups * quarter) + (draft >> 1)
     row = jnp.where(filled[..., None], row, -1)
     row = jnp.where(hp == hp.reshape(2, 1, 1, 1, 1), row, -1).reshape(2 * SLOTS, -1)
 
@@ -328,7 +336,6 @@
     length = jnp.sum(jnp.where(is_mine, context_length, 0), axis=1)
     count = jnp.where(mine >= 0, length - slabs * kv_cache.shape[3], 0).astype(jnp.int32)
 
-    copies = groups * cores
     narrow = pl.pallas_call(
         project_kernel,
         out_shape=jax.ShapeDtypeStruct((TOK_GRP, NARROW), BF16),
@@ -355,7 +362,7 @@
         grid=(SLOTS,),
         in_specs=[VMEM, VMEM, pl.BlockSpec((rows, 1), lambda k: (k, 0)), VMEM, VMEM],
         out_specs=pl.BlockSpec((rows, WIDE), lambda k: (0, k)),
-        scratch_shapes=[pltpu.VMEM((copies * TOK_GRP, 5 * NOPE), BF16)],
+        scratch_shapes=[pltpu.VMEM((groups * cores * TOK_GRP, 5 * NOPE), BF16)],
         compiler_params=pltpu.CompilerParams(
             dimension_semantics=("arbitrary",), vmem_limit_bytes=16 << 20
         ),
@@ -380,20 +387,26 @@
     back = exchange(partials, ("z", "x"), chips)
     both_o = jnp.concatenate([w_o, mate_o], axis=0)
     back, draft_hv, draft_log, both_o = lax.optimization_barrier((back, draft_hv, draft_log, both_o))
-    merged = call(
+    part = jax.ShapeDtypeStruct((groups * quarter, 4 * VDIM + 128), BF16)
+    own_part, mate_part = call(
         merge_kernel,
-        jax.ShapeDtypeStruct((groups * TOK_GRP, 4 * VDIM + 128), BF16),
+        (part, part),
         (core_id, back, row, w_uv, mate_uv),
         [SMEM] + [VMEM] * 4,
         vmem=16,
         cost=pl.CostEstimate(flops=3 << 30, transcendentals=1 << 19, bytes_accessed=8 << 20),
     )
-    home = exchange(merged, ("group", "core"), copies)
+    mate_part = lax.ppermute(mate_part, "core", swap)
+    others = []
+    for k in range(1, groups):
+        at = slice(k * quarter, (k + 1) * quarter)
+        pair = jnp.concatenate([own_part[at], mate_part[at]], axis=0)
+        others.append(lax.ppermute(pair, "group", [(i, (i + k) % groups) for i in range(groups)]))
     sums = call(
         finish_kernel,
         jax.ShapeDtypeStruct((chips, w_o.shape[1]), BF16),
-        (core_id, home, draft_hv, draft_log, both_o),
-        [SMEM] + [VMEM] * 4,
+        (core_id, own_part, mate_part, *others, draft_hv, draft_log, both_o),
+        [SMEM] + [VMEM] * (groups + 4),
     )
     tiles = lax.all_to_all(sums.reshape(chips, 8, -1), ("z", "x"), 0, 0, tiled=True)
     return call(

time: 138 us -> 136 us (0.986)
  blocking collectives: 77.5 us -> 64.7 us
  waiting for transfers between devices: 22.1 us -> 27.7 us
  starting transfers between devices: 11.4 us -> 15.9 us
    all_to_all x2 -> x1, blocking collectives: 55.4 us -> 43.4 us  [exchange(): return lax.all_to_all(blocks, axes, 0, 0, tiled=True).reshape(array.shape)]
    ppermute x0 -> x4, waiting for transfers between devices: none -> 5.66 us  [the longest x3 4.3 us: shards(): lax.ppermute(pair, 'group', [(i, (i + k) % groups) for i in range(groups)])]
    ppermute x0 -> x4, starting transfers between devices: none -> 4.49 us  [the longest x3 4.4 us: shards(): lax.ppermute(pair, 'group', [(i, (i + k) % groups) for i in range(groups)])]
  transfers between devices with their start and end apart: 8 -> 12, of which waited for: 4 -> 8; matrix products, arithmetic and copies ran while one was open for 6% -> 7% of each run, Pallas kernels for 2% -> 2%
where the time goes in v7:
time: 136 us; the launch traced here: 135 us
  blocking collectives  64.7 us (48%)
  waiting for transfers between devices  27.7 us (20%)
  Pallas kernels  17.7 us (13%)
  starting transfers between devices  15.9 us (12%)
  other arithmetic  7.4 us (5%)
  local copies, waits for them, and re-layouts  1.62 us (1%)
    all_to_all x1, blocking collectives, exchange(): return lax.all_to_all(blocks, axes, 0, 0, tiled=True).reshape(array.shape)  43.4 us
    all_to_all x1, blocking collectives, shards(): lax.all_to_all(sums.reshape(chips, 8, -1), ('z', 'x'), 0, 0, tiled=True)  21.3 us
    all_to_all x1, waiting for transfers between devices, exchange(): return lax.all_to_all(blocks, axes, 0, 0, tiled=True).reshape(array.shape)  18.9 us
    pallas_call x1, Pallas kernels, attend(): pl.pallas_call(attend_kernel, out_shape=jax.ShapeDtypeStruct((rows, PART)...  7.83 us
    pallas_call x4, Pallas kernels, call(): pl.pallas_call(kernel, out_shape=outs, in_specs=specs, out_specs=jax.tree...  6.87 us
    concatenate x1, other arithmetic, shards(): both_o = jnp.concatenate([w_o, mate_o], axis=0)  6.58 us
    ppermute x3, starting transfers between devices, shards(): lax.ppermute(narrow, 'group', [(i, (i + k) % groups) for i in range(group...  5.9 us
    all_to_all x1, starting transfers between devices, exchange(): return lax.all_to_all(blocks, axes, 0, 0, tiled=True).reshape(array.shape)  4.87 us
  transfers between devices with their start and end apart: 12, of which 8 were waited for; matrix products, arithmetic and copies ran while one was open for 7% of the time, Pallas kernels for 2%

profile of v7, /device:TPU:32, one launch (start us, length us, event | category | flops | bytes accessed | tf_op | source)
XLA Modules:
  0.0 135.3 jit_solution(8875132613259998405)
XLA Ops:
  0.0 1.7 %shard_map.109 = bf16[64,384]{1,0:T(8,128)(2,1)S(1)} custom-call(bf16[64,1536]{1,0:T(8,128)(2,1)} %q_hbm.1, bf16[1536,256]{1,0:T(8,128)(2,1)} %wn_hbm.1, bf16[1536,128]{1,0:T(8,128)(2,1)} %wr_hbm.1), custom_call_target="tpu_custom_call" | custom-call | flops 2147483648 | bytes 4194304 | tf_op jit(solution)/shard_map/pallas_call | solution.py:339
  1.7 1.7 %collective-permute-start = (bf16[64,384]{1,0:T(8,128)(2,1)S(1)}, bf16[64,384]{1,0:T(8,128)(2,1)S(1)}, u32[]{:S(2)}, u32[]{:S(2)}) collective-permute-start(bf16[64,384]{1,0:T(8,128)(2,1)S(1)} %shard_map.109), channel_id=1, source_target_pairs={{0,64},{64,128},{128,192},{192,0},{1,65},{65,129},{129,193},{193,1... | collective-permute-start | bytes 147464 | tf_op jit(solution)/shard_map/ppermute | solution.py:354
  3.3 2.9 %collective-permute-start.1 = (bf16[64,384]{1,0:T(8,128)(2,1)S(1)}, bf16[64,384]{1,0:T(8,128)(2,1)S(1)}, u32[]{:S(2)}, u32[]{:S(2)}) collective-permute-start(bf16[64,384]{1,0:T(8,128)(2,1)S(1)} %shard_map.109), channel_id=1, source_target_pairs={{0,128},{64,192},{128,0},{192,64},{1,129},{65,193},{129,1},{193,65... | collective-permute-start | bytes 147464 | tf_op jit(solution)/shard_map/ppermute | solution.py:354
  6.2 1.3 collective-permute-start.2
  7.9 0.7 constant_dynamic-slice_fusion.2
  9.6 0.7 collective-permute-done.2
  10.5 1.4 %collective-permute-done.3.mate_q = bf16[256,384]{1,0:T(8,128)(2,1)S(1)} collective-permute-done((bf16[256,384]{1,0:T(8,128)(2,1)S(1)}, bf16[256,384]{1,0:T(8,128)(2,1)S(1)}, u32[]{:S(2)}, u32[]{:S(2)}) %collective-permute-start.3) | collective-permute-done | bytes 196640 | tf_op jit(solution)/shard_map/ppermute | solution.py:356
  11.9 1.3 shard_map.110
  13.2 43.4 %all_to_all.15 = bf16[32,8,2304]{2,1,0:T(8,128)(2,1)S(1)} all-to-all(bf16[32,8,2304]{2,1,0:T(8,128)(2,1)S(1)} %bitcast.29), channel_id=1, replica_groups=mesh['group'=4,'z'=8,'x'=4,'core'=2] {'z','x'}, dimensions={0} | all-to-all | bytes 2359296 | tf_op jit(solution)/shard_map/all_to_all | solution.py:291
  56.6 7.8 %shard_map.111 = bf16[256,2176]{1,0:T(8,128)(2,1)} custom-call(s32[2]{0:T(128)S(1)} %compare_select_fusion.3.count_ref, bf16[256,2304]{1,0:T(8,128)(2,1)S(1)} %bitcast.27, bf16[2,576,2048]{2,1,0:T(8,128)(2,1)S(1)} %bitcast.26), custom_call_target="tpu_custom_call" | custom-call | tf_op jit(solution)/shard_map/pallas_call | solution.py:195
  64.5 4.9 %all-to-all-start.1 = ((bf16[32,8,2176]{2,1,0:T(8,128)(2,1)}), bf16[32,8,2176]{2,1,0:T(8,128)(2,1)S(1)}, u32[]{:S(2)}, u32[]{:S(2)}) async-start(bf16[32,8,2176]{2,1,0:T(8,128)(2,1)} %bitcast.9), calls=%async_computation.1 | async-start | bytes 2228224 | tf_op jit(solution)/shard_map/all_to_all | solution.py:291
  69.5 0.5 collective-permute-start.5
  70.3 1.0 collective-permute-done.5.mate_uv.mate_ref
  71.3 2.2 %shard_map.112 = (f32[32,512]{1,0:T(8,128)S(1)}, f32[32,128]{1,0:T(8,128)S(1)}) custom-call(s32[1]{0:T(128)} %bitcast.core_ref, bf16[256,384]{1,0:T(8,128)(2,1)S(1)} %constant_dynamic-update-slice_fusion.own_q, bf16[256,384]{1,0:T(8,128)(2,1)S(1)} %collective-permute-done.3.mate_q, bf16[2,128,512]{2,1,0:T(8,128)(2,1)S(1)} %copy-done.3, ...), custom_call_target="tpu_custom_call" | custom-call | tf_op jit(solution)/shard_map/pallas_call | solution.py:45
  73.5 6.6 %pad_maximum_fusion.refs_5_ = bf16[512,7168]{1,0:T(8,128)(2,1)} fusion(bf16[256,7168]{1,0:T(8,128)(2,1)} %collective-permute-done.6, bf16[256,7168]{1,0:T(8,128)(2,1)} %param.16), kind=kLoop, calls=%fused_computation | loop fusion | flops 14680064 | bytes 14680064 | tf_op jit(solution)/shard_map/concatenate | solution.py:388
  80.1 18.9 %all-to-all-done.1 = bf16[32,8,2176]{2,1,0:T(8,128)(2,1)S(1)} async-done(((bf16[32,8,2176]{2,1,0:T(8,128)(2,1)}), bf16[32,8,2176]{2,1,0:T(8,128)(2,1)S(1)}, u32[]{:S(2)}, u32[]{:S(2)}) %all-to-all-start.1) | async-done | bytes 1114144 | tf_op jit(solution)/shard_map/all_to_all | solution.py:291
  99.0 2.0 %shard_map.113 = (bf16[128,640]{1,0:T(8,128)(2,1)S(1)}, bf16[128,640]{1,0:T(8,128)(2,1)S(1)}) custom-call(s32[1]{0:T(128)} %bitcast.core_ref, bf16[256,2176]{1,0:T(8,128)(2,1)S(1)} %bitcast.30, s32[4,256]{1,0:T(4,128)S(1)} %select_n.69.code_ref, bf16[2,512,128]{2,1,0:T(8,128)(2,1)S(1)} %copy-done.4, ...), custom_call_target="tpu_custom_call" | custom-call | flops 3221225472 | bytes 8388608 | tf_op jit(solution)/shard_map/pallas_call | solution.py:45
  101.1 1.4 %collective-permute-done.7.mate_ref = bf16[128,640]{1,0:T(8,128)(2,1)S(1)} collective-permute-done((bf16[128,640]{1,0:T(8,128)(2,1)S(1)}, bf16[128,640]{1,0:T(8,128)(2,1)S(1)}, u32[]{:S(2)}, u32[]{:S(2)}) %collective-permute-start.7) | collective-permute-done | bytes 163872 | tf_op jit(solution)/shard_map/ppermute | solution.py:399
  102.9 3.8 %collective-permute-start.9 = (bf16[64,640]{1,0:T(8,128)(2,1)S(1)}, bf16[64,640]{1,0:T(8,128)(2,1)S(1)}, u32[]{:S(2)}, u32[]{:S(2)}) collective-permute-start(bf16[64,640]{1,0:T(8,128)(2,1)S(1)} %pad_maximum_fusion.2), channel_id=1, source_target_pairs={{0,128},{64,192},{128,0},{192,64},{1,129},{65,193},{129,1},{193,65... | collective-permute-start | bytes 245768 | tf_op jit(solution)/shard_map/ppermute | solution.py:404
  106.9 1.4 %collective-permute-done.8.refs_0_ = bf16[64,640]{1,0:T(8,128)(2,1)S(1)} collective-permute-done((bf16[64,640]{1,0:T(8,128)(2,1)S(1)}, bf16[64,640]{1,0:T(8,128)(2,1)S(1)}, u32[]{:S(2)}, u32[]{:S(2)}) %collective-permute-start.8) | collective-permute-done | bytes 81952 | tf_op jit(solution)/shard_map/ppermute | solution.py:404
  108.3 2.5 %collective-permute-done.9.refs_1_ = bf16[64,640]{1,0:T(8,128)(2,1)S(1)} collective-permute-done((bf16[64,640]{1,0:T(8,128)(2,1)S(1)}, bf16[64,640]{1,0:T(8,128)(2,1)S(1)}, u32[]{:S(2)}, u32[]{:S(2)}) %collective-permute-start.9) | collective-permute-done | bytes 81952 | tf_op jit(solution)/shard_map/ppermute | solution.py:404
  111.2 2.0 %shard_map.114 = bf16[32,7168]{1,0:T(8,128)(2,1)S(1)} custom-call(s32[1]{0:T(128)} %bitcast.core_ref, bf16[128,640]{1,0:T(8,128)(2,1)S(1)} %get-tuple-element.30.own_ref, bf16[128,640]{1,0:T(8,128)(2,1)S(1)} %collective-permute-done.7.mate_ref, bf16[64,640]{1,0:T(8,128)(2,1)S(1)} %collective-permute-done.8.refs_0_, ...), custom_call_target="tpu_custom_call" | custom-call | tf_op jit(solution)/shard_map/pallas_call | solution.py:45
  113.3 21.3 %all_to_all.16.tiles_ref = bf16[32,8,896]{2,1,0:T(8,128)(2,1)S(1)} all-to-all(bf16[32,8,896]{2,1,0:T(8,128)(2,1)S(1)} %bitcast.31), channel_id=1, replica_groups=mesh['group'=4,'z'=8,'x'=4,'core'=2] {'z','x'}, dimensions={0} | all-to-all | bytes 917504 | tf_op jit(solution)/shard_map/all_to_all | solution.py:411
  134.7 0.7 shard_map.115
  (55 shorter events, 3.0 us)
Async XLA Ops:
  0.0 7.6 %copy-start = (s32[4,64,2]{1,2,0:T(2,128)S(1)}, s32[4,64,2]{1,2,0:T(2,128)}, u32[]{:S(2)}) copy-start(s32[4,64,2]{1,2,0:T(2,128)} %param.20) | copy-start | bytes 6148
  0.0 7.6 %copy-start.3 = (bf16[2,128,512]{2,1,0:T(8,128)(2,1)S(1)}, bf16[2,128,512]{2,1,0:T(8,128)(2,1)}, u32[]{:S(2)}) copy-start(bf16[2,128,512]{2,1,0:T(8,128)(2,1)} %own_uk.1) | copy-start | bytes 786436
  0.0 9.1 %copy-start.6 = (s32[64]{0:T(128)S(1)}, s32[64]{0:T(128)}, u32[]{:S(2)}) copy-start(s32[64]{0:T(128)} %param.19) | copy-start | bytes 772
  1.7 7.9 %collective-permute-start = (bf16[64,384]{1,0:T(8,128)(2,1)S(1)}, bf16[64,384]{1,0:T(8,128)(2,1)S(1)}, u32[]{:S(2)}, u32[]{:S(2)}) collective-permute-start(bf16[64,384]{1,0:T(8,128)(2,1)S(1)} %shard_map.109), channel_id=1, source_target_pairs={{0,64},{64,128},{128,192},{192,0},{1,65},{65,129},{129,193},{193,1... | collective-permute-start | bytes 147464 | tf_op jit(solution)/shard_map/ppermute | solution.py:354
  3.3 6.2 %collective-permute-start.1 = (bf16[64,384]{1,0:T(8,128)(2,1)S(1)}, bf16[64,384]{1,0:T(8,128)(2,1)S(1)}, u32[]{:S(2)}, u32[]{:S(2)}) collective-permute-start(bf16[64,384]{1,0:T(8,128)(2,1)S(1)} %shard_map.109), channel_id=1, source_target_pairs={{0,128},{64,192},{128,0},{192,64},{1,129},{65,193},{129,1},{193,65... | collective-permute-start | bytes 147464 | tf_op jit(solution)/shard_map/ppermute | solution.py:354
  6.2 4.1 %collective-permute-start.2 = (bf16[64,384]{1,0:T(8,128)(2,1)S(1)}, bf16[64,384]{1,0:T(8,128)(2,1)S(1)}, u32[]{:S(2)}, u32[]{:S(2)}) collective-permute-start(bf16[64,384]{1,0:T(8,128)(2,1)S(1)} %shard_map.109), channel_id=1, source_target_pairs={{0,192},{64,0},{128,64},{192,128},{1,193},{65,1},{129,65},{193,129... | collective-permute-start | bytes 147464 | tf_op jit(solution)/shard_map/ppermute | solution.py:354
  7.6 4.3 %collective-permute-start.4 = (bf16[2,128,512]{2,1,0:T(8,128)(2,1)S(1)}, bf16[2,128,512]{2,1,0:T(8,128)(2,1)S(1)}, u32[]{:S(2)}, u32[]{:S(2)}) collective-permute-start(bf16[2,128,512]{2,1,0:T(8,128)(2,1)S(1)} %copy-done.3), channel_id=1, source_target_pairs={{0,1},{1,0},{2,3},{3,2},{4,5},{5,4},{6,7},{7,6},{8,9},{9,8},{10,11... | collective-permute-start | bytes 786440 | tf_op jit(solution)/shard_map/ppermute | solution.py:357
  10.3 1.5 %collective-permute-start.3 = (bf16[256,384]{1,0:T(8,128)(2,1)S(1)}, bf16[256,384]{1,0:T(8,128)(2,1)S(1)}, u32[]{:S(2)}, u32[]{:S(2)}) collective-permute-start(bf16[256,384]{1,0:T(8,128)(2,1)S(1)} %constant_dynamic-update-slice_fusion.own_q), channel_id=1, source_target_pairs={{0,1},{1,0},{2,3},{3,2},{4,5},{5,4},{6,7},{7,6},{8,9},{9,8},{10,11... | collective-permute-start | bytes 589832 | tf_op jit(solution)/shard_map/ppermute | solution.py:356
  11.9 44.7 %copy-start.2 = (bf16[1,1,2,2048,576]{3,4,2,1,0:T(8,128)(2,1)S(1)}, bf16[1,1,2,2048,576]{3,4,2,1,0:T(8,128)(2,1)}, u32[]{:S(2)}) copy-start(bf16[1,1,2,2048,576]{3,4,2,1,0:T(8,128)(2,1)} %param.17) | copy-start | bytes 14155780
  56.6 12.9 %copy-start.4 = (bf16[2,512,128]{2,1,0:T(8,128)(2,1)S(1)}, bf16[2,512,128]{2,1,0:T(8,128)(2,1)}, u32[]{:S(2)}) copy-start(bf16[2,512,128]{2,1,0:T(8,128)(2,1)} %own_ref.3) | copy-start | bytes 786436
  56.6 14.7 %copy-start.5 = (bf16[64,576]{1,0:T(8,128)(2,1)S(1)}, bf16[64,576]{1,0:T(8,128)(2,1)}, u32[]{:S(2)}) copy-start(bf16[64,576]{1,0:T(8,128)(2,1)} %kv_ref.1) | copy-start | bytes 221188
  64.4 9.1 %collective-permute-start.6 = (bf16[256,7168]{1,0:T(8,128)(2,1)}, bf16[256,7168]{1,0:T(8,128)(2,1)}, u32[]{:S(2)}, u32[]{:S(2)}) collective-permute-start(bf16[256,7168]{1,0:T(8,128)(2,1)} %param.16), channel_id=1, source_target_pairs={{0,1},{1,0},{2,3},{3,2},{4,5},{5,4},{6,7},{7,6},{8,9},{9,8},{10,11... | collective-permute-start | bytes 11010056 | tf_op jit(solution)/shard_map/ppermute | solution.py:376
  64.5 34.5 %all-to-all-start.1 = ((bf16[32,8,2176]{2,1,0:T(8,128)(2,1)}), bf16[32,8,2176]{2,1,0:T(8,128)(2,1)S(1)}, u32[]{:S(2)}, u32[]{:S(2)}) async-start(bf16[32,8,2176]{2,1,0:T(8,128)(2,1)} %bitcast.9), calls=%async_computation.1 | async-start | bytes 2228224 | tf_op jit(solution)/shard_map/all_to_all | solution.py:291
  69.5 1.8 %collective-permute-start.5 = (bf16[2,512,128]{2,1,0:T(8,128)(2,1)S(1)}, bf16[2,512,128]{2,1,0:T(8,128)(2,1)S(1)}, u32[]{:S(2)}, u32[]{:S(2)}) collective-permute-start(bf16[2,512,128]{2,1,0:T(8,128)(2,1)S(1)} %copy-done.4), channel_id=1, source_target_pairs={{0,1},{1,0},{2,3},{3,2},{4,5},{5,4},{6,7},{7,6},{8,9},{9,8},{10,11... | collective-permute-start | bytes 786440 | tf_op jit(solution)/shard_map/ppermute | solution.py:377
  99.0 12.2 %copy-start.1 = (bf16[512,7168]{1,0:T(8,128)(2,1)S(1)}, bf16[512,7168]{1,0:T(8,128)(2,1)}, u32[]{:S(2)}) copy-start(bf16[512,7168]{1,0:T(8,128)(2,1)} %pad_maximum_fusion.refs_5_) | copy-start | bytes 22020100
  101.0 1.5 %collective-permute-start.7 = (bf16[128,640]{1,0:T(8,128)(2,1)S(1)}, bf16[128,640]{1,0:T(8,128)(2,1)S(1)}, u32[]{:S(2)}, u32[]{:S(2)}) collective-permute-start(bf16[128,640]{1,0:T(8,128)(2,1)S(1)} %get-tuple-element.31), channel_id=1, source_target_pairs={{0,1},{1,0},{2,3},{3,2},{4,5},{5,4},{6,7},{7,6},{8,9},{9,8},{10,11... | collective-permute-start | bytes 491528 | tf_op jit(solution)/shard_map/ppermute | solution.py:399
  102.5 5.8 %collective-permute-start.8 = (bf16[64,640]{1,0:T(8,128)(2,1)S(1)}, bf16[64,640]{1,0:T(8,128)(2,1)S(1)}, u32[]{:S(2)}, u32[]{:S(2)}) collective-permute-start(bf16[64,640]{1,0:T(8,128)(2,1)S(1)} %pad_maximum_fusion.1), channel_id=1, source_target_pairs={{0,64},{64,128},{128,192},{192,0},{1,65},{65,129},{129,193},{193,1... | collective-permute-start | bytes 245768 | tf_op jit(solution)/shard_map/ppermute | solution.py:404
  102.9 7.9 %collective-permute-start.9 = (bf16[64,640]{1,0:T(8,128)(2,1)S(1)}, bf16[64,640]{1,0:T(8,128)(2,1)S(1)}, u32[]{:S(2)}, u32[]{:S(2)}) collective-permute-start(bf16[64,640]{1,0:T(8,128)(2,1)S(1)} %pad_maximum_fusion.2), channel_id=1, source_target_pairs={{0,128},{64,192},{128,0},{192,64},{1,129},{65,193},{129,1},{193,65... | collective-permute-start | bytes 245768 | tf_op jit(solution)/shard_map/ppermute | solution.py:404
  106.7 4.5 %collective-permute-start.10 = (bf16[64,640]{1,0:T(8,128)(2,1)S(1)}, bf16[64,640]{1,0:T(8,128)(2,1)S(1)}, u32[]{:S(2)}, u32[]{:S(2)}) collective-permute-start(bf16[64,640]{1,0:T(8,128)(2,1)S(1)} %pad_maximum_fusion.3), channel_id=1, source_target_pairs={{0,192},{64,0},{128,64},{192,128},{1,193},{65,1},{129,65},{193,129... | collective-permute-start | bytes 245768 | tf_op jit(solution)/shard_map/ppermute | solution.py:404

commit v8 on v7

--- a/solution.py
+++ b/solution.py
@@ -348,13 +348,14 @@
         compiler_params=pltpu.CompilerParams(vmem_limit_bytes=16 << 20),
         cost_estimate=pl.CostEstimate(flops=2 << 30, transcendentals=0, bytes_accessed=4 << 20),
     )(*(in_hbm(a) for a in (q_compressed, w_q_nope, w_q_rope)))
-    late_uk, narrow = lax.optimization_barrier((w_uk, narrow))
     own_q = [narrow]
     for k in range(1, groups):
         own_q.append(lax.ppermute(narrow, "group", [(i, (i + k) % groups) for i in range(groups)]))
     own_q = jnp.concatenate(own_q, axis=0)
     mate_q = lax.ppermute(own_q, "core", swap)
-    mate_uk = lax.ppermute(late_uk, "core", swap)
+    late_o, mate_q = lax.optimization_barrier((w_o, mate_q))
+    mate_o = lax.ppermute(late_o, "core", swap)
+    mate_uk = lax.ppermute(w_uk, "core", swap)
     rows = chips * cores * DRAFT
     wide = pl.pallas_call(
         spread_kernel,
@@ -372,8 +373,7 @@
     count, wide = lax.optimization_barrier((count, wide))
     arrived = exchange(wide, ("z", "x"), chips)
     partials = attend(count, arrived, slabs_kv)
-    late_o, late_uv, partials = lax.optimization_barrier((w_o, w_uv, partials))
-    mate_o = lax.ppermute(late_o, "core", swap)
+    late_uv, partials = lax.optimization_barrier((w_uv, partials))
     mate_uv = lax.ppermute(late_uv, "core", swap)
     draft_hv, draft_log = call(
         draft_kernel,

time: 136 us -> 137 us (level)
    ppermute x3, waiting for transfers between devices: 4.3 us -> 6.32 us  [shards(): lax.ppermute(pair, 'group', [(i, (i + k) % groups) for i in range(groups)])]
    all_to_all x1, waiting for transfers between devices: 18.9 us -> 17.5 us  [exchange(): return lax.all_to_all(blocks, axes, 0, 0, tiled=True).reshape(array.shape)]
  transfers between devices with their start and end apart: 12 -> 12, of which waited for: 8 -> 8; matrix products, arithmetic and copies ran while one was open for 7% -> 7% of each run, Pallas kernels for 2% -> 8%
where the time goes in v8:
time: 137 us; the launch traced here: 136 us
  blocking collectives  65.8 us (48%)
  waiting for transfers between devices  28.6 us (21%)
  Pallas kernels  17.7 us (13%)
  starting transfers between devices  15 us (11%)
  other arithmetic  7.42 us (5%)
  local copies, waits for them, and re-layouts  1.57 us (1%)
    all_to_all x1, blocking collectives, exchange(): return lax.all_to_all(blocks, axes, 0, 0, tiled=True).reshape(array.shape)  43.6 us
    all_to_all x1, blocking collectives, shards(): lax.all_to_all(sums.reshape(chips, 8, -1), ('z', 'x'), 0, 0, tiled=True)  22.2 us
    all_to_all x1, waiting for transfers between devices, exchange(): return lax.all_to_all(blocks, axes, 0, 0, tiled=True).reshape(array.shape)  17.5 us
    pallas_call x1, Pallas kernels, attend(): pl.pallas_call(attend_kernel, out_shape=jax.ShapeDtypeStruct((rows, PART)...  7.84 us
    pallas_call x4, Pallas kernels, call(): pl.pallas_call(kernel, out_shape=outs, in_specs=specs, out_specs=jax.tree...  6.86 us
    concatenate x1, other arithmetic, shards(): both_o = jnp.concatenate([w_o, mate_o], axis=0)  6.58 us
    ppermute x3, waiting for transfers between devices, shards(): lax.ppermute(pair, 'group', [(i, (i + k) % groups) for i in range(groups)])  6.32 us
    ppermute x3, starting transfers between devices, shards(): lax.ppermute(narrow, 'group', [(i, (i + k) % groups) for i in range(group...  5.9 us
  transfers between devices with their start and end apart: 12, of which 8 were waited for; matrix products, arithmetic and copies ran while one was open for 7% of the time, Pallas kernels for 8%

profile of v8, /device:TPU:32, one launch (start us, length us, event | category | flops | bytes accessed | tf_op | source)
XLA Modules:
  0.0 136.3 jit_solution(14554302609414672824)
XLA Ops:
  0.0 1.7 %shard_map.109 = bf16[64,384]{1,0:T(8,128)(2,1)S(1)} custom-call(bf16[64,1536]{1,0:T(8,128)(2,1)} %q_hbm.1, bf16[1536,256]{1,0:T(8,128)(2,1)} %wn_hbm.1, bf16[1536,128]{1,0:T(8,128)(2,1)} %wr_hbm.1), custom_call_target="tpu_custom_call" | custom-call | flops 2147483648 | bytes 4194304 | tf_op jit(solution)/shard_map/pallas_call | solution.py:339
  1.7 1.7 %collective-permute-start = (bf16[64,384]{1,0:T(8,128)(2,1)S(1)}, bf16[64,384]{1,0:T(8,128)(2,1)S(1)}, u32[]{:S(2)}, u32[]{:S(2)}) collective-permute-start(bf16[64,384]{1,0:T(8,128)(2,1)S(1)} %shard_map.109), channel_id=1, source_target_pairs={{0,64},{64,128},{128,192},{192,0},{1,65},{65,129},{129,193},{193,1... | collective-permute-start | bytes 147464 | tf_op jit(solution)/shard_map/ppermute | solution.py:353
  3.3 2.9 %collective-permute-start.1 = (bf16[64,384]{1,0:T(8,128)(2,1)S(1)}, bf16[64,384]{1,0:T(8,128)(2,1)S(1)}, u32[]{:S(2)}, u32[]{:S(2)}) collective-permute-start(bf16[64,384]{1,0:T(8,128)(2,1)S(1)} %shard_map.109), channel_id=1, source_target_pairs={{0,128},{64,192},{128,0},{192,64},{1,129},{65,193},{129,1},{193,65... | collective-permute-start | bytes 147464 | tf_op jit(solution)/shard_map/ppermute | solution.py:353
  6.2 1.3 collective-permute-start.2
  7.9 0.7 constant_dynamic-slice_fusion.2
  9.6 0.8 collective-permute-done.2
  10.5 1.4 %collective-permute-done.3.mate_q = bf16[256,384]{1,0:T(8,128)(2,1)S(1)} collective-permute-done((bf16[256,384]{1,0:T(8,128)(2,1)S(1)}, bf16[256,384]{1,0:T(8,128)(2,1)S(1)}, u32[]{:S(2)}, u32[]{:S(2)}) %collective-permute-start.3) | collective-permute-done | bytes 196640 | tf_op jit(solution)/shard_map/ppermute | solution.py:355
  12.0 1.3 shard_map.110
  13.3 43.6 %all_to_all.15 = bf16[32,8,2304]{2,1,0:T(8,128)(2,1)S(1)} all-to-all(bf16[32,8,2304]{2,1,0:T(8,128)(2,1)S(1)} %bitcast.29), channel_id=1, replica_groups=mesh['group'=4,'z'=8,'x'=4,'core'=2] {'z','x'}, dimensions={0} | all-to-all | bytes 2359296 | tf_op jit(solution)/shard_map/all_to_all | solution.py:291
  57.0 7.8 %shard_map.111 = bf16[256,2176]{1,0:T(8,128)(2,1)} custom-call(s32[2]{0:T(128)S(1)} %compare_select_fusion.3.count_ref, bf16[256,2304]{1,0:T(8,128)(2,1)S(1)} %bitcast.27, bf16[2,576,2048]{2,1,0:T(8,128)(2,1)S(1)} %bitcast.26), custom_call_target="tpu_custom_call" | custom-call | tf_op jit(solution)/shard_map/pallas_call | solution.py:195
  64.8 4.8 %all-to-all-start.1 = ((bf16[32,8,2176]{2,1,0:T(8,128)(2,1)}), bf16[32,8,2176]{2,1,0:T(8,128)(2,1)S(1)}, u32[]{:S(2)}, u32[]{:S(2)}) async-start(bf16[32,8,2176]{2,1,0:T(8,128)(2,1)} %bitcast.9), calls=%async_computation.1 | async-start | bytes 2228224 | tf_op jit(solution)/shard_map/all_to_all | solution.py:291
  70.3 1.2 collective-permute-done.5.mate_uv.mate_ref
  71.5 2.2 %shard_map.112 = (f32[32,512]{1,0:T(8,128)S(1)}, f32[32,128]{1,0:T(8,128)S(1)}) custom-call(s32[1]{0:T(128)} %bitcast.core_ref, bf16[256,384]{1,0:T(8,128)(2,1)S(1)} %pad_maximum_fusion.1.own_q, bf16[256,384]{1,0:T(8,128)(2,1)S(1)} %collective-permute-done.3.mate_q, bf16[2,128,512]{2,1,0:T(8,128)(2,1)S(1)} %copy-done.3, ...), custom_call_target="tpu_custom_call" | custom-call | tf_op jit(solution)/shard_map/pallas_call | solution.py:45
  73.7 6.6 %pad_maximum_fusion.refs_5_ = bf16[512,7168]{1,0:T(8,128)(2,1)} fusion(bf16[256,7168]{1,0:T(8,128)(2,1)} %collective-permute-done.6, bf16[256,7168]{1,0:T(8,128)(2,1)} %param.16), kind=kLoop, calls=%fused_computation | loop fusion | flops 14680064 | bytes 14680064 | tf_op jit(solution)/shard_map/concatenate | solution.py:388
  80.3 17.5 %all-to-all-done.1 = bf16[32,8,2176]{2,1,0:T(8,128)(2,1)S(1)} async-done(((bf16[32,8,2176]{2,1,0:T(8,128)(2,1)}), bf16[32,8,2176]{2,1,0:T(8,128)(2,1)S(1)}, u32[]{:S(2)}, u32[]{:S(2)}) %all-to-all-start.1) | async-done | bytes 1114144 | tf_op jit(solution)/shard_map/all_to_all | solution.py:291
  97.8 2.0 %shard_map.113 = (bf16[128,640]{1,0:T(8,128)(2,1)S(1)}, bf16[128,640]{1,0:T(8,128)(2,1)S(1)}) custom-call(s32[1]{0:T(128)} %bitcast.core_ref, bf16[256,2176]{1,0:T(8,128)(2,1)S(1)} %bitcast.30, s32[4,256]{1,0:T(4,128)S(1)} %select_n.69.code_ref, bf16[2,512,128]{2,1,0:T(8,128)(2,1)S(1)} %copy-done.4, ...), custom_call_target="tpu_custom_call" | custom-call | flops 3221225472 | bytes 8388608 | tf_op jit(solution)/shard_map/pallas_call | solution.py:45
  99.9 1.4 collective-permute-done.7.mate_ref
  101.3 2.6 %collective-permute-start.10 = (bf16[64,640]{1,0:T(8,128)(2,1)S(1)}, bf16[64,640]{1,0:T(8,128)(2,1)S(1)}, u32[]{:S(2)}, u32[]{:S(2)}) collective-permute-start(bf16[64,640]{1,0:T(8,128)(2,1)S(1)} %pad_maximum_fusion.4), channel_id=1, source_target_pairs={{0,192},{64,0},{128,64},{192,128},{1,193},{65,1},{129,65},{193,129... | collective-permute-start | bytes 245768 | tf_op jit(solution)/shard_map/ppermute | solution.py:404
  104.1 0.9 collective-permute-start.8
  105.0 2.7 %collective-permute-done.10.refs_2_ = bf16[64,640]{1,0:T(8,128)(2,1)S(1)} collective-permute-done((bf16[64,640]{1,0:T(8,128)(2,1)S(1)}, bf16[64,640]{1,0:T(8,128)(2,1)S(1)}, u32[]{:S(2)}, u32[]{:S(2)}) %collective-permute-start.10) | collective-permute-done | bytes 81952 | tf_op jit(solution)/shard_map/ppermute | solution.py:404
  107.7 2.9 %collective-permute-done.9.refs_1_ = bf16[64,640]{1,0:T(8,128)(2,1)S(1)} collective-permute-done((bf16[64,640]{1,0:T(8,128)(2,1)S(1)}, bf16[64,640]{1,0:T(8,128)(2,1)S(1)}, u32[]{:S(2)}, u32[]{:S(2)}) %collective-permute-start.9) | collective-permute-done | bytes 81952 | tf_op jit(solution)/shard_map/ppermute | solution.py:404
  111.3 2.0 %shard_map.114 = bf16[32,7168]{1,0:T(8,128)(2,1)S(1)} custom-call(s32[1]{0:T(128)} %bitcast.core_ref, bf16[128,640]{1,0:T(8,128)(2,1)S(1)} %get-tuple-element.28.own_ref, bf16[128,640]{1,0:T(8,128)(2,1)S(1)} %collective-permute-done.7.mate_ref, bf16[64,640]{1,0:T(8,128)(2,1)S(1)} %collective-permute-done.8.refs_0_, ...), custom_call_target="tpu_custom_call" | custom-call | tf_op jit(solution)/shard_map/pallas_call | solution.py:45
  113.4 22.2 %all_to_all.16.tiles_ref = bf16[32,8,896]{2,1,0:T(8,128)(2,1)S(1)} all-to-all(bf16[32,8,896]{2,1,0:T(8,128)(2,1)S(1)} %bitcast.31), channel_id=1, replica_groups=mesh['group'=4,'z'=8,'x'=4,'core'=2] {'z','x'}, dimensions={0} | all-to-all | bytes 917504 | tf_op jit(solution)/shard_map/all_to_all | solution.py:411
  135.6 0.7 shard_map.115
  (52 shorter events, 3.1 us)
Async XLA Ops:
  0.0 7.6 %copy-start = (s32[4,64,2]{1,2,0:T(2,128)S(1)}, s32[4,64,2]{1,2,0:T(2,128)}, u32[]{:S(2)}) copy-start(s32[4,64,2]{1,2,0:T(2,128)} %param.20) | copy-start | bytes 6148
  0.0 7.6 %copy-start.3 = (bf16[2,128,512]{2,1,0:T(8,128)(2,1)S(1)}, bf16[2,128,512]{2,1,0:T(8,128)(2,1)}, u32[]{:S(2)}) copy-start(bf16[2,128,512]{2,1,0:T(8,128)(2,1)} %own_uk.1) | copy-start | bytes 786436
  0.0 9.2 %copy-start.6 = (s32[64]{0:T(128)S(1)}, s32[64]{0:T(128)}, u32[]{:S(2)}) copy-start(s32[64]{0:T(128)} %param.19) | copy-start | bytes 772
  1.7 7.8 %collective-permute-start = (bf16[64,384]{1,0:T(8,128)(2,1)S(1)}, bf16[64,384]{1,0:T(8,128)(2,1)S(1)}, u32[]{:S(2)}, u32[]{:S(2)}) collective-permute-start(bf16[64,384]{1,0:T(8,128)(2,1)S(1)} %shard_map.109), channel_id=1, source_target_pairs={{0,64},{64,128},{128,192},{192,0},{1,65},{65,129},{129,193},{193,1... | collective-permute-start | bytes 147464 | tf_op jit(solution)/shard_map/ppermute | solution.py:353
  3.3 6.2 %collective-permute-start.1 = (bf16[64,384]{1,0:T(8,128)(2,1)S(1)}, bf16[64,384]{1,0:T(8,128)(2,1)S(1)}, u32[]{:S(2)}, u32[]{:S(2)}) collective-permute-start(bf16[64,384]{1,0:T(8,128)(2,1)S(1)} %shard_map.109), channel_id=1, source_target_pairs={{0,128},{64,192},{128,0},{192,64},{1,129},{65,193},{129,1},{193,65... | collective-permute-start | bytes 147464 | tf_op jit(solution)/shard_map/ppermute | solution.py:353
  6.2 4.1 %collective-permute-start.2 = (bf16[64,384]{1,0:T(8,128)(2,1)S(1)}, bf16[64,384]{1,0:T(8,128)(2,1)S(1)}, u32[]{:S(2)}, u32[]{:S(2)}) collective-permute-start(bf16[64,384]{1,0:T(8,128)(2,1)S(1)} %shard_map.109), channel_id=1, source_target_pairs={{0,192},{64,0},{128,64},{192,128},{1,193},{65,1},{129,65},{193,129... | collective-permute-start | bytes 147464 | tf_op jit(solution)/shard_map/ppermute | solution.py:353
  7.6 4.4 %collective-permute-start.4 = (bf16[2,128,512]{2,1,0:T(8,128)(2,1)S(1)}, bf16[2,128,512]{2,1,0:T(8,128)(2,1)S(1)}, u32[]{:S(2)}, u32[]{:S(2)}) collective-permute-start(bf16[2,128,512]{2,1,0:T(8,128)(2,1)S(1)} %copy-done.3), channel_id=1, source_target_pairs={{0,1},{1,0},{2,3},{3,2},{4,5},{5,4},{6,7},{7,6},{8,9},{9,8},{10,11... | collective-permute-start | bytes 786440 | tf_op jit(solution)/shard_map/ppermute | solution.py:358
  10.4 1.5 %collective-permute-start.3 = (bf16[256,384]{1,0:T(8,128)(2,1)S(1)}, bf16[256,384]{1,0:T(8,128)(2,1)S(1)}, u32[]{:S(2)}, u32[]{:S(2)}) collective-permute-start(bf16[256,384]{1,0:T(8,128)(2,1)S(1)} %pad_maximum_fusion.1.own_q), channel_id=1, source_target_pairs={{0,1},{1,0},{2,3},{3,2},{4,5},{5,4},{6,7},{7,6},{8,9},{9,8},{10,11... | collective-permute-start | bytes 589832 | tf_op jit(solution)/shard_map/ppermute | solution.py:355
  11.9 61.8 %collective-permute-start.6 = (bf16[256,7168]{1,0:T(8,128)(2,1)}, bf16[256,7168]{1,0:T(8,128)(2,1)}, u32[]{:S(2)}, u32[]{:S(2)}) collective-permute-start(bf16[256,7168]{1,0:T(8,128)(2,1)} %param.16), channel_id=1, source_target_pairs={{0,1},{1,0},{2,3},{3,2},{4,5},{5,4},{6,7},{7,6},{8,9},{9,8},{10,11... | collective-permute-start | bytes 11010056 | tf_op jit(solution)/shard_map/ppermute | solution.py:357
  12.0 45.0 %copy-start.2 = (bf16[1,1,2,2048,576]{3,4,2,1,0:T(8,128)(2,1)S(1)}, bf16[1,1,2,2048,576]{3,4,2,1,0:T(8,128)(2,1)}, u32[]{:S(2)}) copy-start(bf16[1,1,2,2048,576]{3,4,2,1,0:T(8,128)(2,1)} %param.17) | copy-start | bytes 14155780
  57.0 12.8 %copy-start.4 = (bf16[2,512,128]{2,1,0:T(8,128)(2,1)S(1)}, bf16[2,512,128]{2,1,0:T(8,128)(2,1)}, u32[]{:S(2)}) copy-start(bf16[2,512,128]{2,1,0:T(8,128)(2,1)} %own_ref.3) | copy-start | bytes 786436
  57.0 14.6 %copy-start.5 = (bf16[64,576]{1,0:T(8,128)(2,1)S(1)}, bf16[64,576]{1,0:T(8,128)(2,1)}, u32[]{:S(2)}) copy-start(bf16[64,576]{1,0:T(8,128)(2,1)} %kv_ref.1) | copy-start | bytes 221188
  64.8 32.9 %all-to-all-start.1 = ((bf16[32,8,2176]{2,1,0:T(8,128)(2,1)}), bf16[32,8,2176]{2,1,0:T(8,128)(2,1)S(1)}, u32[]{:S(2)}, u32[]{:S(2)}) async-start(bf16[32,8,2176]{2,1,0:T(8,128)(2,1)} %bitcast.9), calls=%async_computation.1 | async-start | bytes 2228224 | tf_op jit(solution)/shard_map/all_to_all | solution.py:291
  69.7 1.8 %collective-permute-start.5 = (bf16[2,512,128]{2,1,0:T(8,128)(2,1)S(1)}, bf16[2,512,128]{2,1,0:T(8,128)(2,1)S(1)}, u32[]{:S(2)}, u32[]{:S(2)}) collective-permute-start(bf16[2,512,128]{2,1,0:T(8,128)(2,1)S(1)} %copy-done.4), channel_id=1, source_target_pairs={{0,1},{1,0},{2,3},{3,2},{4,5},{5,4},{6,7},{7,6},{8,9},{9,8},{10,11... | collective-permute-start | bytes 786440 | tf_op jit(solution)/shard_map/ppermute | solution.py:377
  97.8 13.5 %copy-start.1 = (bf16[512,7168]{1,0:T(8,128)(2,1)S(1)}, bf16[512,7168]{1,0:T(8,128)(2,1)}, u32[]{:S(2)}) copy-start(bf16[512,7168]{1,0:T(8,128)(2,1)} %pad_maximum_fusion.refs_5_) | copy-start | bytes 22020100
  99.8 1.5 %collective-permute-start.7 = (bf16[128,640]{1,0:T(8,128)(2,1)S(1)}, bf16[128,640]{1,0:T(8,128)(2,1)S(1)}, u32[]{:S(2)}, u32[]{:S(2)}) collective-permute-start(bf16[128,640]{1,0:T(8,128)(2,1)S(1)} %get-tuple-element.29), channel_id=1, source_target_pairs={{0,1},{1,0},{2,3},{3,2},{4,5},{5,4},{6,7},{7,6},{8,9},{9,8},{10,11... | collective-permute-start | bytes 491528 | tf_op jit(solution)/shard_map/ppermute | solution.py:399
  101.3 6.4 %collective-permute-start.10 = (bf16[64,640]{1,0:T(8,128)(2,1)S(1)}, bf16[64,640]{1,0:T(8,128)(2,1)S(1)}, u32[]{:S(2)}, u32[]{:S(2)}) collective-permute-start(bf16[64,640]{1,0:T(8,128)(2,1)S(1)} %pad_maximum_fusion.4), channel_id=1, source_target_pairs={{0,192},{64,0},{128,64},{192,128},{1,193},{65,1},{129,65},{193,129... | collective-permute-start | bytes 245768 | tf_op jit(solution)/shard_map/ppermute | solution.py:404
  103.9 6.7 %collective-permute-start.9 = (bf16[64,640]{1,0:T(8,128)(2,1)S(1)}, bf16[64,640]{1,0:T(8,128)(2,1)S(1)}, u32[]{:S(2)}, u32[]{:S(2)}) collective-permute-start(bf16[64,640]{1,0:T(8,128)(2,1)S(1)} %pad_maximum_fusion.3), channel_id=1, source_target_pairs={{0,128},{64,192},{128,0},{192,64},{1,129},{65,193},{129,1},{193,65... | collective-permute-start | bytes 245768 | tf_op jit(solution)/shard_map/ppermute | solution.py:404
  104.1 7.3 %collective-permute-start.8 = (bf16[64,640]{1,0:T(8,128)(2,1)S(1)}, bf16[64,640]{1,0:T(8,128)(2,1)S(1)}, u32[]{:S(2)}, u32[]{:S(2)}) collective-permute-start(bf16[64,640]{1,0:T(8,128)(2,1)S(1)} %pad_maximum_fusion.2), channel_id=1, source_target_pairs={{0,64},{64,128},{128,192},{192,0},{1,65},{65,129},{129,193},{193,1... | collective-permute-start | bytes 245768 | tf_op jit(solution)/shard_map/ppermute | solution.py:404

commit v9 on v8

--- a/solution.py
+++ b/solution.py
@@ -398,7 +398,7 @@
     )
     mate_part = lax.ppermute(mate_part, "core", swap)
     others = []
-    for k in range(1, groups):
+    for k in reversed(range(1, groups)):
         at = slice(k * quarter, (k + 1) * quarter)
         pair = jnp.concatenate([own_part[at], mate_part[at]], axis=0)
         others.append(lax.ppermute(pair, "group", [(i, (i + k) % groups) for i in range(groups)]))

time: 137 us -> 135 us (0.985)
  waiting for transfers between devices: 28.6 us -> 26.5 us
    ppermute x3, waiting for transfers between devices: 6.32 us -> 4.31 us  [shards(): lax.ppermute(pair, 'group', [(i, (i + k) % groups) for i in range(groups)])]
where the time goes in v9:
time: 135 us; the launch traced here: 134 us
  blocking collectives  65 us (48%)
  waiting for transfers between devices  26.5 us (20%)
  Pallas kernels  17.7 us (13%)
  starting transfers between devices  15.7 us (12%)
  other arithmetic  7.42 us (5%)
  local copies, waits for them, and re-layouts  1.57 us (1%)
    all_to_all x1, blocking collectives, exchange(): return lax.all_to_all(blocks, axes, 0, 0, tiled=True).reshape(array.shape)  43.6 us
    all_to_all x1, blocking collectives, shards(): lax.all_to_all(sums.reshape(chips, 8, -1), ('z', 'x'), 0, 0, tiled=True)  21.3 us
    all_to_all x1, waiting for transfers between devices, exchange(): return lax.all_to_all(blocks, axes, 0, 0, tiled=True).reshape(array.shape)  17.5 us
    pallas_call x1, Pallas kernels, attend(): pl.pallas_call(attend_kernel, out_shape=jax.ShapeDtypeStruct((rows, PART)...  7.84 us
    pallas_call x4, Pallas kernels, call(): pl.pallas_call(kernel, out_shape=outs, in_specs=specs, out_specs=jax.tree...  6.86 us
    concatenate x1, other arithmetic, shards(): both_o = jnp.concatenate([w_o, mate_o], axis=0)  6.58 us
    ppermute x3, starting transfers between devices, shards(): lax.ppermute(narrow, 'group', [(i, (i + k) % groups) for i in range(group...  5.9 us
    all_to_all x1, starting transfers between devices, exchange(): return lax.all_to_all(blocks, axes, 0, 0, tiled=True).reshape(array.shape)  4.78 us
  transfers between devices with their start and end apart: 12, of which 8 were waited for; matrix products, arithmetic and copies ran while one was open for 7% of the time, Pallas kernels for 8%

profile of v9, /device:TPU:32, one launch (start us, length us, event | category | flops | bytes accessed | tf_op | source)
XLA Modules:
  0.0 134.1 jit_solution(2668566302535617954)
XLA Ops:
  0.0 1.7 %shard_map.109 = bf16[64,384]{1,0:T(8,128)(2,1)S(1)} custom-call(bf16[64,1536]{1,0:T(8,128)(2,1)} %q_hbm.1, bf16[1536,256]{1,0:T(8,128)(2,1)} %wn_hbm.1, bf16[1536,128]{1,0:T(8,128)(2,1)} %wr_hbm.1), custom_call_target="tpu_custom_call" | custom-call | flops 2147483648 | bytes 4194304 | tf_op jit(solution)/shard_map/pallas_call | solution.py:339
  1.7 1.7 %collective-permute-start = (bf16[64,384]{1,0:T(8,128)(2,1)S(1)}, bf16[64,384]{1,0:T(8,128)(2,1)S(1)}, u32[]{:S(2)}, u32[]{:S(2)}) collective-permute-start(bf16[64,384]{1,0:T(8,128)(2,1)S(1)} %shard_map.109), channel_id=1, source_target_pairs={{0,64},{64,128},{128,192},{192,0},{1,65},{65,129},{129,193},{193,1... | collective-permute-start | bytes 147464 | tf_op jit(solution)/shard_map/ppermute | solution.py:353
  3.3 2.9 %collective-permute-start.1 = (bf16[64,384]{1,0:T(8,128)(2,1)S(1)}, bf16[64,384]{1,0:T(8,128)(2,1)S(1)}, u32[]{:S(2)}, u32[]{:S(2)}) collective-permute-start(bf16[64,384]{1,0:T(8,128)(2,1)S(1)} %shard_map.109), channel_id=1, source_target_pairs={{0,128},{64,192},{128,0},{192,64},{1,129},{65,193},{129,1},{193,65... | collective-permute-start | bytes 147464 | tf_op jit(solution)/shard_map/ppermute | solution.py:353
  6.2 1.3 %collective-permute-start.2 = (bf16[64,384]{1,0:T(8,128)(2,1)S(1)}, bf16[64,384]{1,0:T(8,128)(2,1)S(1)}, u32[]{:S(2)}, u32[]{:S(2)}) collective-permute-start(bf16[64,384]{1,0:T(8,128)(2,1)S(1)} %shard_map.109), channel_id=1, source_target_pairs={{0,192},{64,0},{128,64},{192,128},{1,193},{65,1},{129,65},{193,129... | collective-permute-start | bytes 147464 | tf_op jit(solution)/shard_map/ppermute | solution.py:353
  7.9 0.7 constant_dynamic-slice_fusion.2
  9.6 0.8 collective-permute-done.2
  10.5 1.4 %collective-permute-done.3.mate_q = bf16[256,384]{1,0:T(8,128)(2,1)S(1)} collective-permute-done((bf16[256,384]{1,0:T(8,128)(2,1)S(1)}, bf16[256,384]{1,0:T(8,128)(2,1)S(1)}, u32[]{:S(2)}, u32[]{:S(2)}) %collective-permute-start.3) | collective-permute-done | bytes 196640 | tf_op jit(solution)/shard_map/ppermute | solution.py:355
  12.0 1.3 shard_map.110
  13.3 43.6 %all_to_all.15 = bf16[32,8,2304]{2,1,0:T(8,128)(2,1)S(1)} all-to-all(bf16[32,8,2304]{2,1,0:T(8,128)(2,1)S(1)} %bitcast.29), channel_id=1, replica_groups=mesh['group'=4,'z'=8,'x'=4,'core'=2] {'z','x'}, dimensions={0} | all-to-all | bytes 2359296 | tf_op jit(solution)/shard_map/all_to_all | solution.py:291
  57.0 7.8 %shard_map.111 = bf16[256,2176]{1,0:T(8,128)(2,1)} custom-call(s32[2]{0:T(128)S(1)} %compare_select_fusion.3.count_ref, bf16[256,2304]{1,0:T(8,128)(2,1)S(1)} %bitcast.27, bf16[2,576,2048]{2,1,0:T(8,128)(2,1)S(1)} %bitcast.26), custom_call_target="tpu_custom_call" | custom-call | tf_op jit(solution)/shard_map/pallas_call | solution.py:195
  64.8 4.8 %all-to-all-start.1 = ((bf16[32,8,2176]{2,1,0:T(8,128)(2,1)}), bf16[32,8,2176]{2,1,0:T(8,128)(2,1)S(1)}, u32[]{:S(2)}, u32[]{:S(2)}) async-start(bf16[32,8,2176]{2,1,0:T(8,128)(2,1)} %bitcast.9), calls=%async_computation.1 | async-start | bytes 2228224 | tf_op jit(solution)/shard_map/all_to_all | solution.py:291
  70.3 1.2 collective-permute-done.5.mate_uv.mate_ref
  71.5 2.2 %shard_map.112 = (f32[32,512]{1,0:T(8,128)S(1)}, f32[32,128]{1,0:T(8,128)S(1)}) custom-call(s32[1]{0:T(128)} %bitcast.core_ref, bf16[256,384]{1,0:T(8,128)(2,1)S(1)} %pad_maximum_fusion.1.own_q, bf16[256,384]{1,0:T(8,128)(2,1)S(1)} %collective-permute-done.3.mate_q, bf16[2,128,512]{2,1,0:T(8,128)(2,1)S(1)} %copy-done.3, ...), custom_call_target="tpu_custom_call" | custom-call | tf_op jit(solution)/shard_map/pallas_call | solution.py:45
  73.7 6.6 %pad_maximum_fusion.refs_5_ = bf16[512,7168]{1,0:T(8,128)(2,1)} fusion(bf16[256,7168]{1,0:T(8,128)(2,1)} %collective-permute-done.6, bf16[256,7168]{1,0:T(8,128)(2,1)} %param.16), kind=kLoop, calls=%fused_computation | loop fusion | flops 14680064 | bytes 14680064 | tf_op jit(solution)/shard_map/concatenate | solution.py:388
  80.3 17.5 %all-to-all-done.1 = bf16[32,8,2176]{2,1,0:T(8,128)(2,1)S(1)} async-done(((bf16[32,8,2176]{2,1,0:T(8,128)(2,1)}), bf16[32,8,2176]{2,1,0:T(8,128)(2,1)S(1)}, u32[]{:S(2)}, u32[]{:S(2)}) %all-to-all-start.1) | async-done | bytes 1114144 | tf_op jit(solution)/shard_map/all_to_all | solution.py:291
  97.8 2.0 %shard_map.113 = (bf16[128,640]{1,0:T(8,128)(2,1)S(1)}, bf16[128,640]{1,0:T(8,128)(2,1)S(1)}) custom-call(s32[1]{0:T(128)} %bitcast.core_ref, bf16[256,2176]{1,0:T(8,128)(2,1)S(1)} %bitcast.30, s32[4,256]{1,0:T(4,128)S(1)} %select_n.69.code_ref, bf16[2,512,128]{2,1,0:T(8,128)(2,1)S(1)} %copy-done.4, ...), custom_call_target="tpu_custom_call" | custom-call | flops 3221225472 | bytes 8388608 | tf_op jit(solution)/shard_map/pallas_call | solution.py:45
  99.9 1.4 %collective-permute-done.7.mate_ref = bf16[128,640]{1,0:T(8,128)(2,1)S(1)} collective-permute-done((bf16[128,640]{1,0:T(8,128)(2,1)S(1)}, bf16[128,640]{1,0:T(8,128)(2,1)S(1)}, u32[]{:S(2)}, u32[]{:S(2)}) %collective-permute-start.7) | collective-permute-done | bytes 163872 | tf_op jit(solution)/shard_map/ppermute | solution.py:399
  101.5 4.0 %collective-permute-start.9 = (bf16[64,640]{1,0:T(8,128)(2,1)S(1)}, bf16[64,640]{1,0:T(8,128)(2,1)S(1)}, u32[]{:S(2)}, u32[]{:S(2)}) collective-permute-start(bf16[64,640]{1,0:T(8,128)(2,1)S(1)} %pad_maximum_fusion.3), channel_id=1, source_target_pairs={{0,128},{64,192},{128,0},{192,64},{1,129},{65,193},{129,1},{193,65... | collective-permute-start | bytes 245768 | tf_op jit(solution)/shard_map/ppermute | solution.py:404
  105.7 1.4 %collective-permute-done.10.refs_2_ = bf16[64,640]{1,0:T(8,128)(2,1)S(1)} collective-permute-done((bf16[64,640]{1,0:T(8,128)(2,1)S(1)}, bf16[64,640]{1,0:T(8,128)(2,1)S(1)}, u32[]{:S(2)}, u32[]{:S(2)}) %collective-permute-start.10) | collective-permute-done | bytes 81952 | tf_op jit(solution)/shard_map/ppermute | solution.py:404
  107.1 2.6 %collective-permute-done.9.refs_1_ = bf16[64,640]{1,0:T(8,128)(2,1)S(1)} collective-permute-done((bf16[64,640]{1,0:T(8,128)(2,1)S(1)}, bf16[64,640]{1,0:T(8,128)(2,1)S(1)}, u32[]{:S(2)}, u32[]{:S(2)}) %collective-permute-start.9) | collective-permute-done | bytes 81952 | tf_op jit(solution)/shard_map/ppermute | solution.py:404
  109.6 0.4 collective-permute-done.8.refs_0_
  110.0 2.0 %shard_map.114 = bf16[32,7168]{1,0:T(8,128)(2,1)S(1)} custom-call(s32[1]{0:T(128)} %bitcast.core_ref, bf16[128,640]{1,0:T(8,128)(2,1)S(1)} %get-tuple-element.28.own_ref, bf16[128,640]{1,0:T(8,128)(2,1)S(1)} %collective-permute-done.7.mate_ref, bf16[64,640]{1,0:T(8,128)(2,1)S(1)} %collective-permute-done.8.refs_0_, ...), custom_call_target="tpu_custom_call" | custom-call | tf_op jit(solution)/shard_map/pallas_call | solution.py:45
  112.1 21.3 %all_to_all.16.tiles_ref = bf16[32,8,896]{2,1,0:T(8,128)(2,1)S(1)} all-to-all(bf16[32,8,896]{2,1,0:T(8,128)(2,1)S(1)} %bitcast.31), channel_id=1, replica_groups=mesh['group'=4,'z'=8,'x'=4,'core'=2] {'z','x'}, dimensions={0} | all-to-all | bytes 917504 | tf_op jit(solution)/shard_map/all_to_all | solution.py:411
  133.4 0.7 shard_map.115
  (52 shorter events, 2.7 us)
Async XLA Ops:
  0.0 7.6 %copy-start = (s32[4,64,2]{1,2,0:T(2,128)S(1)}, s32[4,64,2]{1,2,0:T(2,128)}, u32[]{:S(2)}) copy-start(s32[4,64,2]{1,2,0:T(2,128)} %param.20) | copy-start | bytes 6148
  0.0 7.6 %copy-start.3 = (bf16[2,128,512]{2,1,0:T(8,128)(2,1)S(1)}, bf16[2,128,512]{2,1,0:T(8,128)(2,1)}, u32[]{:S(2)}) copy-start(bf16[2,128,512]{2,1,0:T(8,128)(2,1)} %own_uk.1) | copy-start | bytes 786436
  0.0 9.2 %copy-start.6 = (s32[64]{0:T(128)S(1)}, s32[64]{0:T(128)}, u32[]{:S(2)}) copy-start(s32[64]{0:T(128)} %param.19) | copy-start | bytes 772
  1.7 7.8 %collective-permute-start = (bf16[64,384]{1,0:T(8,128)(2,1)S(1)}, bf16[64,384]{1,0:T(8,128)(2,1)S(1)}, u32[]{:S(2)}, u32[]{:S(2)}) collective-permute-start(bf16[64,384]{1,0:T(8,128)(2,1)S(1)} %shard_map.109), channel_id=1, source_target_pairs={{0,64},{64,128},{128,192},{192,0},{1,65},{65,129},{129,193},{193,1... | collective-permute-start | bytes 147464 | tf_op jit(solution)/shard_map/ppermute | solution.py:353
  3.3 6.2 %collective-permute-start.1 = (bf16[64,384]{1,0:T(8,128)(2,1)S(1)}, bf16[64,384]{1,0:T(8,128)(2,1)S(1)}, u32[]{:S(2)}, u32[]{:S(2)}) collective-permute-start(bf16[64,384]{1,0:T(8,128)(2,1)S(1)} %shard_map.109), channel_id=1, source_target_pairs={{0,128},{64,192},{128,0},{192,64},{1,129},{65,193},{129,1},{193,65... | collective-permute-start | bytes 147464 | tf_op jit(solution)/shard_map/ppermute | solution.py:353
  6.2 4.1 %collective-permute-start.2 = (bf16[64,384]{1,0:T(8,128)(2,1)S(1)}, bf16[64,384]{1,0:T(8,128)(2,1)S(1)}, u32[]{:S(2)}, u32[]{:S(2)}) collective-permute-start(bf16[64,384]{1,0:T(8,128)(2,1)S(1)} %shard_map.109), channel_id=1, source_target_pairs={{0,192},{64,0},{128,64},{192,128},{1,193},{65,1},{129,65},{193,129... | collective-permute-start | bytes 147464 | tf_op jit(solution)/shard_map/ppermute | solution.py:353
  7.6 4.4 %collective-permute-start.4 = (bf16[2,128,512]{2,1,0:T(8,128)(2,1)S(1)}, bf16[2,128,512]{2,1,0:T(8,128)(2,1)S(1)}, u32[]{:S(2)}, u32[]{:S(2)}) collective-permute-start(bf16[2,128,512]{2,1,0:T(8,128)(2,1)S(1)} %copy-done.3), channel_id=1, source_target_pairs={{0,1},{1,0},{2,3},{3,2},{4,5},{5,4},{6,7},{7,6},{8,9},{9,8},{10,11... | collective-permute-start | bytes 786440 | tf_op jit(solution)/shard_map/ppermute | solution.py:358
  10.4 1.5 %collective-permute-start.3 = (bf16[256,384]{1,0:T(8,128)(2,1)S(1)}, bf16[256,384]{1,0:T(8,128)(2,1)S(1)}, u32[]{:S(2)}, u32[]{:S(2)}) collective-permute-start(bf16[256,384]{1,0:T(8,128)(2,1)S(1)} %pad_maximum_fusion.1.own_q), channel_id=1, source_target_pairs={{0,1},{1,0},{2,3},{3,2},{4,5},{5,4},{6,7},{7,6},{8,9},{9,8},{10,11... | collective-permute-start | bytes 589832 | tf_op jit(solution)/shard_map/ppermute | solution.py:355
  11.9 61.8 %collective-permute-start.6 = (bf16[256,7168]{1,0:T(8,128)(2,1)}, bf16[256,7168]{1,0:T(8,128)(2,1)}, u32[]{:S(2)}, u32[]{:S(2)}) collective-permute-start(bf16[256,7168]{1,0:T(8,128)(2,1)} %param.16), channel_id=1, source_target_pairs={{0,1},{1,0},{2,3},{3,2},{4,5},{5,4},{6,7},{7,6},{8,9},{9,8},{10,11... | collective-permute-start | bytes 11010056 | tf_op jit(solution)/shard_map/ppermute | solution.py:357
  12.0 45.0 %copy-start.2 = (bf16[1,1,2,2048,576]{3,4,2,1,0:T(8,128)(2,1)S(1)}, bf16[1,1,2,2048,576]{3,4,2,1,0:T(8,128)(2,1)}, u32[]{:S(2)}) copy-start(bf16[1,1,2,2048,576]{3,4,2,1,0:T(8,128)(2,1)} %param.17) | copy-start | bytes 14155780
  57.0 12.8 %copy-start.4 = (bf16[2,512,128]{2,1,0:T(8,128)(2,1)S(1)}, bf16[2,512,128]{2,1,0:T(8,128)(2,1)}, u32[]{:S(2)}) copy-start(bf16[2,512,128]{2,1,0:T(8,128)(2,1)} %own_ref.3) | copy-start | bytes 786436
  57.0 14.6 %copy-start.5 = (bf16[64,576]{1,0:T(8,128)(2,1)S(1)}, bf16[64,576]{1,0:T(8,128)(2,1)}, u32[]{:S(2)}) copy-start(bf16[64,576]{1,0:T(8,128)(2,1)} %kv_ref.1) | copy-start | bytes 221188
  64.8 32.9 %all-to-all-start.1 = ((bf16[32,8,2176]{2,1,0:T(8,128)(2,1)}), bf16[32,8,2176]{2,1,0:T(8,128)(2,1)S(1)}, u32[]{:S(2)}, u32[]{:S(2)}) async-start(bf16[32,8,2176]{2,1,0:T(8,128)(2,1)} %bitcast.9), calls=%async_computation.1 | async-start | bytes 2228224 | tf_op jit(solution)/shard_map/all_to_all | solution.py:291
  69.7 1.8 %collective-permute-start.5 = (bf16[2,512,128]{2,1,0:T(8,128)(2,1)S(1)}, bf16[2,512,128]{2,1,0:T(8,128)(2,1)S(1)}, u32[]{:S(2)}, u32[]{:S(2)}) collective-permute-start(bf16[2,512,128]{2,1,0:T(8,128)(2,1)S(1)} %copy-done.4), channel_id=1, source_target_pairs={{0,1},{1,0},{2,3},{3,2},{4,5},{5,4},{6,7},{7,6},{8,9},{9,8},{10,11... | collective-permute-start | bytes 786440 | tf_op jit(solution)/shard_map/ppermute | solution.py:377
  97.8 12.2 %copy-start.1 = (bf16[512,7168]{1,0:T(8,128)(2,1)S(1)}, bf16[512,7168]{1,0:T(8,128)(2,1)}, u32[]{:S(2)}) copy-start(bf16[512,7168]{1,0:T(8,128)(2,1)} %pad_maximum_fusion.refs_5_) | copy-start | bytes 22020100
  99.8 1.5 %collective-permute-start.7 = (bf16[128,640]{1,0:T(8,128)(2,1)S(1)}, bf16[128,640]{1,0:T(8,128)(2,1)S(1)}, u32[]{:S(2)}, u32[]{:S(2)}) collective-permute-start(bf16[128,640]{1,0:T(8,128)(2,1)S(1)} %get-tuple-element.29), channel_id=1, source_target_pairs={{0,1},{1,0},{2,3},{3,2},{4,5},{5,4},{6,7},{7,6},{8,9},{9,8},{10,11... | collective-permute-start | bytes 491528 | tf_op jit(solution)/shard_map/ppermute | solution.py:399
  101.3 5.8 %collective-permute-start.10 = (bf16[64,640]{1,0:T(8,128)(2,1)S(1)}, bf16[64,640]{1,0:T(8,128)(2,1)S(1)}, u32[]{:S(2)}, u32[]{:S(2)}) collective-permute-start(bf16[64,640]{1,0:T(8,128)(2,1)S(1)} %pad_maximum_fusion.4), channel_id=1, source_target_pairs={{0,64},{64,128},{128,192},{192,0},{1,65},{65,129},{129,193},{193,1... | collective-permute-start | bytes 245768 | tf_op jit(solution)/shard_map/ppermute | solution.py:404
  101.5 8.1 %collective-permute-start.9 = (bf16[64,640]{1,0:T(8,128)(2,1)S(1)}, bf16[64,640]{1,0:T(8,128)(2,1)S(1)}, u32[]{:S(2)}, u32[]{:S(2)}) collective-permute-start(bf16[64,640]{1,0:T(8,128)(2,1)S(1)} %pad_maximum_fusion.3), channel_id=1, source_target_pairs={{0,128},{64,192},{128,0},{192,64},{1,129},{65,193},{129,1},{193,65... | collective-permute-start | bytes 245768 | tf_op jit(solution)/shard_map/ppermute | solution.py:404
  105.5 4.5 %collective-permute-start.8 = (bf16[64,640]{1,0:T(8,128)(2,1)S(1)}, bf16[64,640]{1,0:T(8,128)(2,1)S(1)}, u32[]{:S(2)}, u32[]{:S(2)}) collective-permute-start(bf16[64,640]{1,0:T(8,128)(2,1)S(1)} %pad_maximum_fusion.2), channel_id=1, source_target_pairs={{0,192},{64,0},{128,64},{192,128},{1,193},{65,1},{129,65},{193,129... | collective-permute-start | bytes 245768 | tf_op jit(solution)/shard_map/ppermute | solution.py:404

commit v10 on v9

--- a/solution.py
+++ b/solution.py
@@ -156,13 +156,19 @@
             queries[at, :LATENT] = x_ref[:, first : first + LATENT]
             first = slot * WIDE + 2 * LATENT + par * ROPE
             queries[at, LATENT:] = x_ref[:, first : first + ROPE]
-        peak = jnp.full((2 * half, 1), EMPTY, F32)
-        for first in range(0, slab, chunk):
-            score = dot(queries[...], kv_ref[slot, :, first : first + chunk])
-            position = lax.broadcasted_iota(jnp.int32, score.shape, 1) + first
-            score = jnp.where(position < count, score, EMPTY)
-            scores[:, first : first + chunk] = score
-            peak = jnp.maximum(peak, jnp.max(score, axis=1, keepdims=True))
+
+        def score_slab(masked, slot=slot, count=count):
+            peak = jnp.full((2 * half, 1), EMPTY, F32)
+            for first in range(0, slab, chunk):
+                score = dot(queries[...], kv_ref[slot, :, first : first + chunk])
+                if masked:
+                    position = lax.broadcasted_iota(jnp.int32, score.shape, 1) + first
+                    score = jnp.where(position < count, score, EMPTY)
+                scores[:, first : first + chunk] = score
+                peak = jnp.maximum(peak, jnp.max(score, axis=1, keepdims=True))
+            return peak
+
+        peak = lax.cond(count >= slab, lambda: score_slab(False), lambda: score_slab(True))
         reference = jnp.maximum(peak, EMPTY / 10)
         total = jnp.zeros((2 * half, 1), F32)
         for first in range(0, slab, chunk):

time: 135 us -> 136 us (level)
  transfers between devices with their start and end apart: 12 -> 12, of which waited for: 8 -> 8; matrix products, arithmetic and copies ran while one was open for 7% -> 7% of each run, Pallas kernels for 8% -> 9%
where the time goes in v10:
time: 136 us; the launch traced here: 135 us
  blocking collectives  65 us (48%)
  waiting for transfers between devices  26.7 us (20%)
  Pallas kernels  18.4 us (14%)
  starting transfers between devices  15.5 us (11%)
  other arithmetic  7.42 us (5%)
  local copies, waits for them, and re-layouts  1.57 us (1%)
    all_to_all x1, blocking collectives, exchange(): return lax.all_to_all(blocks, axes, 0, 0, tiled=True).reshape(array.shape)  43.6 us
    all_to_all x1, blocking collectives, shards(): lax.all_to_all(sums.reshape(chips, 8, -1), ('z', 'x'), 0, 0, tiled=True)  21.3 us
    all_to_all x1, waiting for transfers between devices, exchange(): return lax.all_to_all(blocks, axes, 0, 0, tiled=True).reshape(array.shape)  17.6 us
    pallas_call x1, Pallas kernels, attend(): pl.pallas_call(attend_kernel, out_shape=jax.ShapeDtypeStruct((rows, PART)...  8.56 us
    pallas_call x4, Pallas kernels, call(): pl.pallas_call(kernel, out_shape=outs, in_specs=specs, out_specs=jax.tree...  6.86 us
    concatenate x1, other arithmetic, shards(): both_o = jnp.concatenate([w_o, mate_o], axis=0)  6.58 us
    ppermute x3, starting transfers between devices, shards(): lax.ppermute(narrow, 'group', [(i, (i + k) % groups) for i in range(group...  5.9 us
    all_to_all x1, starting transfers between devices, exchange(): return lax.all_to_all(blocks, axes, 0, 0, tiled=True).reshape(array.shape)  4.8 us
  transfers between devices with their start and end apart: 12, of which 8 were waited for; matrix products, arithmetic and copies ran while one was open for 7% of the time, Pallas kernels for 9%

profile of v10, /device:TPU:32, one launch (start us, length us, event | category | flops | bytes accessed | tf_op | source)
XLA Modules:
  0.0 134.9 jit_solution(6310580361554444026)
XLA Ops:
  0.0 1.7 %shard_map.109 = bf16[64,384]{1,0:T(8,128)(2,1)S(1)} custom-call(bf16[64,1536]{1,0:T(8,128)(2,1)} %q_hbm.1, bf16[1536,256]{1,0:T(8,128)(2,1)} %wn_hbm.1, bf16[1536,128]{1,0:T(8,128)(2,1)} %wr_hbm.1), custom_call_target="tpu_custom_call" | custom-call | flops 2147483648 | bytes 4194304 | tf_op jit(solution)/shard_map/pallas_call | solution.py:345
  1.7 1.7 %collective-permute-start = (bf16[64,384]{1,0:T(8,128)(2,1)S(1)}, bf16[64,384]{1,0:T(8,128)(2,1)S(1)}, u32[]{:S(2)}, u32[]{:S(2)}) collective-permute-start(bf16[64,384]{1,0:T(8,128)(2,1)S(1)} %shard_map.109), channel_id=1, source_target_pairs={{0,64},{64,128},{128,192},{192,0},{1,65},{65,129},{129,193},{193,1... | collective-permute-start | bytes 147464 | tf_op jit(solution)/shard_map/ppermute | solution.py:359
  3.3 2.9 %collective-permute-start.1 = (bf16[64,384]{1,0:T(8,128)(2,1)S(1)}, bf16[64,384]{1,0:T(8,128)(2,1)S(1)}, u32[]{:S(2)}, u32[]{:S(2)}) collective-permute-start(bf16[64,384]{1,0:T(8,128)(2,1)S(1)} %shard_map.109), channel_id=1, source_target_pairs={{0,128},{64,192},{128,0},{192,64},{1,129},{65,193},{129,1},{193,65... | collective-permute-start | bytes 147464 | tf_op jit(solution)/shard_map/ppermute | solution.py:359
  6.2 1.3 collective-permute-start.2
  7.9 0.7 constant_dynamic-slice_fusion.2
  9.6 0.8 collective-permute-done.2
  10.5 1.4 %collective-permute-done.3.mate_q = bf16[256,384]{1,0:T(8,128)(2,1)S(1)} collective-permute-done((bf16[256,384]{1,0:T(8,128)(2,1)S(1)}, bf16[256,384]{1,0:T(8,128)(2,1)S(1)}, u32[]{:S(2)}, u32[]{:S(2)}) %collective-permute-start.3) | collective-permute-done | bytes 196640 | tf_op jit(solution)/shard_map/ppermute | solution.py:361
  12.0 1.3 shard_map.110
  13.3 43.6 %all_to_all.15 = bf16[32,8,2304]{2,1,0:T(8,128)(2,1)S(1)} all-to-all(bf16[32,8,2304]{2,1,0:T(8,128)(2,1)S(1)} %bitcast.29), channel_id=1, replica_groups=mesh['group'=4,'z'=8,'x'=4,'core'=2] {'z','x'}, dimensions={0} | all-to-all | bytes 2359296 | tf_op jit(solution)/shard_map/all_to_all | solution.py:297
  57.0 8.6 %shard_map.111 = bf16[256,2176]{1,0:T(8,128)(2,1)} custom-call(s32[2]{0:T(128)S(1)} %compare_select_fusion.3.count_ref, bf16[256,2304]{1,0:T(8,128)(2,1)S(1)} %bitcast.27, bf16[2,576,2048]{2,1,0:T(8,128)(2,1)S(1)} %bitcast.26), custom_call_target="tpu_custom_call" | custom-call | tf_op jit(solution)/shard_map/pallas_call | solution.py:201
  65.6 4.8 %all-to-all-start.1 = ((bf16[32,8,2176]{2,1,0:T(8,128)(2,1)}), bf16[32,8,2176]{2,1,0:T(8,128)(2,1)S(1)}, u32[]{:S(2)}, u32[]{:S(2)}) async-start(bf16[32,8,2176]{2,1,0:T(8,128)(2,1)} %bitcast.9), calls=%async_computation.1 | async-start | bytes 2228224 | tf_op jit(solution)/shard_map/all_to_all | solution.py:297
  70.9 1.2 collective-permute-done.5.mate_uv.mate_ref
  72.1 2.2 %shard_map.112 = (f32[32,512]{1,0:T(8,128)S(1)}, f32[32,128]{1,0:T(8,128)S(1)}) custom-call(s32[1]{0:T(128)} %bitcast.core_ref, bf16[256,384]{1,0:T(8,128)(2,1)S(1)} %pad_maximum_fusion.1.own_q, bf16[256,384]{1,0:T(8,128)(2,1)S(1)} %collective-permute-done.3.mate_q, bf16[2,128,512]{2,1,0:T(8,128)(2,1)S(1)} %copy-done.3, ...), custom_call_target="tpu_custom_call" | custom-call | tf_op jit(solution)/shard_map/pallas_call | solution.py:45
  74.3 6.6 %pad_maximum_fusion.refs_5_ = bf16[512,7168]{1,0:T(8,128)(2,1)} fusion(bf16[256,7168]{1,0:T(8,128)(2,1)} %collective-permute-done.6, bf16[256,7168]{1,0:T(8,128)(2,1)} %param.16), kind=kLoop, calls=%fused_computation | loop fusion | flops 14680064 | bytes 14680064 | tf_op jit(solution)/shard_map/concatenate | solution.py:394
  80.9 17.6 %all-to-all-done.1 = bf16[32,8,2176]{2,1,0:T(8,128)(2,1)S(1)} async-done(((bf16[32,8,2176]{2,1,0:T(8,128)(2,1)}), bf16[32,8,2176]{2,1,0:T(8,128)(2,1)S(1)}, u32[]{:S(2)}, u32[]{:S(2)}) %all-to-all-start.1) | async-done | bytes 1114144 | tf_op jit(solution)/shard_map/all_to_all | solution.py:297
  98.5 2.0 %shard_map.113 = (bf16[128,640]{1,0:T(8,128)(2,1)S(1)}, bf16[128,640]{1,0:T(8,128)(2,1)S(1)}) custom-call(s32[1]{0:T(128)} %bitcast.core_ref, bf16[256,2176]{1,0:T(8,128)(2,1)S(1)} %bitcast.30, s32[4,256]{1,0:T(4,128)S(1)} %select_n.69.code_ref, bf16[2,512,128]{2,1,0:T(8,128)(2,1)S(1)} %copy-done.4, ...), custom_call_target="tpu_custom_call" | custom-call | flops 3221225472 | bytes 8388608 | tf_op jit(solution)/shard_map/pallas_call | solution.py:45
  100.6 1.4 %collective-permute-done.7.mate_ref = bf16[128,640]{1,0:T(8,128)(2,1)S(1)} collective-permute-done((bf16[128,640]{1,0:T(8,128)(2,1)S(1)}, bf16[128,640]{1,0:T(8,128)(2,1)S(1)}, u32[]{:S(2)}, u32[]{:S(2)}) %collective-permute-start.7) | collective-permute-done | bytes 163872 | tf_op jit(solution)/shard_map/ppermute | solution.py:405
  102.2 4.0 %collective-permute-start.9 = (bf16[64,640]{1,0:T(8,128)(2,1)S(1)}, bf16[64,640]{1,0:T(8,128)(2,1)S(1)}, u32[]{:S(2)}, u32[]{:S(2)}) collective-permute-start(bf16[64,640]{1,0:T(8,128)(2,1)S(1)} %pad_maximum_fusion.3), channel_id=1, source_target_pairs={{0,128},{64,192},{128,0},{192,64},{1,129},{65,193},{129,1},{193,65... | collective-permute-start | bytes 245768 | tf_op jit(solution)/shard_map/ppermute | solution.py:410
  106.4 1.4 %collective-permute-done.10.refs_2_ = bf16[64,640]{1,0:T(8,128)(2,1)S(1)} collective-permute-done((bf16[64,640]{1,0:T(8,128)(2,1)S(1)}, bf16[64,640]{1,0:T(8,128)(2,1)S(1)}, u32[]{:S(2)}, u32[]{:S(2)}) %collective-permute-start.10) | collective-permute-done | bytes 81952 | tf_op jit(solution)/shard_map/ppermute | solution.py:410
  107.8 2.5 %collective-permute-done.9.refs_1_ = bf16[64,640]{1,0:T(8,128)(2,1)S(1)} collective-permute-done((bf16[64,640]{1,0:T(8,128)(2,1)S(1)}, bf16[64,640]{1,0:T(8,128)(2,1)S(1)}, u32[]{:S(2)}, u32[]{:S(2)}) %collective-permute-start.9) | collective-permute-done | bytes 81952 | tf_op jit(solution)/shard_map/ppermute | solution.py:410
  110.4 0.4 collective-permute-done.8.refs_0_
  110.8 2.0 %shard_map.114 = bf16[32,7168]{1,0:T(8,128)(2,1)S(1)} custom-call(s32[1]{0:T(128)} %bitcast.core_ref, bf16[128,640]{1,0:T(8,128)(2,1)S(1)} %get-tuple-element.28.own_ref, bf16[128,640]{1,0:T(8,128)(2,1)S(1)} %collective-permute-done.7.mate_ref, bf16[64,640]{1,0:T(8,128)(2,1)S(1)} %collective-permute-done.8.refs_0_, ...), custom_call_target="tpu_custom_call" | custom-call | tf_op jit(solution)/shard_map/pallas_call | solution.py:45
  112.8 21.3 %all_to_all.16.tiles_ref = bf16[32,8,896]{2,1,0:T(8,128)(2,1)S(1)} all-to-all(bf16[32,8,896]{2,1,0:T(8,128)(2,1)S(1)} %bitcast.31), channel_id=1, replica_groups=mesh['group'=4,'z'=8,'x'=4,'core'=2] {'z','x'}, dimensions={0} | all-to-all | bytes 917504 | tf_op jit(solution)/shard_map/all_to_all | solution.py:417
  134.2 0.7 shard_map.115
  (52 shorter events, 2.5 us)
Async XLA Ops:
  0.0 7.6 %copy-start = (s32[4,64,2]{1,2,0:T(2,128)S(1)}, s32[4,64,2]{1,2,0:T(2,128)}, u32[]{:S(2)}) copy-start(s32[4,64,2]{1,2,0:T(2,128)} %param.20) | copy-start | bytes 6148
  0.0 7.6 %copy-start.3 = (bf16[2,128,512]{2,1,0:T(8,128)(2,1)S(1)}, bf16[2,128,512]{2,1,0:T(8,128)(2,1)}, u32[]{:S(2)}) copy-start(bf16[2,128,512]{2,1,0:T(8,128)(2,1)} %own_uk.1) | copy-start | bytes 786436
  0.0 9.2 %copy-start.6 = (s32[64]{0:T(128)S(1)}, s32[64]{0:T(128)}, u32[]{:S(2)}) copy-start(s32[64]{0:T(128)} %param.19) | copy-start | bytes 772
  1.7 7.8 %collective-permute-start = (bf16[64,384]{1,0:T(8,128)(2,1)S(1)}, bf16[64,384]{1,0:T(8,128)(2,1)S(1)}, u32[]{:S(2)}, u32[]{:S(2)}) collective-permute-start(bf16[64,384]{1,0:T(8,128)(2,1)S(1)} %shard_map.109), channel_id=1, source_target_pairs={{0,64},{64,128},{128,192},{192,0},{1,65},{65,129},{129,193},{193,1... | collective-permute-start | bytes 147464 | tf_op jit(solution)/shard_map/ppermute | solution.py:359
  3.3 6.2 %collective-permute-start.1 = (bf16[64,384]{1,0:T(8,128)(2,1)S(1)}, bf16[64,384]{1,0:T(8,128)(2,1)S(1)}, u32[]{:S(2)}, u32[]{:S(2)}) collective-permute-start(bf16[64,384]{1,0:T(8,128)(2,1)S(1)} %shard_map.109), channel_id=1, source_target_pairs={{0,128},{64,192},{128,0},{192,64},{1,129},{65,193},{129,1},{193,65... | collective-permute-start | bytes 147464 | tf_op jit(solution)/shard_map/ppermute | solution.py:359
  6.2 4.1 %collective-permute-start.2 = (bf16[64,384]{1,0:T(8,128)(2,1)S(1)}, bf16[64,384]{1,0:T(8,128)(2,1)S(1)}, u32[]{:S(2)}, u32[]{:S(2)}) collective-permute-start(bf16[64,384]{1,0:T(8,128)(2,1)S(1)} %shard_map.109), channel_id=1, source_target_pairs={{0,192},{64,0},{128,64},{192,128},{1,193},{65,1},{129,65},{193,129... | collective-permute-start | bytes 147464 | tf_op jit(solution)/shard_map/ppermute | solution.py:359
  7.6 4.4 %collective-permute-start.4 = (bf16[2,128,512]{2,1,0:T(8,128)(2,1)S(1)}, bf16[2,128,512]{2,1,0:T(8,128)(2,1)S(1)}, u32[]{:S(2)}, u32[]{:S(2)}) collective-permute-start(bf16[2,128,512]{2,1,0:T(8,128)(2,1)S(1)} %copy-done.3), channel_id=1, source_target_pairs={{0,1},{1,0},{2,3},{3,2},{4,5},{5,4},{6,7},{7,6},{8,9},{9,8},{10,11... | collective-permute-start | bytes 786440 | tf_op jit(solution)/shard_map/ppermute | solution.py:364
  10.4 1.5 %collective-permute-start.3 = (bf16[256,384]{1,0:T(8,128)(2,1)S(1)}, bf16[256,384]{1,0:T(8,128)(2,1)S(1)}, u32[]{:S(2)}, u32[]{:S(2)}) collective-permute-start(bf16[256,384]{1,0:T(8,128)(2,1)S(1)} %pad_maximum_fusion.1.own_q), channel_id=1, source_target_pairs={{0,1},{1,0},{2,3},{3,2},{4,5},{5,4},{6,7},{7,6},{8,9},{9,8},{10,11... | collective-permute-start | bytes 589832 | tf_op jit(solution)/shard_map/ppermute | solution.py:361
  11.9 62.4 %collective-permute-start.6 = (bf16[256,7168]{1,0:T(8,128)(2,1)}, bf16[256,7168]{1,0:T(8,128)(2,1)}, u32[]{:S(2)}, u32[]{:S(2)}) collective-permute-start(bf16[256,7168]{1,0:T(8,128)(2,1)} %param.16), channel_id=1, source_target_pairs={{0,1},{1,0},{2,3},{3,2},{4,5},{5,4},{6,7},{7,6},{8,9},{9,8},{10,11... | collective-permute-start | bytes 11010056 | tf_op jit(solution)/shard_map/ppermute | solution.py:363
  12.0 45.0 %copy-start.2 = (bf16[1,1,2,2048,576]{3,4,2,1,0:T(8,128)(2,1)S(1)}, bf16[1,1,2,2048,576]{3,4,2,1,0:T(8,128)(2,1)}, u32[]{:S(2)}) copy-start(bf16[1,1,2,2048,576]{3,4,2,1,0:T(8,128)(2,1)} %param.17) | copy-start | bytes 14155780
  57.0 13.5 %copy-start.4 = (bf16[2,512,128]{2,1,0:T(8,128)(2,1)S(1)}, bf16[2,512,128]{2,1,0:T(8,128)(2,1)}, u32[]{:S(2)}) copy-start(bf16[2,512,128]{2,1,0:T(8,128)(2,1)} %own_ref.3) | copy-start | bytes 786436
  57.0 15.1 %copy-start.5 = (bf16[64,576]{1,0:T(8,128)(2,1)S(1)}, bf16[64,576]{1,0:T(8,128)(2,1)}, u32[]{:S(2)}) copy-start(bf16[64,576]{1,0:T(8,128)(2,1)} %kv_ref.1) | copy-start | bytes 221188
  65.6 33.0 %all-to-all-start.1 = ((bf16[32,8,2176]{2,1,0:T(8,128)(2,1)}), bf16[32,8,2176]{2,1,0:T(8,128)(2,1)S(1)}, u32[]{:S(2)}, u32[]{:S(2)}) async-start(bf16[32,8,2176]{2,1,0:T(8,128)(2,1)} %bitcast.9), calls=%async_computation.1 | async-start | bytes 2228224 | tf_op jit(solution)/shard_map/all_to_all | solution.py:297
  70.5 1.6 %collective-permute-start.5 = (bf16[2,512,128]{2,1,0:T(8,128)(2,1)S(1)}, bf16[2,512,128]{2,1,0:T(8,128)(2,1)S(1)}, u32[]{:S(2)}, u32[]{:S(2)}) collective-permute-start(bf16[2,512,128]{2,1,0:T(8,128)(2,1)S(1)} %copy-done.4), channel_id=1, source_target_pairs={{0,1},{1,0},{2,3},{3,2},{4,5},{5,4},{6,7},{7,6},{8,9},{9,8},{10,11... | collective-permute-start | bytes 786440 | tf_op jit(solution)/shard_map/ppermute | solution.py:383
  98.5 12.2 %copy-start.1 = (bf16[512,7168]{1,0:T(8,128)(2,1)S(1)}, bf16[512,7168]{1,0:T(8,128)(2,1)}, u32[]{:S(2)}) copy-start(bf16[512,7168]{1,0:T(8,128)(2,1)} %pad_maximum_fusion.refs_5_) | copy-start | bytes 22020100
  100.5 1.5 %collective-permute-start.7 = (bf16[128,640]{1,0:T(8,128)(2,1)S(1)}, bf16[128,640]{1,0:T(8,128)(2,1)S(1)}, u32[]{:S(2)}, u32[]{:S(2)}) collective-permute-start(bf16[128,640]{1,0:T(8,128)(2,1)S(1)} %get-tuple-element.29), channel_id=1, source_target_pairs={{0,1},{1,0},{2,3},{3,2},{4,5},{5,4},{6,7},{7,6},{8,9},{9,8},{10,11... | collective-permute-start | bytes 491528 | tf_op jit(solution)/shard_map/ppermute | solution.py:405
  102.0 5.8 %collective-permute-start.10 = (bf16[64,640]{1,0:T(8,128)(2,1)S(1)}, bf16[64,640]{1,0:T(8,128)(2,1)S(1)}, u32[]{:S(2)}, u32[]{:S(2)}) collective-permute-start(bf16[64,640]{1,0:T(8,128)(2,1)S(1)} %pad_maximum_fusion.4), channel_id=1, source_target_pairs={{0,64},{64,128},{128,192},{192,0},{1,65},{65,129},{129,193},{193,1... | collective-permute-start | bytes 245768 | tf_op jit(solution)/shard_map/ppermute | solution.py:410
  102.2 8.1 %collective-permute-start.9 = (bf16[64,640]{1,0:T(8,128)(2,1)S(1)}, bf16[64,640]{1,0:T(8,128)(2,1)S(1)}, u32[]{:S(2)}, u32[]{:S(2)}) collective-permute-start(bf16[64,640]{1,0:T(8,128)(2,1)S(1)} %pad_maximum_fusion.3), channel_id=1, source_target_pairs={{0,128},{64,192},{128,0},{192,64},{1,129},{65,193},{129,1},{193,65... | collective-permute-start | bytes 245768 | tf_op jit(solution)/shard_map/ppermute | solution.py:410
  106.2 4.5 %collective-permute-start.8 = (bf16[64,640]{1,0:T(8,128)(2,1)S(1)}, bf16[64,640]{1,0:T(8,128)(2,1)S(1)}, u32[]{:S(2)}, u32[]{:S(2)}) collective-permute-start(bf16[64,640]{1,0:T(8,128)(2,1)S(1)} %pad_maximum_fusion.2), channel_id=1, source_target_pairs={{0,192},{64,0},{128,64},{192,128},{1,193},{65,1},{129,65},{193,129... | collective-permute-start | bytes 245768 | tf_op jit(solution)/shard_map/ppermute | solution.py:410
